TPU v7x, 128 devices: a whole 4x4x4 slice. The times are simulated.
128 devices in a mesh: gx: 8 (over x, core), gy: 16 (over z, y).
Axes of the slice: x: 4, y: 4, z: 4, core: 2. Of those that a mesh axis runs over, the one named last changes fastest.
Arguments:
- density: float32 [2, 128, 1024], P(None, 'gy', 'gx'), may hold values from 0.1 to 10
- point_position: float32 [3, 2, 128, 1024], P(None, None, 'gy', 'gx'), may hold values from 0 to 1
- block_owner: int32 [2, 128, 128], P(None, 'gy', 'gx'), may hold values from 0 to 127, as said below
- block_slot: int32 [2, 128, 128], P(None, 'gy', 'gx'), may hold values from 0 to 511, as said below
- block_count: int32 [2, 128, 8], P(None, 'gy', 'gx'), may hold values from 8 to 16
- site_position: float32 [3, 8388608], P(None, ('gx', 'gy')), may hold values from 0 to 1
- site_weight: float32 [8388608], P(('gx', 'gy')), may hold values from -0.2 to 11.5
Outputs:
- potential: float32 [2, 128, 1024], P(None, 'gy', 'gx')
- site_mass: float32 [8388608], P(('gx', 'gy'))
- barycentre: float32 [3, 8388608], P(None, ('gx', 'gy'))
Inputs may be any that keep to these rules, and one draw needn't show every extreme that they name: `block_owner`: owners are device indices with gx slowest. Among the entries held by one device, padding included, no owner is named more than 4 times, and one owner is named exactly 4 times by every device. `block_slot`: the entries held by one device name distinct blocks.
All inputs are finite; a program needn't handle non-finite values.
Results may differ from a plain program's by a relative error of at most 0.0003.
Values sent between devices are 32-bit elements; how exact they have to be, the bound alone decides.
No kernel may reach another device: no remote copies, remote signals or barrier semaphores. Data moves between devices by JAX's collectives and lax.ppermute only.
A program may use at most 64 MiB of HBM per device.

v0:
```python
import jax
import jax.numpy as jnp
from jax import lax
from jax.sharding import PartitionSpec as P

PZ = 2
TILE = 128
CAND = 16
SITE_BLOCK = 128
SB_DEV = 512
HALF = 8


EPSILON = 0.05
PRIOR_MASS = 0.5
SIGMA_CELLS = 4.0


def extended(cells, sides, width):
    for axis, dim in sides:
        count = lax.axis_size(axis)
        head = lax.slice_in_dim(cells, 0, width, axis=dim)
        tail = lax.slice_in_dim(cells, cells.shape[dim] - width, cells.shape[dim], axis=dim)
        cells = jnp.concatenate(
            [
                lax.ppermute(tail, axis, [(i, (i + 1) % count) for i in range(count)]),
                cells,
                lax.ppermute(head, axis, [((i + 1) % count, i) for i in range(count)]),
            ],
            axis=dim,
        )
    return cells


def gauss_kernel():
    offsets = jnp.arange(-HALF, HALF + 1).astype(jnp.float32)
    values = jnp.exp(-offsets * offsets / (2.0 * SIGMA_CELLS * SIGMA_CELLS))
    return values / jnp.sum(values)


def extended_pass(padded, kernel, axis_dim, length):
    running = jnp.zeros_like(lax.slice_in_dim(padded, 0, length, axis=axis_dim))
    for offset in range(2 * HALF + 1):
        running = running + kernel[offset] * lax.slice_in_dim(
            padded, offset, offset + length, axis=axis_dim
        )
    return running


def planar_pass(field_in, kernel):
    padded = jnp.pad(field_in, ((HALF, HALF), (0, 0), (0, 0)))
    running = jnp.zeros_like(field_in)
    for offset in range(2 * HALF + 1):
        running = running + kernel[offset] * padded[offset : offset + PZ]
    return running


def local(
    density, point_position, block_owner, block_slot, block_count, site_position, site_weight
):
    kernel = gauss_kernel()
    rows_dev = density.shape[1]
    padded = extended(density, (("gx", 2),), HALF)
    first_pass = extended_pass(padded, kernel, 2, TILE)
    padded_rows = extended(first_pass, (("gy", 1),), HALF)
    second_pass = extended_pass(padded_rows, kernel, 1, rows_dev)
    smoothed = planar_pass(second_pass, kernel)
    column_count = lax.axis_size("gx")
    row_count = lax.axis_size("gy")
    owner_total = column_count * row_count
    tile_total = PZ * rows_dev
    entry_total = tile_total * CAND
    capacity = max(2, 2 * entry_total // owner_total)
    slot_total = owner_total * capacity
    owners = jnp.transpose(block_owner.reshape(tile_total, CAND)).reshape(entry_total)
    slot_ids = jnp.transpose(block_slot.reshape(tile_total, CAND)).reshape(entry_total)
    live_mask = jnp.arange(CAND)[:, None] < block_count.reshape(1, tile_total)
    live_flat = live_mask.reshape(entry_total)
    one_hot = (owners[:, None] == jnp.arange(owner_total)[None, :]).astype(jnp.int32)
    rank_in = jnp.sum((jnp.cumsum(one_hot, axis=0) - 1) * one_hot, axis=1)
    target = owners * capacity + rank_in
    requests = (
        jnp.full((slot_total,), -1, jnp.int32).at[target].set(jnp.where(live_flat, slot_ids, -1))
    )
    asked_ids = lax.all_to_all(
        requests.reshape(owner_total, capacity),
        ("gx", "gy"),
        split_axis=0,
        concat_axis=0,
        tiled=True,
    )
    asked_flat = asked_ids.reshape(slot_total)
    asked_live = (asked_flat >= 0).astype(jnp.float32)
    site_table = jnp.concatenate([site_position, site_weight[None, :]], axis=0).reshape(
        4, SB_DEV, SITE_BLOCK
    )
    picked = jnp.take(site_table, jnp.maximum(asked_flat, 0), axis=1) * asked_live[None, :, None]
    arrived = lax.all_to_all(
        picked.reshape(4, owner_total, capacity, SITE_BLOCK),
        ("gx", "gy"),
        split_axis=1,
        concat_axis=1,
        tiled=True,
    )
    fetched = jnp.take(arrived.reshape(4, slot_total, SITE_BLOCK), target, axis=1).reshape(
        4, CAND, tile_total, SITE_BLOCK
    )
    point_coords = point_position.reshape(3, tile_total, TILE)
    weights_in = smoothed.reshape(tile_total, TILE)

    def block_scores(column):
        site_block = lax.dynamic_index_in_dim(fetched, column, 1, keepdims=False)
        distance = (point_coords[0][:, :, None] - site_block[0][:, None, :]) ** 2
        distance = distance + (point_coords[1][:, :, None] - site_block[1][:, None, :]) ** 2
        distance = distance + (point_coords[2][:, :, None] - site_block[2][:, None, :]) ** 2
        scores = (site_block[3][:, None, :] - distance) / EPSILON
        column_live = lax.dynamic_index_in_dim(live_mask, column, 0, keepdims=False)
        return jnp.where(column_live[:, None, None], scores, -jnp.inf)

    first_scores = block_scores(0)
    running_max = jnp.max(first_scores, axis=2)
    running_sum = jnp.sum(jnp.exp(first_scores - running_max[:, :, None]), axis=2)

    def absorb(column, state_in):
        old_max, old_sum = state_in
        scores = block_scores(column)
        new_max = jnp.maximum(old_max, jnp.max(scores, axis=2))
        new_sum = old_sum * jnp.exp(old_max - new_max) + jnp.sum(
            jnp.exp(scores - new_max[:, :, None]), axis=2
        )
        return (new_max, new_sum)

    running_max, running_sum = lax.fori_loop(1, CAND, absorb, (running_max, running_sum))
    potential = running_max + jnp.log(running_sum)
    loadings = jnp.stack(
        [
            weights_in,
            weights_in * point_coords[0],
            weights_in * point_coords[1],
            weights_in * point_coords[2],
        ]
    )

    def moment_block(column):
        transport = jnp.exp(block_scores(column) - potential[:, :, None])
        return jnp.einsum("ktp,tps->tks", loadings, transport, precision=lax.Precision.HIGHEST)

    moments = lax.map(moment_block, jnp.arange(CAND))
    outgoing = (
        jnp.zeros((slot_total, 4, SITE_BLOCK), jnp.float32)
        .at[target]
        .set(moments.reshape(entry_total, 4, SITE_BLOCK))
    )
    returned = lax.all_to_all(
        outgoing.reshape(owner_total, capacity, 4, SITE_BLOCK),
        ("gx", "gy"),
        split_axis=0,
        concat_axis=0,
        tiled=True,
    )
    returned = returned.reshape(slot_total, 4, SITE_BLOCK)
    slot_hits = (asked_flat[:, None] == jnp.arange(SB_DEV)[None, :]).astype(jnp.float32)
    site_sums = jnp.einsum(
        "rb,rks->kbs", slot_hits, returned, precision=lax.Precision.HIGHEST
    ).reshape(4, SB_DEV * SITE_BLOCK)
    site_mass = site_sums[0]
    barycentre = (site_sums[1:4] + PRIOR_MASS * site_position) / (site_mass[None, :] + PRIOR_MASS)
    return (potential.reshape(PZ, rows_dev, TILE), site_mass, barycentre)


def solution(mesh):
    in_specs = (
        P(None, "gy", "gx"),
        P(None, None, "gy", "gx"),
        P(None, "gy", "gx"),
        P(None, "gy", "gx"),
        P(None, "gy", "gx"),
        P(None, ("gx", "gy")),
        P(("gx", "gy")),
    )
    out_specs = (P(None, "gy", "gx"), P(("gx", "gy")), P(None, ("gx", "gy")))
    return jax.shard_map(local, mesh=mesh, in_specs=in_specs, out_specs=out_specs, check_vma=False)
```

profile of v0, /device:TPU:1, one launch (start us, length us, event | category | flops | bytes accessed | tf_op | source)
XLA Modules:
  0.0 267.5 jit_solution(12814210319235461552)
XLA Ops:
  10.8 11.0 %all-to-all-start = ((s32[128,1,4]{2,1,0:T(1,128)}), s32[128,1,4]{2,1,0:T(1,128)S(1)}, u32[]{:S(2)}, u32[]{:S(2)}) async-start(s32[128,1,4]{2,1,0:T(1,128)} %bitcast.28), calls=%async_computation | async-start | bytes 131072 | tf_op jit(solution)/shard_map/all_to_all | solution.py:85
  25.6 5.9 %all-to-all-done = s32[128,1,4]{2,1,0:T(1,128)S(1)} async-done(((s32[128,1,4]{2,1,0:T(1,128)}), s32[128,1,4]{2,1,0:T(1,128)S(1)}, u32[]{:S(2)}, u32[]{:S(2)}) %all-to-all-start) | async-done | bytes 2080 | tf_op jit(solution)/shard_map/all_to_all | solution.py:85
  37.6 4.3 %all-to-all-start.1 = ((f32[4,128,4,128]{3,0,2,1:T(4,128)}), f32[4,128,4,128]{3,0,2,1:T(4,128)S(1)}, u32[]{:S(2)}, u32[]{:S(2)}) async-start(f32[4,128,4,128]{3,0,2,1:T(4,128)} %select_multiply_fusion), calls=%async_computation.1 | async-start | bytes 2097152 | tf_op jit(solution)/shard_map/all_to_all | solution.py:98
  41.9 10.6 %fusion.89 = f32[2,8,128]{2,1,0:T(8,128)S(1)} fusion(f32[2,8,8]{2,1,0:T(8,128)S(1)} %collective-permute-done, f32[2,8,128]{2,1,0:T(8,128)S(1)} %copy-done.5, f32[2,8,136]{2,1,0:T(8,128)S(1)} %constant_dynamic-update-slice_fusion, f32[]{:T(128)} %bitcast.63, f32[]{:T(128)} %bitcast.62, f32[]{:T(128)} %bitcast.61, f32[]{:T(128)} %bitcast.60, f32[]{:T(128)} %bitcast.59, ...), kind=kLoop, calls=%fused_computation.170 | loop fusion | flops 83968 | bytes 82500 | tf_op jit(solution)/shard_map/add | solution.py:44
  54.0 4.3 %collective-permute-start.3 = (f32[2,8,128]{2,1,0:T(8,128)S(1)}, f32[2,8,128]{2,1,0:T(8,128)S(1)}, u32[]{:S(2)}, u32[]{:S(2)}) collective-permute-start(f32[2,8,128]{2,1,0:T(8,128)S(1)} %fusion.89), channel_id=1, source_target_pairs={{1,0},{2,1},{3,2},{4,3},{5,4},{6,5},{7,6},{8,7},{9,8},{10,9},{11,1... | collective-permute-start | bytes 24584 | tf_op jit(solution)/shard_map/ppermute | solution.py:28
  67.0 10.5 %fusion.41 = f32[2,8,128]{2,1,0:T(8,128)S(1)} fusion(f32[2,8,128]{2,1,0:T(8,128)S(1)} %fusion.89, f32[2,8,128]{2,1,0:T(8,128)S(1)} %collective-permute-done.3, f32[2,8,128]{2,1,0:T(8,128)S(1)} %collective-permute-done.2, f32[]{:T(128)} %bitcast.63, f32[]{:T(128)} %bitcast.62, f32[]{:T(128)} %bitcast.61, f32[]{:T(128)} %bitcast.60, f32[]{:T(128)} %bitcast.59, ...), kind=kLoop, calls=%fused_computation.122 | loop fusion | flops 96256 | bytes 32836 | tf_op jit(solution)/shard_map/add | solution.py:44
  84.0 50.8 %while.27 = (s32[]{:T(128)}, f32[16,128]{1,0:T(8,128)S(1)}, f32[16,128]{1,0:T(8,128)S(1)}, pred[16,16]{1,0:T(8,128)(4,1)S(1)}, f32[4,16,16,128]{3,2,1,0:T(8,128)...) while((s32[]{:T(128)}, f32[16,128]{1,0:T(8,128)S(1)}, ...), condition=%wide.region_9.10_spmd, body=%wide.region_6.9_spmd.sunk | while | flops 6557704 | bytes 336151 | solution.py:133
  134.9 92.4 %while.28 = (s32[]{:T(128)}, f32[16,16,4,128]{3,2,1,0:T(4,128)}, s32[16]{0:T(128)S(1)}, pred[16,16]{1,0:T(8,128)(4,1)S(1)}, f32[4,16,16,128]{3,2,1,0:T(8,128)S(1...) while((s32[]{:T(128)}, f32[16,16,4,128]{3,2,1,0:T(4,128)}, ...), condition=%wide.region_12.13_spmd, body=%wide.region_11.12_spmd.sunk | while | flops 15728648 | bytes 246555 | solution.py:148
  137.5 3.2 %fusion.138 = f32[16,16,4,128]{3,2,1,0:T(4,128)} fusion(f32[16,16,4,128]{3,2,1,0:T(4,128)} %get-tuple-element.519, s32[]{:T(128)} %get-tuple-element.518, f32[4,16,128]{2,0,1:T(4,128)S(1)} %get-tuple-element.539, f32[16,128]{1,0:T(8,128)S(1)} %get-tuple-element.538, f32[16,128]{1,0:T(8,128)S(1)} %get-tuple-element.461, ...), kind=kOutput, calls=%fused_computation.17.clone.1 | convolution fusion | flops 15728640 | bytes 131600 | tf_op jit(solution)/shard_map/while/body/eval_jaxpr/ktp,tps->tks/dot_general | solution.py:146
  143.2 3.2 %fusion.138 = f32[16,16,4,128]{3,2,1,0:T(4,128)} fusion(f32[16,16,4,128]{3,2,1,0:T(4,128)} %get-tuple-element.519, s32[]{:T(128)} %get-tuple-element.518, f32[4,16,128]{2,0,1:T(4,128)S(1)} %get-tuple-element.539, f32[16,128]{1,0:T(8,128)S(1)} %get-tuple-element.538, f32[16,128]{1,0:T(8,128)S(1)} %get-tuple-element.461, ...), kind=kOutput, calls=%fused_computation.17.clone.1 | convolution fusion | flops 15728640 | bytes 131600 | tf_op jit(solution)/shard_map/while/body/eval_jaxpr/ktp,tps->tks/dot_general | solution.py:146
  154.8 3.2 %fusion.138 = f32[16,16,4,128]{3,2,1,0:T(4,128)} fusion(f32[16,16,4,128]{3,2,1,0:T(4,128)} %get-tuple-element.519, s32[]{:T(128)} %get-tuple-element.518, f32[4,16,128]{2,0,1:T(4,128)S(1)} %get-tuple-element.539, f32[16,128]{1,0:T(8,128)S(1)} %get-tuple-element.538, f32[16,128]{1,0:T(8,128)S(1)} %get-tuple-element.461, ...), kind=kOutput, calls=%fused_computation.17.clone.1 | convolution fusion | flops 15728640 | bytes 131600 | tf_op jit(solution)/shard_map/while/body/eval_jaxpr/ktp,tps->tks/dot_general | solution.py:146
  160.6 3.2 %fusion.138 = f32[16,16,4,128]{3,2,1,0:T(4,128)} fusion(f32[16,16,4,128]{3,2,1,0:T(4,128)} %get-tuple-element.519, s32[]{:T(128)} %get-tuple-element.518, f32[4,16,128]{2,0,1:T(4,128)S(1)} %get-tuple-element.539, f32[16,128]{1,0:T(8,128)S(1)} %get-tuple-element.538, f32[16,128]{1,0:T(8,128)S(1)} %get-tuple-element.461, ...), kind=kOutput, calls=%fused_computation.17.clone.1 | convolution fusion | flops 15728640 | bytes 131600 | tf_op jit(solution)/shard_map/while/body/eval_jaxpr/ktp,tps->tks/dot_general | solution.py:146
  166.3 3.2 %fusion.138 = f32[16,16,4,128]{3,2,1,0:T(4,128)} fusion(f32[16,16,4,128]{3,2,1,0:T(4,128)} %get-tuple-element.519, s32[]{:T(128)} %get-tuple-element.518, f32[4,16,128]{2,0,1:T(4,128)S(1)} %get-tuple-element.539, f32[16,128]{1,0:T(8,128)S(1)} %get-tuple-element.538, f32[16,128]{1,0:T(8,128)S(1)} %get-tuple-element.461, ...), kind=kOutput, calls=%fused_computation.17.clone.1 | convolution fusion | flops 15728640 | bytes 131600 | tf_op jit(solution)/shard_map/while/body/eval_jaxpr/ktp,tps->tks/dot_general | solution.py:146
  172.1 3.2 %fusion.138 = f32[16,16,4,128]{3,2,1,0:T(4,128)} fusion(f32[16,16,4,128]{3,2,1,0:T(4,128)} %get-tuple-element.519, s32[]{:T(128)} %get-tuple-element.518, f32[4,16,128]{2,0,1:T(4,128)S(1)} %get-tuple-element.539, f32[16,128]{1,0:T(8,128)S(1)} %get-tuple-element.538, f32[16,128]{1,0:T(8,128)S(1)} %get-tuple-element.461, ...), kind=kOutput, calls=%fused_computation.17.clone.1 | convolution fusion | flops 15728640 | bytes 131600 | tf_op jit(solution)/shard_map/while/body/eval_jaxpr/ktp,tps->tks/dot_general | solution.py:146
  177.9 3.2 %fusion.138 = f32[16,16,4,128]{3,2,1,0:T(4,128)} fusion(f32[16,16,4,128]{3,2,1,0:T(4,128)} %get-tuple-element.519, s32[]{:T(128)} %get-tuple-element.518, f32[4,16,128]{2,0,1:T(4,128)S(1)} %get-tuple-element.539, f32[16,128]{1,0:T(8,128)S(1)} %get-tuple-element.538, f32[16,128]{1,0:T(8,128)S(1)} %get-tuple-element.461, ...), kind=kOutput, calls=%fused_computation.17.clone.1 | convolution fusion | flops 15728640 | bytes 131600 | tf_op jit(solution)/shard_map/while/body/eval_jaxpr/ktp,tps->tks/dot_general | solution.py:146
  189.4 3.2 %fusion.138 = f32[16,16,4,128]{3,2,1,0:T(4,128)} fusion(f32[16,16,4,128]{3,2,1,0:T(4,128)} %get-tuple-element.519, s32[]{:T(128)} %get-tuple-element.518, f32[4,16,128]{2,0,1:T(4,128)S(1)} %get-tuple-element.539, f32[16,128]{1,0:T(8,128)S(1)} %get-tuple-element.538, f32[16,128]{1,0:T(8,128)S(1)} %get-tuple-element.461, ...), kind=kOutput, calls=%fused_computation.17.clone.1 | convolution fusion | flops 15728640 | bytes 131600 | tf_op jit(solution)/shard_map/while/body/eval_jaxpr/ktp,tps->tks/dot_general | solution.py:146
  195.2 3.2 %fusion.138 = f32[16,16,4,128]{3,2,1,0:T(4,128)} fusion(f32[16,16,4,128]{3,2,1,0:T(4,128)} %get-tuple-element.519, s32[]{:T(128)} %get-tuple-element.518, f32[4,16,128]{2,0,1:T(4,128)S(1)} %get-tuple-element.539, f32[16,128]{1,0:T(8,128)S(1)} %get-tuple-element.538, f32[16,128]{1,0:T(8,128)S(1)} %get-tuple-element.461, ...), kind=kOutput, calls=%fused_computation.17.clone.1 | convolution fusion | flops 15728640 | bytes 131600 | tf_op jit(solution)/shard_map/while/body/eval_jaxpr/ktp,tps->tks/dot_general | solution.py:146
  206.8 3.2 %fusion.138 = f32[16,16,4,128]{3,2,1,0:T(4,128)} fusion(f32[16,16,4,128]{3,2,1,0:T(4,128)} %get-tuple-element.519, s32[]{:T(128)} %get-tuple-element.518, f32[4,16,128]{2,0,1:T(4,128)S(1)} %get-tuple-element.539, f32[16,128]{1,0:T(8,128)S(1)} %get-tuple-element.538, f32[16,128]{1,0:T(8,128)S(1)} %get-tuple-element.461, ...), kind=kOutput, calls=%fused_computation.17.clone.1 | convolution fusion | flops 15728640 | bytes 131600 | tf_op jit(solution)/shard_map/while/body/eval_jaxpr/ktp,tps->tks/dot_general | solution.py:146
  212.5 3.2 %fusion.138 = f32[16,16,4,128]{3,2,1,0:T(4,128)} fusion(f32[16,16,4,128]{3,2,1,0:T(4,128)} %get-tuple-element.519, s32[]{:T(128)} %get-tuple-element.518, f32[4,16,128]{2,0,1:T(4,128)S(1)} %get-tuple-element.539, f32[16,128]{1,0:T(8,128)S(1)} %get-tuple-element.538, f32[16,128]{1,0:T(8,128)S(1)} %get-tuple-element.461, ...), kind=kOutput, calls=%fused_computation.17.clone.1 | convolution fusion | flops 15728640 | bytes 131600 | tf_op jit(solution)/shard_map/while/body/eval_jaxpr/ktp,tps->tks/dot_general | solution.py:146
  218.3 3.2 %fusion.138 = f32[16,16,4,128]{3,2,1,0:T(4,128)} fusion(f32[16,16,4,128]{3,2,1,0:T(4,128)} %get-tuple-element.519, s32[]{:T(128)} %get-tuple-element.518, f32[4,16,128]{2,0,1:T(4,128)S(1)} %get-tuple-element.539, f32[16,128]{1,0:T(8,128)S(1)} %get-tuple-element.538, f32[16,128]{1,0:T(8,128)S(1)} %get-tuple-element.461, ...), kind=kOutput, calls=%fused_computation.17.clone.1 | convolution fusion | flops 15728640 | bytes 131600 | tf_op jit(solution)/shard_map/while/body/eval_jaxpr/ktp,tps->tks/dot_general | solution.py:146
  224.1 3.2 %fusion.138 = f32[16,16,4,128]{3,2,1,0:T(4,128)} fusion(f32[16,16,4,128]{3,2,1,0:T(4,128)} %get-tuple-element.519, s32[]{:T(128)} %get-tuple-element.518, f32[4,16,128]{2,0,1:T(4,128)S(1)} %get-tuple-element.539, f32[16,128]{1,0:T(8,128)S(1)} %get-tuple-element.538, f32[16,128]{1,0:T(8,128)S(1)} %get-tuple-element.461, ...), kind=kOutput, calls=%fused_computation.17.clone.1 | convolution fusion | flops 15728640 | bytes 131600 | tf_op jit(solution)/shard_map/while/body/eval_jaxpr/ktp,tps->tks/dot_general | solution.py:146
  228.3 7.0 %scatter_fusion = f32[512,4,128]{2,1,0:T(4,128)S(1)} fusion(f32[512,4,128]{2,1,0:T(4,128)S(1)} %broadcast_in_dim.120, s32[256]{0:T(256)S(1)} %bitcast.175, f32[256,4,128]{2,1,0:T(4,128)S(1)} %bitcast.159), kind=kCustom, calls=%fused_computation.3 | custom fusion | bytes 1573888 | tf_op jit(solution)/shard_map/scatter | solution.py:152
  236.6 6.2 %all-to-all-start.2 = ((f32[128,4,4,128]{3,1,2,0:T(4,128)}), f32[128,4,4,128]{3,1,2,0:T(4,128)S(1)}, u32[]{:S(2)}, u32[]{:S(2)}) async-start(f32[128,4,4,128]{3,1,2,0:T(4,128)} %copy.75), calls=%async_computation.2 | async-start | bytes 2097152 | tf_op jit(solution)/shard_map/all_to_all | solution.py:154
  242.8 18.8 %all-to-all-done.2 = f32[128,4,4,128]{3,1,2,0:T(4,128)S(1)} async-done(((f32[128,4,4,128]{3,1,2,0:T(4,128)}), f32[128,4,4,128]{3,1,2,0:T(4,128)S(1)}, u32[]{:S(2)}, u32[]{:S(2)}) %all-to-all-start.2) | async-done | bytes 1048608 | tf_op jit(solution)/shard_map/all_to_all | solution.py:154
  (276 shorter events, 105.0 us)
Async XLA Ops:
  0.6 23.5 %copy-start = (f32[3,65536]{1,0:T(4,128)S(1)}, f32[3,65536]{1,0:T(4,128)}, u32[]{:S(2)}) copy-start(f32[3,65536]{1,0:T(4,128)} %param.16) | copy-start | bytes 2359300
  1.5 24.1 %collective-permute-start.1 = (f32[2,8,8]{2,1,0:T(8,128)S(1)}, f32[2,8,8]{2,1,0:T(8,128)S(1)}, u32[]{:S(2)}, u32[]{:S(2)}) collective-permute-start(f32[2,8,8]{2,1,0:T(8,128)S(1)} %get-tuple-element.332), channel_id=1, source_target_pairs={{16,0},{32,16},{48,32},{64,48},{80,64},{96,80},{112,96},{0,112},{1... | collective-permute-start | bytes 1544 | tf_op jit(solution)/shard_map/ppermute | solution.py:28
  2.9 39.0 %collective-permute-start = (f32[2,8,8]{2,1,0:T(8,128)S(1)}, f32[2,8,8]{2,1,0:T(8,128)S(1)}, u32[]{:S(2)}, u32[]{:S(2)}) collective-permute-start(f32[2,8,8]{2,1,0:T(8,128)S(1)} %get-tuple-element.333), channel_id=1, source_target_pairs={{0,16},{16,32},{32,48},{48,64},{64,80},{80,96},{96,112},{112,0},{1... | collective-permute-start | bytes 1544 | tf_op jit(solution)/shard_map/ppermute | solution.py:26
  10.8 20.8 %all-to-all-start = ((s32[128,1,4]{2,1,0:T(1,128)}), s32[128,1,4]{2,1,0:T(1,128)S(1)}, u32[]{:S(2)}, u32[]{:S(2)}) async-start(s32[128,1,4]{2,1,0:T(1,128)} %bitcast.28), calls=%async_computation | async-start | bytes 131072 | tf_op jit(solution)/shard_map/all_to_all | solution.py:85
  21.8 2.2 copy-start.2
  24.1 1.4 copy-start.5
  37.6 41.9 %all-to-all-start.1 = ((f32[4,128,4,128]{3,0,2,1:T(4,128)}), f32[4,128,4,128]{3,0,2,1:T(4,128)S(1)}, u32[]{:S(2)}, u32[]{:S(2)}) async-start(f32[4,128,4,128]{3,0,2,1:T(4,128)} %select_multiply_fusion), calls=%async_computation.1 | async-start | bytes 2097152 | tf_op jit(solution)/shard_map/all_to_all | solution.py:98
  52.5 14.4 %collective-permute-start.2 = (f32[2,8,128]{2,1,0:T(8,128)S(1)}, f32[2,8,128]{2,1,0:T(8,128)S(1)}, u32[]{:S(2)}, u32[]{:S(2)}) collective-permute-start(f32[2,8,128]{2,1,0:T(8,128)S(1)} %fusion.89), channel_id=1, source_target_pairs={{0,1},{1,2},{2,3},{3,4},{4,5},{5,6},{6,7},{7,8},{8,9},{9,10},{10,1... | collective-permute-start | bytes 24584 | tf_op jit(solution)/shard_map/ppermute | solution.py:26
  54.0 13.0 %collective-permute-start.3 = (f32[2,8,128]{2,1,0:T(8,128)S(1)}, f32[2,8,128]{2,1,0:T(8,128)S(1)}, u32[]{:S(2)}, u32[]{:S(2)}) collective-permute-start(f32[2,8,128]{2,1,0:T(8,128)S(1)} %fusion.89), channel_id=1, source_target_pairs={{1,0},{2,1},{3,2},{4,3},{5,4},{6,5},{7,6},{8,7},{9,8},{10,9},{11,1... | collective-permute-start | bytes 24584 | tf_op jit(solution)/shard_map/ppermute | solution.py:28
  227.3 0.6 copy-start.6
  227.3 1.0 copy-start.4
  236.6 25.1 %all-to-all-start.2 = ((f32[128,4,4,128]{3,1,2,0:T(4,128)}), f32[128,4,4,128]{3,1,2,0:T(4,128)S(1)}, u32[]{:S(2)}, u32[]{:S(2)}) async-start(f32[128,4,4,128]{3,1,2,0:T(4,128)} %copy.75), calls=%async_computation.2 | async-start | bytes 2097152 | tf_op jit(solution)/shard_map/all_to_all | solution.py:154
  263.0 1.0 copy-start.1
  264.0 0.9 slice-start
  265.0 0.7 copy-start.3
where the time goes:
time: 269 us; the launch traced here: 267 us
  other arithmetic  86.4 us (32%)
  matrix products  52.3 us (19%)
  loops' own time  32.7 us (12%)
  local copies, waits for them, and re-layouts  32 us (12%)
  starting transfers between devices  29.8 us (11%)
  waiting for transfers between devices  24.7 us (9%)
  between operations  9.63 us (4%)
    dot_general x16, matrix products, moment_block(): jnp.einsum('ktp,tps->tks', loadings, transport, precision=lax.Precision.H...  51.1 us
    another operation x1, loops' own time, local(): moments = lax.map(moment_block, jnp.arange(CAND))  31.5 us
    reduce_sum x15, other arithmetic, absorb(): jnp.sum(jnp.exp(scores - new_max[:, :, None]), axis=2)  28.9 us
    add x2, other arithmetic, extended_pass(): running + kernel[offset] * lax.slice_in_dim(padded, offset, offset + leng...  21.2 us
    reduce_max x15, other arithmetic, absorb(): new_max = jnp.maximum(old_max, jnp.max(scores, axis=2))  20 us
    all_to_all x1, waiting for transfers between devices, local(): lax.all_to_all(outgoing.reshape(owner_total, capacity, 4, SITE_BLOCK), ('...  18.8 us
    all_to_all x1, starting transfers between devices, local(): lax.all_to_all(requests.reshape(owner_total, capacity), ('gx', 'gy'), spl...  11 us
    dynamic_slice x16, local copies, waits for them, and re-layouts, local(): moments = lax.map(moment_block, jnp.arange(CAND))  9.32 us
  transfers between devices with their start and end apart: 7, of which 2 were waited for; matrix products, arithmetic and copies ran while one was open for 15% of the time, Pallas kernels for 0%

commit v1 on v0

v1 whole, which is shorter than its diff:
```python
import math

import jax
import jax.numpy as jnp
import numpy as np
from jax import lax
from jax.experimental import pallas as pl
from jax.experimental.pallas import tpu as pltpu
from jax.sharding import PartitionSpec as P

PZ = 2
CY = 8
TILE = 128
CAND = 16
SITE_BLOCK = 128
SB_DEV = 512
HALF = 8
CAP = 4
OWNERS = 128
TILES = PZ * CY
SLOTS = OWNERS * CAP
ENTRIES = TILES * CAND

EPSILON = 0.05
PRIOR_MASS = 0.5
SIGMA_CELLS = 4.0
KAPPA = math.log2(math.e) / EPSILON
DEAD = -1e30
F32 = jnp.float32
BF16 = jnp.bfloat16
I32 = jnp.int32
VMEM = pl.BlockSpec(memory_space=pltpu.VMEM)
SMEM = pl.BlockSpec(memory_space=pltpu.SMEM)
AXES = ("gx", "gy")


def gauss_values():
    offsets = np.arange(-HALF, HALF + 1, dtype=np.float64)
    values = np.exp(-offsets * offsets / (2.0 * SIGMA_CELLS * SIGMA_CELLS))
    return values / values.sum()


GAUSS = [float(v) for v in gauss_values()]
GAUSS_PEAK = GAUSS[HALF]


def iota(shape, dim):
    return lax.broadcasted_iota(I32, shape, dim)


def rounded(values):
    return values.astype(BF16).astype(F32)


def request_kernel(owner_ref, slot_ref, count_ref, request_ref, target_ref):
    owners = owner_ref[...]
    slots = slot_ref[...]
    counts = count_ref[...]
    lane = iota((TILES, 128), 1)
    hots = []
    values = []
    for k in range(CAND):
        hots.append((owners[:, k : k + 1] == lane).astype(F32))
        values.append(jnp.where(k < counts, slots[:, k : k + 1] + 1, 0))
    hot = jnp.concatenate(hots, axis=0)
    value = jnp.concatenate(values, axis=0)
    square = (ENTRIES, ENTRIES)
    lower = (iota(square, 1) < iota(square, 0)).astype(F32).astype(BF16)
    hot_low = hot.astype(BF16)
    before = jnp.dot(lower, hot_low, preferred_element_type=F32)
    rank = jnp.sum(before * hot, axis=1, keepdims=True).astype(I32)
    wide = iota((ENTRIES, 128), 1)
    high_part = (value & -32).astype(F32)
    low_part = (value & 31).astype(F32)
    spread = jnp.where(wide == rank, high_part, 0.0) + jnp.where(wide == rank + CAP, low_part, 0.0)
    request = lax.dot_general(
        hot_low, spread.astype(BF16), (((0,), (0,)), ((), ())), preferred_element_type=F32
    )
    request = request + pltpu.roll(request, 128 - CAP, 1)
    request_ref[...] = request.astype(I32) - 1
    target = jnp.where(lane == CAND, counts, 0)
    for k in range(CAND):
        place = owners[:, k : k + 1] * CAP + rank[k * TILES : (k + 1) * TILES]
        target = jnp.where(lane == k, place, target)
    target_ref[...] = target


def gather_kernel(asked_ref, position_ref, weight_ref, out_ref, ids_ref, ids_smem, sem):
    ids_ref[...] = jnp.transpose(asked_ref[...].astype(F32))[0:8].astype(I32)
    copy = pltpu.make_async_copy(ids_ref, ids_smem, sem)
    copy.start()
    copy.wait()

    def peer(step, carry):
        for r in range(CAP):
            asked = ids_smem[r, step]
            block = jnp.maximum(asked, 0)
            start = pl.multiple_of(block * SITE_BLOCK, SITE_BLOCK)
            weight = weight_ref[pl.ds(block, 1), :]
            out_ref[step * CAP + r, 0:3, :] = position_ref[:, pl.ds(start, SITE_BLOCK)]
            out_ref[step * CAP + r, 3:4, :] = jnp.where(asked >= 0, weight, DEAD)
        return carry

    lax.fori_loop(0, OWNERS, peer, 0, unroll=4)


def filter_kernel(left_ref, mid_ref, right_ref, out_ref):
    shape = (3 * TILE, TILE)
    shift = iota(shape, 0) - iota(shape, 1) - TILE
    taps = jnp.zeros(shape, F32)
    for offset in range(HALF + 1):
        taps = jnp.where(jnp.abs(shift) == offset, GAUSS[HALF + offset], taps)
    cells = jnp.concatenate([left_ref[...], mid_ref[...], right_ref[...]], axis=1)
    out_ref[...] = jnp.dot(
        cells, taps, preferred_element_type=F32, precision=lax.Precision.HIGHEST
    )


def transport_kernel(
    target_ref,
    arrived_ref,
    point_ref,
    above_ref,
    mid_ref,
    below_ref,
    potential_ref,
    out_ref,
    rows_ref,
    load_ref,
    top_ref,
    sum_ref,
    e_ref,
):
    planes = []
    for z in range(PZ):
        rows_ref[z, 0:CY, :] = above_ref[z * CY : (z + 1) * CY, :]
        rows_ref[z, CY : 2 * CY, :] = mid_ref[z * CY : (z + 1) * CY, :]
        rows_ref[z, 2 * CY : 3 * CY, :] = below_ref[z * CY : (z + 1) * CY, :]
        total = GAUSS[0] * rows_ref[z, 0:CY, :]
        for j in range(1, 2 * HALF + 1):
            total = total + GAUSS[j] * rows_ref[z, j : j + CY, :]
        planes.append(total)
    load_ref[0:CY, :] = GAUSS[HALF] * planes[0] + GAUSS[HALF + 1] * planes[1]
    load_ref[CY : 2 * CY, :] = GAUSS[HALF - 1] * planes[0] + GAUSS[HALF] * planes[1]

    def tile_top(t, carry):
        top = arrived_ref[target_ref[t, 0], 3:4, :]
        for k in range(1, CAND):
            top = jnp.maximum(top, arrived_ref[target_ref[t, k], 3:4, :])
        top_ref[pl.ds(t, 1), :] = top
        return carry

    lax.fori_loop(0, TILES, tile_top, 0)
    top_ref[...] = jnp.broadcast_to(
        jnp.max(top_ref[...], axis=1, keepdims=True), (TILES, 128)
    )

    row = iota((8, 128), 0)

    def tile_step(t, carry):
        coords = [point_ref[c, pl.ds(t, 1), :] for c in range(3)]
        point = jnp.where(
            row % 4 == 0,
            coords[0],
            jnp.where(row % 4 == 1, coords[1], jnp.where(row % 4 == 2, coords[2], 1.0)),
        )
        scaled = jnp.where(row < 3, (2.0 * KAPPA) * (point - 0.5), 0.0)
        a1 = rounded(scaled)
        rest = scaled - a1
        a2 = rounded(rest)
        a3 = rest - a2
        lead = jnp.where(row >= 4, 1.0, a1)
        lhs = jnp.concatenate([lead, lead, lead, a2, a2, a3], axis=0)
        lhs = jnp.transpose(lhs).astype(BF16)
        centre = jnp.where(row % 4 == 3, top_ref[pl.ds(t, 1), :], 0.5)

        def spread(k):
            block = arrived_ref[target_ref[t, k]]
            both = jnp.concatenate([block, block], axis=0) - centre
            terms = jnp.where(
                row < 4, both, both * jnp.where(row == 7, KAPPA, -KAPPA * both)
            )
            t1 = rounded(terms)
            rest = terms - t1
            t2 = rounded(rest)
            t3 = rest - t2
            return jnp.concatenate([t1, t2, t3, t1, t2, t1], axis=0).astype(BF16)

        total = None
        for q in range(CAND // 2):
            rhs = jnp.concatenate([spread(2 * q), spread(2 * q + 1)], axis=1)
            e = jnp.exp2(jnp.dot(lhs, rhs, preferred_element_type=F32))
            part = e[:, :128] + e[:, 128:]
            total = part if total is None else total + part
            high = e.astype(BF16)
            e_ref[q, 0:128, :] = high
            e_ref[q, 128:256, :] = (e - high.astype(F32)).astype(BF16)
        sums = jnp.sum(jnp.transpose(total), axis=0, keepdims=True)
        sum_ref[pl.ds(t, 1), :] = sums
        unit = load_ref[pl.ds(t, 1), :] / sums
        loads = unit * point
        high = rounded(loads)
        half = jnp.where(row < 4, high, loads - high).astype(BF16)
        lhs2 = jnp.concatenate([half, half], axis=1)
        for q in range(CAND // 2):
            found = jnp.dot(lhs2, e_ref[q], preferred_element_type=F32)
            found = found[0:4] + found[4:8]
            out_ref[target_ref[t, 2 * q]] = found[:, :128]
            out_ref[target_ref[t, 2 * q + 1]] = found[:, 128:]
        return carry

    lax.fori_loop(0, TILES, tile_step, 0)
    square = (
        (point_ref[0] - 0.5) ** 2 + (point_ref[1] - 0.5) ** 2 + (point_ref[2] - 0.5) ** 2
    )
    potential_ref[...] = jnp.log(sum_ref[...]) + (top_ref[...] - square) / EPSILON


def reduce_kernel(ids_ref, back_ref, position_ref, mass_ref, centre_ref, acc_ref, scale_ref):
    acc_ref[...] = jnp.zeros_like(acc_ref)

    def peer(step, carry):
        places = []
        sums = []
        for r in range(CAP):
            asked = ids_ref[r, step]
            place = jnp.where(asked < 0, SB_DEV + r, asked)
            places.append(place)
            sums.append(acc_ref[place] + back_ref[step * CAP + r])
        for place, total in zip(places, sums):
            acc_ref[place] = total
        return carry

    lax.fori_loop(0, OWNERS, peer, 0, unroll=2)
    mass = acc_ref[0:SB_DEV, 3, :]
    mass_ref[...] = mass
    scale_ref[...] = 1.0 / (mass + PRIOR_MASS)

    def finish(b, carry):
        start = pl.multiple_of(b * SITE_BLOCK, SITE_BLOCK)
        place = position_ref[:, pl.ds(start, SITE_BLOCK)]
        centre_ref[:, pl.ds(start, SITE_BLOCK)] = (
            acc_ref[b, 0:3, :] + PRIOR_MASS * place
        ) * scale_ref[pl.ds(b, 1), :]
        return carry

    lax.fori_loop(0, SB_DEV, finish, 0, unroll=8)


def shape_of(*dims, dtype=F32):
    return jax.ShapeDtypeStruct(dims, dtype)


def exchange(values):
    return lax.all_to_all(values, AXES, split_axis=0, concat_axis=0, tiled=True)


def neighbours(values, axis):
    count = lax.axis_size(axis)
    before = lax.ppermute(values, axis, [(i, (i + 1) % count) for i in range(count)])
    after = lax.ppermute(values, axis, [((i + 1) % count, i) for i in range(count)])
    return before, after


def local(
    density, point_position, block_owner, block_slot, block_count, site_position, site_weight
):
    cells = density.reshape(TILES, TILE)
    left, right = neighbours(cells, "gx")
    request, target = pl.pallas_call(
        request_kernel,
        out_shape=(shape_of(OWNERS, 128, dtype=I32), shape_of(TILES, 128, dtype=I32)),
        in_specs=[VMEM] * 3,
        out_specs=(VMEM, VMEM),
        name="request",
    )(
        block_owner.reshape(TILES, CAND),
        block_slot.reshape(TILES, CAND),
        block_count.reshape(TILES, 1),
    )
    asked = exchange(request)
    blocks, ids = pl.pallas_call(
        gather_kernel,
        out_shape=(shape_of(SLOTS, 4, SITE_BLOCK), shape_of(8, 128, dtype=I32)),
        in_specs=[VMEM] * 3,
        out_specs=(VMEM, VMEM),
        scratch_shapes=[pltpu.SMEM((8, 128), I32), pltpu.SemaphoreType.DMA],
        name="gather",
    )(asked, site_position, site_weight.reshape(SB_DEV, SITE_BLOCK))
    arrived = exchange(blocks)
    first_pass = pl.pallas_call(
        filter_kernel,
        out_shape=shape_of(TILES, TILE),
        in_specs=[VMEM] * 3,
        out_specs=VMEM,
        name="filter",
    )(left, cells, right)
    above, below = neighbours(first_pass, "gy")
    potential, moments = pl.pallas_call(
        transport_kernel,
        out_shape=(shape_of(TILES, TILE), shape_of(SLOTS, 4, SITE_BLOCK)),
        in_specs=[SMEM] + [VMEM] * 5,
        out_specs=(VMEM, VMEM),
        scratch_shapes=[
            pltpu.VMEM((PZ, 3 * CY, 128), F32),
            pltpu.VMEM((TILES, 128), F32),
            pltpu.VMEM((TILES, 128), F32),
            pltpu.VMEM((TILES, 128), F32),
            pltpu.VMEM((CAND // 2, 256, 256), BF16),
        ],
        name="transport",
    )(target, arrived, point_position.reshape(3, TILES, TILE), above, first_pass, below)
    returned = exchange(moments)
    site_mass, barycentre = pl.pallas_call(
        reduce_kernel,
        out_shape=(shape_of(SB_DEV, SITE_BLOCK), shape_of(3, SB_DEV * SITE_BLOCK)),
        in_specs=[SMEM] + [VMEM] * 2,
        out_specs=(VMEM, VMEM),
        scratch_shapes=[
            pltpu.VMEM((SB_DEV + CAP, 4, SITE_BLOCK), F32),
            pltpu.VMEM((SB_DEV, SITE_BLOCK), F32),
        ],
        name="reduce",
    )(ids, returned, site_position)
    return (
        potential.reshape(PZ, CY, TILE),
        site_mass.reshape(SB_DEV * SITE_BLOCK),
        barycentre,
    )


def solution(mesh):
    in_specs = (
        P(None, "gy", "gx"),
        P(None, None, "gy", "gx"),
        P(None, "gy", "gx"),
        P(None, "gy", "gx"),
        P(None, "gy", "gx"),
        P(None, ("gx", "gy")),
        P(("gx", "gy")),
    )
    out_specs = (P(None, "gy", "gx"), P(("gx", "gy")), P(None, ("gx", "gy")))
    return jax.shard_map(local, mesh=mesh, in_specs=in_specs, out_specs=out_specs, check_vma=False)
```

time: 269 us -> 109 us (0.41)
  other arithmetic: 86.4 us -> 0.66 us
  matrix products: 52.3 us -> 0 us
  blocking collectives: 0 us -> 46.6 us
  loops' own time: 32.7 us -> 0 us
  local copies, waits for them, and re-layouts: 32 us -> 3.52 us
  Pallas kernels: 0 us -> 27.6 us
  starting transfers between devices: 29.8 us -> 11.5 us
  between operations: 9.63 us -> 0.69 us
  waiting for transfers between devices: 24.7 us -> 17.5 us
    dot_general x17 -> x0, matrix products: 52.3 us -> none  [the longest x16 51.1 us: moment_block(): jnp.einsum('ktp,tps->tks', loadings, transport, precision=lax.Precision.H...]
    all_to_all x0 -> x2, blocking collectives: none -> 46.6 us  [exchange(): return lax.all_to_all(values, AXES, split_axis=0, concat_axis=0, tiled=True)]
    another operation x2 -> x0, loops' own time: 32.7 us -> none  [the longest x1 31.5 us: local(): moments = lax.map(moment_block, jnp.arange(CAND))]
    reduce_sum x18 -> x0, other arithmetic: 31.6 us -> none  [the longest x15 28.9 us: absorb(): jnp.sum(jnp.exp(scores - new_max[:, :, None]), axis=2)]
    pallas_call x0 -> x5, Pallas kernels: none -> 27.6 us  [the longest x1 13.5 us: local(): pl.pallas_call(transport_kernel, out_shape=(shape_of(TILES, TILE), shape_...]
    all_to_all x3 -> x1, waiting for transfers between devices: 24.7 us -> 0.01 us  [exchange(): return lax.all_to_all(values, AXES, split_axis=0, concat_axis=0, tiled=True)]
    add x20 -> x0, other arithmetic: 23.3 us -> none  [the longest x2 21.2 us: extended_pass(): running + kernel[offset] * lax.slice_in_dim(padded, offset, offset + leng...]
    reduce_max x16 -> x0, other arithmetic: 21.3 us -> none  [the longest x15 20 us: absorb(): new_max = jnp.maximum(old_max, jnp.max(scores, axis=2))]
  transfers between devices with their start and end apart: 7 -> 5, of which waited for: 2 -> 3; matrix products, arithmetic and copies ran while one was open for 15% -> 0% of each run, Pallas kernels for 0% -> 1%
where the time goes in v1:
time: 109 us; the launch traced here: 108 us
  blocking collectives  46.6 us (43%)
  Pallas kernels  27.6 us (25%)
  waiting for transfers between devices  17.5 us (16%)
  starting transfers between devices  11.5 us (11%)
  local copies, waits for them, and re-layouts  3.52 us (3%)
    all_to_all x2, blocking collectives, exchange(): return lax.all_to_all(values, AXES, split_axis=0, concat_axis=0, tiled=True)  46.6 us
    pallas_call x1, Pallas kernels, local(): pl.pallas_call(transport_kernel, out_shape=(shape_of(TILES, TILE), shape_...  13.5 us
    ppermute x2, waiting for transfers between devices, neighbours(): lax.ppermute(values, axis, [((i + 1) % count, i) for i in range(count)])  12.5 us
    ppermute x2, starting transfers between devices, neighbours(): lax.ppermute(values, axis, [((i + 1) % count, i) for i in range(count)])  6.69 us
    pallas_call x1, Pallas kernels, local(): pl.pallas_call(reduce_kernel, out_shape=(shape_of(SB_DEV, SITE_BLOCK), sh...  5.58 us
    ppermute x2, waiting for transfers between devices, neighbours(): lax.ppermute(values, axis, [(i, (i + 1) % count) for i in range(count)])  5.03 us
    pallas_call x1, Pallas kernels, local(): pl.pallas_call(gather_kernel, out_shape=(shape_of(SLOTS, 4, SITE_BLOCK),...  4.95 us
    all_to_all x1, starting transfers between devices, exchange(): return lax.all_to_all(values, AXES, split_axis=0, concat_axis=0, tiled=True)  4.27 us
  transfers between devices with their start and end apart: 5, of which 3 were waited for; matrix products, arithmetic and copies ran while one was open for 0% of the time, Pallas kernels for 1%

profile of v1, /device:TPU:1, one launch (start us, length us, event | category | flops | bytes accessed | tf_op | source)
XLA Modules:
  0.0 108.2 jit_solution(945844863347051949)
XLA Ops:
  0.6 0.5 broadcast.3
  1.2 0.2 copy-done.6
  1.3 0.7 reduce.4
  2.0 0.7 reshape.40.count_ref
  2.7 2.0 %request.1 = (s32[128,128]{1,0:T(8,128)}, s32[16,128]{1,0:T(8,128)}) custom-call(s32[16,16]{1,0:T(8,128)} %bitcast.16, s32[16,16]{1,0:T(8,128)} %bitcast.17, s32[16,1]{1,0:T(8,128)} %reshape.40.count_ref), custom_call_target="tpu_custom_call" | custom-call | tf_op jit(solution)/shard_map/request/pallas_call | solution.py:270
  4.6 21.7 %all_to_all.21 = s32[128,1,128]{2,1,0:T(1,128)} all-to-all(s32[128,1,128]{2,1,0:T(1,128)} %bitcast.14), channel_id=1, replica_groups=mesh['gx'=8,'gy'=16] {'gx','gy'}, dimensions={0} | all-to-all | bytes 131072 | tf_op jit(solution)/shard_map/all_to_all | solution.py:255
  26.4 5.0 %gather.1 = (f32[512,4,128]{2,1,0:T(4,128)}, s32[8,128]{1,0:T(8,128)}) custom-call(s32[128,128]{1,0:T(8,128)} %bitcast.13, f32[3,65536]{1,0:T(4,128)} %position_ref.3, f32[512,128]{1,0:T(8,128)} %bitcast.12), custom_call_target="tpu_custom_call" | custom-call | tf_op jit(solution)/shard_map/gather/pallas_call | solution.py:282
  31.3 0.0 copy-start.3
  31.3 4.3 %all-to-all-start.1 = ((f32[512,4,128]{2,1,0:T(4,128)}), f32[512,4,128]{2,1,0:T(4,128)S(1)}, u32[]{:S(2)}, u32[]{:S(2)}) async-start(f32[512,4,128]{2,1,0:T(4,128)} %get-tuple-element.13), calls=%async_computation.1 | async-start | bytes 2097152 | tf_op jit(solution)/shard_map/all_to_all | solution.py:255
  35.6 1.2 %collective-permute-start.1 = (f32[16,128]{1,0:T(8,128)S(1)}, f32[16,128]{1,0:T(8,128)S(1)}, u32[]{:S(2)}, u32[]{:S(2)}) collective-permute-start(f32[16,128]{1,0:T(8,128)S(1)} %bitcast.19), channel_id=1, source_target_pairs={{16,0},{32,16},{48,32},{64,48},{80,64},{96,80},{112,96},{0,112},{1... | collective-permute-start | bytes 24584 | tf_op jit(solution)/shard_map/ppermute | solution.py:261
  36.8 0.6 collective-permute-start
  37.4 11.5 %collective-permute-done.1.right_ref = f32[16,128]{1,0:T(8,128)S(1)} collective-permute-done((f32[16,128]{1,0:T(8,128)S(1)}, f32[16,128]{1,0:T(8,128)S(1)}, u32[]{:S(2)}, u32[]{:S(2)}) %collective-permute-start.1) | collective-permute-done | bytes 8224 | tf_op jit(solution)/shard_map/ppermute | solution.py:261
  48.9 0.0 collective-permute-done.left_ref
  48.9 0.6 copy-done.4
  49.5 0.6 copy-done.5
  50.1 1.6 %filter.1.mid_ref = f32[16,128]{1,0:T(8,128)} custom-call(f32[16,128]{1,0:T(8,128)} %copy-done.5, f32[16,128]{1,0:T(8,128)} %bitcast.18, f32[16,128]{1,0:T(8,128)} %copy-done.4), custom_call_target="tpu_custom_call" | custom-call | tf_op jit(solution)/shard_map/filter/pallas_call | solution.py:291
  51.7 5.5 %collective-permute-start.3 = (f32[16,128]{1,0:T(8,128)}, f32[16,128]{1,0:T(8,128)S(1)}, u32[]{:S(2)}, u32[]{:S(2)}) collective-permute-start(f32[16,128]{1,0:T(8,128)} %filter.1.mid_ref), channel_id=1, source_target_pairs={{1,0},{2,1},{3,2},{4,3},{5,4},{6,5},{7,6},{8,7},{9,8},{10,9},{11,1... | collective-permute-start | bytes 24584 | tf_op jit(solution)/shard_map/ppermute | solution.py:261
  57.2 1.0 collective-permute-done.3.below_ref
  58.2 5.0 %collective-permute-done.2.above_ref = f32[16,128]{1,0:T(8,128)S(1)} collective-permute-done((f32[16,128]{1,0:T(8,128)}, f32[16,128]{1,0:T(8,128)S(1)}, u32[]{:S(2)}, u32[]{:S(2)}) %collective-permute-start.2) | collective-permute-done | bytes 8224 | tf_op jit(solution)/shard_map/ppermute | solution.py:260
  63.2 0.6 copy-done.2
  63.8 0.4 copy-done
  64.2 13.5 %transport.1 = (f32[16,128]{1,0:T(8,128)}, f32[512,4,128]{2,1,0:T(4,128)}) custom-call(s32[16,128]{1,0:T(8,128)} %get-tuple-element.11.target_ref, f32[512,4,128]{2,1,0:T(4,128)} %copy-done, f32[3,16,128]{2,1,0:T(8,128)} %bitcast.15, f32[16,128]{1,0:T(8,128)} %copy-done.2, f32[16,128]{1,0:T(8,128)} %filter.1.mid_ref, f32[16,128]{1,0:T(8,128)} %copy-done.1), custom_call_target="tpu_custom_call" | custom-call | tf_op jit(solution)/shard_map/transport/pallas_call | solution.py:299
  77.7 24.9 %all_to_all.22.back_ref = f32[512,4,128]{2,1,0:T(4,128)} all-to-all(f32[512,4,128]{2,1,0:T(4,128)} %get-tuple-element.16), channel_id=1, replica_groups=mesh['gx'=8,'gy'=16] {'gx','gy'}, dimensions={0} | all-to-all | bytes 2097152 | tf_op jit(solution)/shard_map/all_to_all | solution.py:255
  102.6 5.6 %reduce.5 = (f32[512,128]{1,0:T(8,128)}, f32[3,65536]{1,0:T(4,128)}) custom-call(s32[8,128]{1,0:T(8,128)} %get-tuple-element.15.ids_ref, f32[512,4,128]{2,1,0:T(4,128)} %all_to_all.22.back_ref, f32[3,65536]{1,0:T(4,128)} %position_ref.3), custom_call_target="tpu_custom_call" | custom-call | tf_op jit(solution)/shard_map/reduce/pallas_call | solution.py:314
  (10 shorter events, 0.0 us)
Async XLA Ops:
  0.6 0.7 copy-start.6
  31.3 4.3 %copy-start.3 = (f32[2,8,128]{2,1,0:T(8,128)S(1)}, f32[2,8,128]{2,1,0:T(8,128)}, u32[]{:S(2)}) copy-start(f32[2,8,128]{2,1,0:T(8,128)} %param.7) | copy-start | bytes 24580
  31.3 31.9 %all-to-all-start.1 = ((f32[512,4,128]{2,1,0:T(4,128)}), f32[512,4,128]{2,1,0:T(4,128)S(1)}, u32[]{:S(2)}, u32[]{:S(2)}) async-start(f32[512,4,128]{2,1,0:T(4,128)} %get-tuple-element.13), calls=%async_computation.1 | async-start | bytes 2097152 | tf_op jit(solution)/shard_map/all_to_all | solution.py:255
  35.6 13.2 %collective-permute-start.1 = (f32[16,128]{1,0:T(8,128)S(1)}, f32[16,128]{1,0:T(8,128)S(1)}, u32[]{:S(2)}, u32[]{:S(2)}) collective-permute-start(f32[16,128]{1,0:T(8,128)S(1)} %bitcast.19), channel_id=1, source_target_pairs={{16,0},{32,16},{48,32},{64,48},{80,64},{96,80},{112,96},{0,112},{1... | collective-permute-start | bytes 24584 | tf_op jit(solution)/shard_map/ppermute | solution.py:261
  36.8 12.1 %collective-permute-start = (f32[16,128]{1,0:T(8,128)S(1)}, f32[16,128]{1,0:T(8,128)S(1)}, u32[]{:S(2)}, u32[]{:S(2)}) collective-permute-start(f32[16,128]{1,0:T(8,128)S(1)} %bitcast.20), channel_id=1, source_target_pairs={{0,16},{16,32},{32,48},{48,64},{64,80},{80,96},{96,112},{112,0},{1... | collective-permute-start | bytes 24584 | tf_op jit(solution)/shard_map/ppermute | solution.py:260
  48.9 0.6 copy-start.4
  49.5 0.6 copy-start.5
  51.7 6.5 %collective-permute-start.3 = (f32[16,128]{1,0:T(8,128)}, f32[16,128]{1,0:T(8,128)S(1)}, u32[]{:S(2)}, u32[]{:S(2)}) collective-permute-start(f32[16,128]{1,0:T(8,128)} %filter.1.mid_ref), channel_id=1, source_target_pairs={{1,0},{2,1},{3,2},{4,3},{5,4},{6,5},{7,6},{8,7},{9,8},{10,9},{11,1... | collective-permute-start | bytes 24584 | tf_op jit(solution)/shard_map/ppermute | solution.py:261
  57.2 6.0 %collective-permute-start.2 = (f32[16,128]{1,0:T(8,128)}, f32[16,128]{1,0:T(8,128)S(1)}, u32[]{:S(2)}, u32[]{:S(2)}) collective-permute-start(f32[16,128]{1,0:T(8,128)} %filter.1.mid_ref), channel_id=1, source_target_pairs={{0,1},{1,2},{2,3},{3,4},{4,5},{5,6},{6,7},{7,8},{8,9},{9,10},{10,1... | collective-permute-start | bytes 24584 | tf_op jit(solution)/shard_map/ppermute | solution.py:260
  58.2 5.0 %copy-start.1 = (f32[16,128]{1,0:T(8,128)}, f32[16,128]{1,0:T(8,128)S(1)}, u32[]{:S(2)}) copy-start(f32[16,128]{1,0:T(8,128)S(1)} %collective-permute-done.3.below_ref) | copy-start | bytes 24580
  63.2 0.6 copy-start.2
  63.2 1.0 copy-start

commit v2 on v1

--- a/solution.py
+++ b/solution.py
@@ -32,6 +32,7 @@
 VMEM = pl.BlockSpec(memory_space=pltpu.VMEM)
 SMEM = pl.BlockSpec(memory_space=pltpu.SMEM)
 AXES = ("gx", "gy")
+LIMIT = pltpu.CompilerParams(vmem_limit_bytes=16 << 20)
 
 
 def gauss_values():
@@ -55,8 +56,15 @@
 def request_kernel(owner_ref, slot_ref, count_ref, request_ref, target_ref):
     owners = owner_ref[...]
     slots = slot_ref[...]
-    counts = count_ref[...]
     lane = iota((TILES, 128), 1)
+    corner = iota((CY, CY), 0) == iota((CY, CY), 1)
+    counts = jnp.concatenate(
+        [
+            jnp.sum(jnp.where(corner, count_ref[z], 0), axis=1, keepdims=True)
+            for z in range(PZ)
+        ],
+        axis=0,
+    )
     hots = []
     values = []
     for k in range(CAND):
@@ -85,10 +93,35 @@
     target_ref[...] = target
 
 
-def gather_kernel(asked_ref, position_ref, weight_ref, out_ref, ids_ref, ids_smem, sem):
+def filter_columns(left_ref, mid_ref, right_ref, out_ref):
+    shape = (3 * TILE, TILE)
+    shift = iota(shape, 0) - iota(shape, 1) - TILE
+    taps = jnp.zeros(shape, F32)
+    for offset in range(HALF + 1):
+        taps = jnp.where(jnp.abs(shift) == offset, GAUSS[HALF + offset], taps)
+    cells = jnp.concatenate([left_ref[...], mid_ref[...], right_ref[...]], axis=1)
+    out_ref[...] = jnp.dot(
+        cells, taps, preferred_element_type=F32, precision=lax.Precision.HIGHEST
+    )
+
+
+def gather_kernel(
+    asked_ref,
+    position_ref,
+    weight_ref,
+    left_ref,
+    mid_ref,
+    right_ref,
+    out_ref,
+    ids_ref,
+    first_ref,
+    ids_smem,
+    sem,
+):
     ids_ref[...] = jnp.transpose(asked_ref[...].astype(F32))[0:8].astype(I32)
     copy = pltpu.make_async_copy(ids_ref, ids_smem, sem)
     copy.start()
+    filter_columns(left_ref, mid_ref, right_ref, first_ref)
     copy.wait()
 
     def peer(step, carry):
@@ -102,18 +135,6 @@
         return carry
 
     lax.fori_loop(0, OWNERS, peer, 0, unroll=4)
-
-
-def filter_kernel(left_ref, mid_ref, right_ref, out_ref):
-    shape = (3 * TILE, TILE)
-    shift = iota(shape, 0) - iota(shape, 1) - TILE
-    taps = jnp.zeros(shape, F32)
-    for offset in range(HALF + 1):
-        taps = jnp.where(jnp.abs(shift) == offset, GAUSS[HALF + offset], taps)
-    cells = jnp.concatenate([left_ref[...], mid_ref[...], right_ref[...]], axis=1)
-    out_ref[...] = jnp.dot(
-        cells, taps, preferred_element_type=F32, precision=lax.Precision.HIGHEST
-    )
 
 
 def transport_kernel(
@@ -272,29 +293,28 @@
         out_shape=(shape_of(OWNERS, 128, dtype=I32), shape_of(TILES, 128, dtype=I32)),
         in_specs=[VMEM] * 3,
         out_specs=(VMEM, VMEM),
+        compiler_params=LIMIT,
         name="request",
     )(
         block_owner.reshape(TILES, CAND),
         block_slot.reshape(TILES, CAND),
-        block_count.reshape(TILES, 1),
+        jnp.transpose(block_count, (0, 2, 1)),
     )
     asked = exchange(request)
-    blocks, ids = pl.pallas_call(
+    blocks, ids, first_pass = pl.pallas_call(
         gather_kernel,
-        out_shape=(shape_of(SLOTS, 4, SITE_BLOCK), shape_of(8, 128, dtype=I32)),
-        in_specs=[VMEM] * 3,
-        out_specs=(VMEM, VMEM),
+        out_shape=(
+            shape_of(SLOTS, 4, SITE_BLOCK),
+            shape_of(8, 128, dtype=I32),
+            shape_of(TILES, TILE),
+        ),
+        in_specs=[VMEM] * 6,
+        out_specs=(VMEM, VMEM, VMEM),
+        compiler_params=LIMIT,
         scratch_shapes=[pltpu.SMEM((8, 128), I32), pltpu.SemaphoreType.DMA],
         name="gather",
-    )(asked, site_position, site_weight.reshape(SB_DEV, SITE_BLOCK))
+    )(asked, site_position, site_weight.reshape(SB_DEV, SITE_BLOCK), left, cells, right)
     arrived = exchange(blocks)
-    first_pass = pl.pallas_call(
-        filter_kernel,
-        out_shape=shape_of(TILES, TILE),
-        in_specs=[VMEM] * 3,
-        out_specs=VMEM,
-        name="filter",
-    )(left, cells, right)
     above, below = neighbours(first_pass, "gy")
     potential, moments = pl.pallas_call(
         transport_kernel,
@@ -308,6 +328,7 @@
             pltpu.VMEM((TILES, 128), F32),
             pltpu.VMEM((CAND // 2, 256, 256), BF16),
         ],
+        compiler_params=LIMIT,
         name="transport",
     )(target, arrived, point_position.reshape(3, TILES, TILE), above, first_pass, below)
     returned = exchange(moments)
@@ -320,6 +341,7 @@
             pltpu.VMEM((SB_DEV + CAP, 4, SITE_BLOCK), F32),
             pltpu.VMEM((SB_DEV, SITE_BLOCK), F32),
         ],
+        compiler_params=LIMIT,
         name="reduce",
     )(ids, returned, site_position)
     return (

time: 109 us -> 95.2 us (0.87)
  blocking collectives: 46.6 us -> 23.1 us
  starting transfers between devices: 11.5 us -> 23.2 us
  Pallas kernels: 27.6 us -> 22.2 us
  waiting for transfers between devices: 17.5 us -> 21.2 us
    all_to_all x2 -> x1, blocking collectives: 46.6 us -> 23.1 us  [exchange(): return lax.all_to_all(values, AXES, split_axis=0, concat_axis=0, tiled=True)]
    all_to_all x1 -> x2, waiting for transfers between devices: 0.01 us -> 12.8 us  [exchange(): return lax.all_to_all(values, AXES, split_axis=0, concat_axis=0, tiled=True)]
    all_to_all x1 -> x2, starting transfers between devices: 4.27 us -> 15.8 us  [exchange(): return lax.all_to_all(values, AXES, split_axis=0, concat_axis=0, tiled=True)]
    ppermute x2, waiting for transfers between devices: 12.5 us -> 2.41 us  [neighbours(): lax.ppermute(values, axis, [((i + 1) % count, i) for i in range(count)])]
    pallas_call x1 -> x0, Pallas kernels: 1.61 us -> none  [local(): pl.pallas_call(filter_kernel, out_shape=shape_of(TILES, TILE), in_specs=[...]
    unnamed x15 -> x16, local copies, waits for them, and re-layouts: 2.84 us -> 4.25 us
    pallas_call x1, Pallas kernels: 4.95 us -> 3.79 us  [local(): pl.pallas_call(gather_kernel, out_shape=(shape_of(SLOTS, 4, SITE_BLOCK),...]
  transfers between devices with their start and end apart: 5 -> 6, of which waited for: 3 -> 6; matrix products, arithmetic and copies ran while one was open for 0% -> 0% of each run, Pallas kernels for 1% -> 0%
where the time goes in v2:
time: 95.2 us; the launch traced here: 94.7 us
  starting transfers between devices  23.2 us (24%)
  blocking collectives  23.1 us (24%)
  Pallas kernels  22.2 us (23%)
  waiting for transfers between devices  21.2 us (22%)
  local copies, waits for them, and re-layouts  4.25 us (4%)
    all_to_all x1, blocking collectives, exchange(): return lax.all_to_all(values, AXES, split_axis=0, concat_axis=0, tiled=True)  23.1 us
    all_to_all x2, starting transfers between devices, exchange(): return lax.all_to_all(values, AXES, split_axis=0, concat_axis=0, tiled=True)  15.8 us
    all_to_all x2, waiting for transfers between devices, exchange(): return lax.all_to_all(values, AXES, split_axis=0, concat_axis=0, tiled=True)  12.8 us
    pallas_call x1, Pallas kernels, local(): pl.pallas_call(transport_kernel, out_shape=(shape_of(TILES, TILE), shape_...  12.5 us
    ppermute x2, starting transfers between devices, neighbours(): lax.ppermute(values, axis, [((i + 1) % count, i) for i in range(count)])  6.69 us
    ppermute x2, waiting for transfers between devices, neighbours(): lax.ppermute(values, axis, [(i, (i + 1) % count) for i in range(count)])  6.02 us
    pallas_call x1, Pallas kernels, local(): pl.pallas_call(reduce_kernel, out_shape=(shape_of(SB_DEV, SITE_BLOCK), sh...  4.63 us
    unnamed x16, local copies, waits for them, and re-layouts  4.25 us
  transfers between devices with their start and end apart: 6, of which 6 were waited for; matrix products, arithmetic and copies ran while one was open for 0% of the time, Pallas kernels for 0%

profile of v2, /device:TPU:1, one launch (start us, length us, event | category | flops | bytes accessed | tf_op | source)
XLA Modules:
  0.0 94.7 jit_solution(8220717851573916933)
XLA Ops:
  0.6 0.0 copy-start.7
  0.6 0.7 copy-done.7
  1.3 0.7 copy-done.5
  2.0 0.7 copy-done.6
  2.7 1.3 %request.1 = (s32[128,128]{1,0:T(8,128)}, s32[16,128]{1,0:T(8,128)S(1)}) custom-call(s32[16,16]{1,0:T(8,128)S(1)} %bitcast.20, s32[16,16]{1,0:T(8,128)S(1)} %bitcast.21, s32[2,1,8]{2,1,0:T(1,128)S(1)} %bitcast.22), custom_call_target="tpu_custom_call" | custom-call | tf_op jit(solution)/shard_map/request/pallas_call | solution.py:291
  4.0 11.5 %all-to-all-start = ((s32[128,1,128]{2,1,0:T(1,128)}), s32[128,1,128]{2,1,0:T(1,128)S(1)}, u32[]{:S(2)}, u32[]{:S(2)}) async-start(s32[128,1,128]{2,1,0:T(1,128)} %bitcast.5), calls=%async_computation | async-start | bytes 131072 | tf_op jit(solution)/shard_map/all_to_all | solution.py:276
  15.5 1.1 %collective-permute-start.1 = (f32[16,128]{1,0:T(8,128)S(1)}, f32[16,128]{1,0:T(8,128)S(1)}, u32[]{:S(2)}, u32[]{:S(2)}) collective-permute-start(f32[16,128]{1,0:T(8,128)S(1)} %bitcast.17), channel_id=1, source_target_pairs={{16,0},{32,16},{48,32},{64,48},{80,64},{96,80},{112,96},{0,112},{1... | collective-permute-start | bytes 24584 | tf_op jit(solution)/shard_map/ppermute | solution.py:282
  16.6 0.7 collective-permute-start
  17.3 1.6 %collective-permute-done.1.right_ref = f32[16,128]{1,0:T(8,128)S(1)} collective-permute-done((f32[16,128]{1,0:T(8,128)S(1)}, f32[16,128]{1,0:T(8,128)S(1)}, u32[]{:S(2)}, u32[]{:S(2)}) %collective-permute-start.1) | collective-permute-done | bytes 8224 | tf_op jit(solution)/shard_map/ppermute | solution.py:282
  18.9 0.3 collective-permute-done.left_ref
  19.1 6.1 %all-to-all-done = s32[128,1,128]{2,1,0:T(1,128)S(1)} async-done(((s32[128,1,128]{2,1,0:T(1,128)}), s32[128,1,128]{2,1,0:T(1,128)S(1)}, u32[]{:S(2)}, u32[]{:S(2)}) %all-to-all-start) | async-done | bytes 65568 | tf_op jit(solution)/shard_map/all_to_all | solution.py:276
  25.2 1.2 %copy-done = f32[3,65536]{1,0:T(4,128)S(1)} copy-done((f32[3,65536]{1,0:T(4,128)S(1)}, f32[3,65536]{1,0:T(4,128)}, u32[]{:S(2)}) %copy-start) | copy-done | bytes 786456
  26.5 0.9 %copy-done.2 = f32[65536]{0:T(1024)S(1)} copy-done((f32[65536]{0:T(1024)S(1)}, f32[65536]{0:T(1024)}, u32[]{:S(2)}) %copy-start.2) | copy-done | bytes 262168
  27.4 3.8 %gather.1 = (f32[512,4,128]{2,1,0:T(4,128)}, s32[8,128]{1,0:T(8,128)S(1)}, f32[16,128]{1,0:T(8,128)S(1)}) custom-call(s32[128,128]{1,0:T(8,128)S(1)} %bitcast.14, f32[3,65536]{1,0:T(4,128)S(1)} %copy-done, f32[512,128]{1,0:T(8,128)S(1)} %bitcast.15, f32[16,128]{1,0:T(8,128)S(1)} %collective-permute-done.left_ref, f32[16,128]{1,0:T(8,128)S(1)} %bitcast.19, ...), custom_call_target="tpu_custom_call" | custom-call | tf_op jit(solution)/shard_map/gather/pallas_call | solution.py:304
  31.2 0.0 copy-start.3
  31.2 4.4 %all-to-all-start.1 = ((f32[512,4,128]{2,1,0:T(4,128)}), f32[512,4,128]{2,1,0:T(4,128)S(1)}, u32[]{:S(2)}, u32[]{:S(2)}) async-start(f32[512,4,128]{2,1,0:T(4,128)} %get-tuple-element.14), calls=%async_computation.1 | async-start | bytes 2097152 | tf_op jit(solution)/shard_map/all_to_all | solution.py:276
  35.6 5.6 %collective-permute-start.3 = (f32[16,128]{1,0:T(8,128)S(1)}, f32[16,128]{1,0:T(8,128)S(1)}, u32[]{:S(2)}, u32[]{:S(2)}) collective-permute-start(f32[16,128]{1,0:T(8,128)S(1)} %get-tuple-element.15.mid_ref), channel_id=1, source_target_pairs={{1,0},{2,1},{3,2},{4,3},{5,4},{6,5},{7,6},{8,7},{9,8},{10,9},{11,1... | collective-permute-start | bytes 24584 | tf_op jit(solution)/shard_map/ppermute | solution.py:282
  41.2 0.0 collective-permute-start.2
  41.2 0.8 collective-permute-done.3.below_ref
  42.0 5.8 %collective-permute-done.2.above_ref = f32[16,128]{1,0:T(8,128)S(1)} collective-permute-done((f32[16,128]{1,0:T(8,128)S(1)}, f32[16,128]{1,0:T(8,128)S(1)}, u32[]{:S(2)}, u32[]{:S(2)}) %collective-permute-start.2) | collective-permute-done | bytes 8224 | tf_op jit(solution)/shard_map/ppermute | solution.py:281
  47.8 6.7 %all-to-all-done.1.arrived_ref = f32[512,4,128]{2,1,0:T(4,128)S(1)} async-done(((f32[512,4,128]{2,1,0:T(4,128)}), f32[512,4,128]{2,1,0:T(4,128)S(1)}, u32[]{:S(2)}, u32[]{:S(2)}) %all-to-all-start.1) | async-done | bytes 1048608 | tf_op jit(solution)/shard_map/all_to_all | solution.py:276
  54.5 12.5 %transport.1 = (f32[16,128]{1,0:T(8,128)}, f32[512,4,128]{2,1,0:T(4,128)S(1)}) custom-call(s32[16,128]{1,0:T(8,128)S(1)} %get-tuple-element.12.target_ref, f32[512,4,128]{2,1,0:T(4,128)S(1)} %all-to-all-done.1.arrived_ref, f32[3,16,128]{2,1,0:T(8,128)S(1)} %bitcast.16, f32[16,128]{1,0:T(8,128)S(1)} %collective-permute-done.2.above_ref, ...), custom_call_target="tpu_custom_call" | custom-call | tf_op jit(solution)/shard_map/transport/pallas_call | solution.py:319
  67.0 23.1 %all_to_all.21.back_ref = f32[512,4,128]{2,1,0:T(4,128)S(1)} all-to-all(f32[512,4,128]{2,1,0:T(4,128)S(1)} %get-tuple-element.18), channel_id=1, replica_groups=mesh['gx'=8,'gy'=16] {'gx','gy'}, dimensions={0} | all-to-all | bytes 2097152 | tf_op jit(solution)/shard_map/all_to_all | solution.py:276
  90.1 4.6 %reduce.1 = (f32[512,128]{1,0:T(8,128)}, f32[3,65536]{1,0:T(4,128)}) custom-call(s32[8,128]{1,0:T(8,128)S(1)} %get-tuple-element.17.ids_ref, f32[512,4,128]{2,1,0:T(4,128)S(1)} %all_to_all.21.back_ref, f32[3,65536]{1,0:T(4,128)S(1)} %copy-done.1), custom_call_target="tpu_custom_call" | custom-call | tf_op jit(solution)/shard_map/reduce/pallas_call | solution.py:335
  (9 shorter events, 0.0 us)
Async XLA Ops:
  0.6 0.7 copy-start.7
  1.3 0.7 copy-start.5
  2.0 0.7 copy-start.6
  4.0 11.5 %copy-start.4 = (f32[2,8,128]{2,1,0:T(8,128)S(1)}, f32[2,8,128]{2,1,0:T(8,128)}, u32[]{:S(2)}) copy-start(f32[2,8,128]{2,1,0:T(8,128)} %param.7) | copy-start | bytes 24580
  4.0 21.2 %all-to-all-start = ((s32[128,1,128]{2,1,0:T(1,128)}), s32[128,1,128]{2,1,0:T(1,128)S(1)}, u32[]{:S(2)}, u32[]{:S(2)}) async-start(s32[128,1,128]{2,1,0:T(1,128)} %bitcast.5), calls=%async_computation | async-start | bytes 131072 | tf_op jit(solution)/shard_map/all_to_all | solution.py:276
  15.5 3.4 %collective-permute-start.1 = (f32[16,128]{1,0:T(8,128)S(1)}, f32[16,128]{1,0:T(8,128)S(1)}, u32[]{:S(2)}, u32[]{:S(2)}) collective-permute-start(f32[16,128]{1,0:T(8,128)S(1)} %bitcast.17), channel_id=1, source_target_pairs={{16,0},{32,16},{48,32},{64,48},{80,64},{96,80},{112,96},{0,112},{1... | collective-permute-start | bytes 24584 | tf_op jit(solution)/shard_map/ppermute | solution.py:282
  16.6 2.6 %collective-permute-start = (f32[16,128]{1,0:T(8,128)S(1)}, f32[16,128]{1,0:T(8,128)S(1)}, u32[]{:S(2)}, u32[]{:S(2)}) collective-permute-start(f32[16,128]{1,0:T(8,128)S(1)} %bitcast.18), channel_id=1, source_target_pairs={{0,16},{16,32},{32,48},{48,64},{64,80},{80,96},{96,112},{112,0},{1... | collective-permute-start | bytes 24584 | tf_op jit(solution)/shard_map/ppermute | solution.py:281
  25.2 1.2 %copy-start = (f32[3,65536]{1,0:T(4,128)S(1)}, f32[3,65536]{1,0:T(4,128)}, u32[]{:S(2)}) copy-start(f32[3,65536]{1,0:T(4,128)} %position_ref.3) | copy-start | bytes 2359300
  26.4 0.9 %copy-start.2 = (f32[65536]{0:T(1024)S(1)}, f32[65536]{0:T(1024)}, u32[]{:S(2)}) copy-start(f32[65536]{0:T(1024)} %param.13) | copy-start | bytes 786436
  31.2 23.3 %copy-start.3 = (f32[3,2,8,128]{3,2,1,0:T(8,128)S(1)}, f32[3,2,8,128]{3,2,1,0:T(8,128)}, u32[]{:S(2)}) copy-start(f32[3,2,8,128]{3,2,1,0:T(8,128)} %param.8) | copy-start | bytes 73732
  31.2 23.3 %all-to-all-start.1 = ((f32[512,4,128]{2,1,0:T(4,128)}), f32[512,4,128]{2,1,0:T(4,128)S(1)}, u32[]{:S(2)}, u32[]{:S(2)}) async-start(f32[512,4,128]{2,1,0:T(4,128)} %get-tuple-element.14), calls=%async_computation.1 | async-start | bytes 2097152 | tf_op jit(solution)/shard_map/all_to_all | solution.py:276
  35.6 6.4 %collective-permute-start.3 = (f32[16,128]{1,0:T(8,128)S(1)}, f32[16,128]{1,0:T(8,128)S(1)}, u32[]{:S(2)}, u32[]{:S(2)}) collective-permute-start(f32[16,128]{1,0:T(8,128)S(1)} %get-tuple-element.15.mid_ref), channel_id=1, source_target_pairs={{1,0},{2,1},{3,2},{4,3},{5,4},{6,5},{7,6},{8,7},{9,8},{10,9},{11,1... | collective-permute-start | bytes 24584 | tf_op jit(solution)/shard_map/ppermute | solution.py:282
  41.2 6.6 %collective-permute-start.2 = (f32[16,128]{1,0:T(8,128)S(1)}, f32[16,128]{1,0:T(8,128)S(1)}, u32[]{:S(2)}, u32[]{:S(2)}) collective-permute-start(f32[16,128]{1,0:T(8,128)S(1)} %get-tuple-element.15.mid_ref), channel_id=1, source_target_pairs={{0,1},{1,2},{2,3},{3,4},{4,5},{5,6},{6,7},{7,8},{8,9},{9,10},{10,1... | collective-permute-start | bytes 24584 | tf_op jit(solution)/shard_map/ppermute | solution.py:281
  67.0 23.1 %copy-start.1 = (f32[3,65536]{1,0:T(4,128)S(1)}, f32[3,65536]{1,0:T(4,128)}, u32[]{:S(2)}) copy-start(f32[3,65536]{1,0:T(4,128)} %position_ref.3) | copy-start | bytes 2359300

commit v3 on v2

v3 whole, which is shorter than its diff:
```python
import math

import jax
import jax.numpy as jnp
import numpy as np
from jax import lax
from jax.experimental import pallas as pl
from jax.experimental.pallas import tpu as pltpu
from jax.sharding import PartitionSpec as P

PZ = 2
CY = 8
TILE = 128
CAND = 16
SITE_BLOCK = 128
SB_DEV = 512
HALF = 8
CAP = 4
OWNERS = 128
TILES = PZ * CY
SLOTS = OWNERS * CAP
ENTRIES = TILES * CAND

EPSILON = 0.05
PRIOR_MASS = 0.5
SIGMA_CELLS = 4.0
KAPPA = math.log2(math.e) / EPSILON
ROOT = math.sqrt(KAPPA)
DEAD = -1e30
F32 = jnp.float32
BF16 = jnp.bfloat16
I32 = jnp.int32
VMEM = pl.BlockSpec(memory_space=pltpu.VMEM)
HBM = pl.BlockSpec(memory_space=pltpu.HBM)
SMEM = pl.BlockSpec(memory_space=pltpu.SMEM)
AXES = ("gx", "gy")
LIMIT = pltpu.CompilerParams(vmem_limit_bytes=16 << 20)
WIDE = pltpu.CompilerParams(vmem_limit_bytes=60 * 1024 * 1024)


def gauss_values():
    offsets = np.arange(-HALF, HALF + 1, dtype=np.float64)
    values = np.exp(-offsets * offsets / (2.0 * SIGMA_CELLS * SIGMA_CELLS))
    return values / values.sum()


GAUSS = [float(v) for v in gauss_values()]
GAUSS_PEAK = GAUSS[HALF]


def iota(shape, dim):
    return lax.broadcasted_iota(I32, shape, dim)


def rounded(values):
    return values.astype(BF16).astype(F32)


def request_kernel(
    owner_hbm, slot_hbm, count_hbm, request_ref, target_ref, owner_ref, slot_ref, count_ref, sems
):
    copies = [
        pltpu.make_async_copy(owner_hbm, owner_ref, sems.at[0]),
        pltpu.make_async_copy(slot_hbm, slot_ref, sems.at[1]),
        pltpu.make_async_copy(count_hbm, count_ref, sems.at[2]),
    ]
    for copy in copies:
        copy.start()
    lane = iota((TILES, 128), 1)
    corner = iota((CY, CY), 0) == iota((CY, CY), 1)
    square = (ENTRIES, ENTRIES)
    lower = (iota(square, 1) < iota(square, 0)).astype(F32).astype(BF16)
    for copy in copies:
        copy.wait()
    owners = owner_ref[...]
    slots = slot_ref[...]
    counts = jnp.concatenate(
        [
            jnp.sum(jnp.where(corner, count_ref[z], 0), axis=1, keepdims=True)
            for z in range(PZ)
        ],
        axis=0,
    )
    hots = []
    values = []
    for k in range(CAND):
        hots.append((owners[:, k : k + 1] == lane).astype(F32))
        values.append(jnp.where(k < counts, slots[:, k : k + 1] + 1, 0))
    hot = jnp.concatenate(hots, axis=0)
    value = jnp.concatenate(values, axis=0)
    hot_low = hot.astype(BF16)
    before = jnp.dot(lower, hot_low, preferred_element_type=F32)
    rank = jnp.sum(before * hot, axis=1, keepdims=True).astype(I32)
    wide = iota((ENTRIES, 128), 1)
    high_part = (value & -32).astype(F32)
    low_part = (value & 31).astype(F32)
    spread = jnp.where(wide == rank, high_part, 0.0) + jnp.where(wide == rank + CAP, low_part, 0.0)
    request = lax.dot_general(
        hot_low, spread.astype(BF16), (((0,), (0,)), ((), ())), preferred_element_type=F32
    )
    request = request + pltpu.roll(request, 128 - CAP, 1)
    request_ref[...] = request.astype(I32) - 1
    target = jnp.where(lane == CAND, counts, 0)
    for k in range(CAND):
        place = owners[:, k : k + 1] * CAP + rank[k * TILES : (k + 1) * TILES]
        target = jnp.where(lane == k, place, target)
    target_ref[...] = target


def table_kernel(position_hbm, weight_hbm, table_ref, start_ref, position_ref, weight_ref, sems):
    first = pltpu.make_async_copy(position_hbm, position_ref, sems.at[0])
    second = pltpu.make_async_copy(weight_hbm, weight_ref, sems.at[1])
    first.start()
    second.start()
    row = iota((4, 128), 0)
    dead = jnp.where(row == 3, DEAD, 0.0)
    for r in range(CAP):
        table_ref[SB_DEV + r] = dead
        start_ref[(SB_DEV + r) * 4 : (SB_DEV + r + 1) * 4, :] = jnp.zeros((4, 128), F32)
    first.wait()
    second.wait()

    def block(b, carry):
        start = pl.multiple_of(b * SITE_BLOCK, SITE_BLOCK)
        place = position_ref[:, pl.ds(start, SITE_BLOCK)]
        table_ref[b, 0:3, :] = (place - 0.5) * ROOT
        table_ref[b, 3:4, :] = weight_ref[pl.ds(b, 1), :]
        line = pl.multiple_of(b * 4, 4)
        start_ref[pl.ds(line, 3), :] = PRIOR_MASS * place
        start_ref[pl.ds(line + 3, 1), :] = jnp.zeros((1, 128), F32)
        return carry

    lax.fori_loop(0, SB_DEV, block, 0, unroll=8)


def filter_columns(left_ref, mid_ref, right_ref, out_ref):
    shape = (3 * TILE, TILE)
    shift = iota(shape, 0) - iota(shape, 1) - TILE
    taps = jnp.zeros(shape, F32)
    for offset in range(HALF + 1):
        taps = jnp.where(jnp.abs(shift) == offset, GAUSS[HALF + offset], taps)
    cells = jnp.concatenate([left_ref[...], mid_ref[...], right_ref[...]], axis=1)
    out_ref[...] = jnp.dot(
        cells, taps, preferred_element_type=F32, precision=lax.Precision.HIGHEST
    )


def gather_kernel(
    asked_ref,
    table_ref,
    left_ref,
    mid_ref,
    right_ref,
    out_ref,
    ids_ref,
    first_ref,
    ids_smem,
    sem,
):
    asked = jnp.transpose(asked_ref[...].astype(F32))[0:8].astype(I32)
    ids_ref[...] = jnp.where(asked < 0, SB_DEV + iota((8, 128), 0) % CAP, asked)
    copy = pltpu.make_async_copy(ids_ref, ids_smem, sem)
    copy.start()
    filter_columns(left_ref, mid_ref, right_ref, first_ref)
    copy.wait()

    def peer(step, carry):
        for r in range(CAP):
            out_ref[step * CAP + r] = table_ref[ids_smem[r, step]]
        return carry

    lax.fori_loop(0, OWNERS, peer, 0, unroll=8)


def prepare_kernel(point_ref, lhs_ref):
    row = iota((8, 128), 0)

    def tile(t, carry):
        coords = [point_ref[c, pl.ds(t, 1), :] for c in range(3)]
        point = jnp.where(row == 0, coords[0], jnp.where(row == 1, coords[1], coords[2]))
        scaled = jnp.where(row < 3, (2.0 * ROOT) * (point - 0.5), 0.0)
        a1 = rounded(scaled)
        rest = scaled - a1
        a2 = rounded(rest)
        a3 = rest - a2
        lead = jnp.where(row == 7, 1.0, jnp.where(row >= 4, -1.0, a1))
        lhs = jnp.concatenate([lead, lead, lead, a2, a2, a3], axis=0)
        lhs_ref[t] = jnp.transpose(lhs).astype(BF16)
        return carry

    lax.fori_loop(0, TILES, tile, 0, unroll=4)


def transport_kernel(
    target_ref,
    arrived_ref,
    lhs_ref,
    point_ref,
    above_ref,
    mid_ref,
    below_ref,
    potential_ref,
    out_ref,
    rows_ref,
    load_ref,
    top_ref,
    sum_ref,
    even_ref,
    odd_ref,
    even_load_ref,
    odd_load_ref,
):
    planes = []
    for z in range(PZ):
        rows_ref[z, 0:CY, :] = above_ref[z * CY : (z + 1) * CY, :]
        rows_ref[z, CY : 2 * CY, :] = mid_ref[z * CY : (z + 1) * CY, :]
        rows_ref[z, 2 * CY : 3 * CY, :] = below_ref[z * CY : (z + 1) * CY, :]
        total = GAUSS[0] * rows_ref[z, 0:CY, :]
        for j in range(1, 2 * HALF + 1):
            total = total + GAUSS[j] * rows_ref[z, j : j + CY, :]
        planes.append(total)
    load_ref[0:CY, :] = GAUSS[HALF] * planes[0] + GAUSS[HALF + 1] * planes[1]
    load_ref[CY : 2 * CY, :] = GAUSS[HALF - 1] * planes[0] + GAUSS[HALF] * planes[1]

    row = iota((8, 128), 0)
    fixed = (row < 4) | (row == 7)
    factor = jnp.where(row == 7, KAPPA, 1.0)

    def find_top(t):
        tops = [arrived_ref[target_ref[t, k], 3:4, :] for k in range(CAND)]
        while len(tops) > 1:
            tops = [jnp.maximum(a, b) for a, b in zip(tops[::2], tops[1::2])]
        top = jnp.max(tops[0], axis=1, keepdims=True)
        top_ref[pl.ds(t, 1), :] = jnp.broadcast_to(top, (1, 128))

    def scores(t, e_ref, unit_ref):
        lhs = lhs_ref[t]
        centre = jnp.where(row % 4 == 3, top_ref[pl.ds(t, 1), :], 0.0)

        def spread(k):
            block = arrived_ref[target_ref[t, k]]
            both = jnp.concatenate([block, block], axis=0) - centre
            terms = both * jnp.where(fixed, factor, both)
            t1 = rounded(terms)
            rest = terms - t1
            t2 = rounded(rest)
            t3 = rest - t2
            return jnp.concatenate([t1, t2, t3, t1, t2, t1], axis=0).astype(BF16)

        total = None
        for q in range(CAND // 2):
            rhs = jnp.concatenate([spread(2 * q), spread(2 * q + 1)], axis=1)
            e = jnp.exp2(jnp.dot(lhs, rhs, preferred_element_type=F32))
            part = e[:, :128] + e[:, 128:]
            total = part if total is None else total + part
            high = e.astype(BF16)
            e_ref[q, 0:128, :] = high
            e_ref[q, 128:256, :] = (e - high.astype(F32)).astype(BF16)
        sums = jnp.sum(jnp.transpose(total), axis=0, keepdims=True)
        sum_ref[pl.ds(t, 1), :] = sums
        coords = [point_ref[c, pl.ds(t, 1), :] for c in range(3)]
        point = jnp.where(
            row % 4 == 0,
            coords[0],
            jnp.where(row % 4 == 1, coords[1], jnp.where(row % 4 == 2, coords[2], 1.0)),
        )
        loads = (load_ref[pl.ds(t, 1), :] / sums) * point
        high = rounded(loads)
        unit_ref[...] = jnp.where(row < 4, high, loads - high)

    def moments(t, e_ref, unit_ref):
        half = unit_ref[...].astype(BF16)
        lhs = jnp.concatenate([half, half], axis=1)
        for q in range(CAND // 2):
            found = jnp.dot(lhs, e_ref[q], preferred_element_type=F32)
            found = found[0:4] + found[4:8]
            out_ref[target_ref[t, 2 * q]] = found[:, :128]
            out_ref[target_ref[t, 2 * q + 1]] = found[:, 128:]

    find_top(0)

    def two_tiles(i, carry):
        t = 2 * i
        find_top(t + 1)
        scores(t, even_ref, even_load_ref)
        moments(jnp.maximum(t - 1, 0), odd_ref, odd_load_ref)
        find_top(jnp.minimum(t + 2, TILES - 1))
        scores(t + 1, odd_ref, odd_load_ref)
        moments(t, even_ref, even_load_ref)
        return carry

    lax.fori_loop(0, TILES // 2, two_tiles, 0)
    moments(TILES - 1, odd_ref, odd_load_ref)
    square = (
        (point_ref[0] - 0.5) ** 2 + (point_ref[1] - 0.5) ** 2 + (point_ref[2] - 0.5) ** 2
    )
    potential_ref[...] = jnp.log(sum_ref[...]) + (top_ref[...] - square) / EPSILON


def reduce_kernel(ids_ref, back_ref, start_ref, mass_ref, centre_ref, acc_ref, scale_ref):
    def peer(step, carry):
        places = []
        sums = []
        for r in range(CAP):
            place = pl.ds(pl.multiple_of(ids_ref[r, step] * 4, 4), 4)
            places.append(place)
            sums.append(acc_ref[place, :] + back_ref[step * CAP + r])
        for place, total in zip(places, sums):
            acc_ref[place, :] = total
        return carry

    lax.fori_loop(0, OWNERS, peer, 0, unroll=4)
    mass = acc_ref[pl.ds(3, SB_DEV, stride=4), :]
    mass_ref[...] = mass
    scale_ref[...] = 1.0 / (mass + PRIOR_MASS)

    def finish(b, carry):
        start = pl.multiple_of(b * SITE_BLOCK, SITE_BLOCK)
        line = pl.multiple_of(b * 4, 4)
        centre_ref[:, pl.ds(start, SITE_BLOCK)] = (
            acc_ref[pl.ds(line, 3), :] * scale_ref[pl.ds(b, 1), :]
        )
        return carry

    lax.fori_loop(0, SB_DEV, finish, 0, unroll=16)


def shape_of(*dims, dtype=F32):
    return jax.ShapeDtypeStruct(dims, dtype)


def exchange(values):
    return lax.all_to_all(values, AXES, split_axis=0, concat_axis=0, tiled=True)


def neighbours(values, axis):
    count = lax.axis_size(axis)
    before = lax.ppermute(values, axis, [(i, (i + 1) % count) for i in range(count)])
    after = lax.ppermute(values, axis, [((i + 1) % count, i) for i in range(count)])
    return before, after


def local(
    density, point_position, block_owner, block_slot, block_count, site_position, site_weight
):
    cells = density.reshape(TILES, TILE)
    left, right = neighbours(cells, "gx")
    request, target = pl.pallas_call(
        request_kernel,
        out_shape=(shape_of(OWNERS, 128, dtype=I32), shape_of(TILES, 128, dtype=I32)),
        in_specs=[HBM] * 3,
        out_specs=(VMEM, VMEM),
        scratch_shapes=[
            pltpu.VMEM((TILES, CAND), I32),
            pltpu.VMEM((TILES, CAND), I32),
            pltpu.VMEM((PZ, 1, CY), I32),
            pltpu.SemaphoreType.DMA((3,)),
        ],
        compiler_params=WIDE,
        name="request",
    )(
        block_owner.reshape(TILES, CAND),
        block_slot.reshape(TILES, CAND),
        jnp.transpose(block_count, (0, 2, 1)),
    )
    asked = exchange(request)
    table, start = pl.pallas_call(
        table_kernel,
        out_shape=(shape_of(SB_DEV + CAP, 4, SITE_BLOCK), shape_of((SB_DEV + CAP) * 4, SITE_BLOCK)),
        in_specs=[HBM] * 2,
        out_specs=(VMEM, VMEM),
        scratch_shapes=[
            pltpu.VMEM((3, SB_DEV * SITE_BLOCK), F32),
            pltpu.VMEM((SB_DEV, SITE_BLOCK), F32),
            pltpu.SemaphoreType.DMA((2,)),
        ],
        compiler_params=LIMIT,
        name="table",
    )(site_position, site_weight.reshape(SB_DEV, SITE_BLOCK))
    blocks, ids, first_pass = pl.pallas_call(
        gather_kernel,
        out_shape=(
            shape_of(SLOTS, 4, SITE_BLOCK),
            shape_of(8, 128, dtype=I32),
            shape_of(TILES, TILE),
        ),
        in_specs=[VMEM] * 5,
        out_specs=(VMEM, VMEM, VMEM),
        compiler_params=LIMIT,
        scratch_shapes=[pltpu.SMEM((8, 128), I32), pltpu.SemaphoreType.DMA],
        name="gather",
    )(asked, table, left, cells, right)
    arrived = exchange(blocks)
    points = point_position.reshape(3, TILES, TILE)
    lhs = pl.pallas_call(
        prepare_kernel,
        out_shape=shape_of(TILES, TILE, 48, dtype=BF16),
        in_specs=[VMEM],
        out_specs=VMEM,
        compiler_params=LIMIT,
        name="prepare",
    )(points)
    above, below = neighbours(first_pass, "gy")
    potential, moments = pl.pallas_call(
        transport_kernel,
        out_shape=(shape_of(TILES, TILE), shape_of(SLOTS, 4, SITE_BLOCK)),
        in_specs=[SMEM] + [VMEM] * 6,
        out_specs=(VMEM, VMEM),
        scratch_shapes=[
            pltpu.VMEM((PZ, 3 * CY, 128), F32),
            pltpu.VMEM((TILES, 128), F32),
            pltpu.VMEM((TILES, 128), F32),
            pltpu.VMEM((TILES, 128), F32),
            pltpu.VMEM((CAND // 2, 256, 256), BF16),
            pltpu.VMEM((CAND // 2, 256, 256), BF16),
            pltpu.VMEM((8, 128), F32),
            pltpu.VMEM((8, 128), F32),
        ],
        compiler_params=LIMIT,
        name="transport",
    )(target, arrived, lhs, points, above, first_pass, below)
    returned = exchange(moments)
    site_mass, barycentre, _ = pl.pallas_call(
        reduce_kernel,
        out_shape=(
            shape_of(SB_DEV, SITE_BLOCK),
            shape_of(3, SB_DEV * SITE_BLOCK),
            shape_of((SB_DEV + CAP) * 4, SITE_BLOCK),
        ),
        in_specs=[SMEM] + [VMEM] * 2,
        out_specs=(VMEM, VMEM, VMEM),
        scratch_shapes=[pltpu.VMEM((SB_DEV, SITE_BLOCK), F32)],
        input_output_aliases={2: 2},
        compiler_params=LIMIT,
        name="reduce",
    )(ids, returned, start)
    return (
        potential.reshape(PZ, CY, TILE),
        site_mass.reshape(SB_DEV * SITE_BLOCK),
        barycentre,
    )


def solution(mesh):
    in_specs = (
        P(None, "gy", "gx"),
        P(None, None, "gy", "gx"),
        P(None, "gy", "gx"),
        P(None, "gy", "gx"),
        P(None, "gy", "gx"),
        P(None, ("gx", "gy")),
        P(("gx", "gy")),
    )
    out_specs = (P(None, "gy", "gx"), P(("gx", "gy")), P(None, ("gx", "gy")))
    return jax.shard_map(local, mesh=mesh, in_specs=in_specs, out_specs=out_specs, check_vma=False)
```

time: 95.2 us -> 85.6 us (0.90)
  Pallas kernels: 22.2 us -> 17.2 us
  waiting for transfers between devices: 21.2 us -> 17.3 us
  local copies, waits for them, and re-layouts: 4.25 us -> 2.19 us
  starting transfers between devices: 23.2 us -> 24.8 us
    pallas_call x1, Pallas kernels: 12.5 us -> 7.41 us  [local(): pl.pallas_call(transport_kernel, out_shape=(shape_of(TILES, TILE), shape_...]
    ppermute x2, waiting for transfers between devices: 2.41 us -> 0.33 us  [neighbours(): lax.ppermute(values, axis, [((i + 1) % count, i) for i in range(count)])]
    unnamed x16 -> x10, local copies, waits for them, and re-layouts: 4.25 us -> 2.19 us
    pallas_call x0 -> x2, Pallas kernels: none -> 1.7 us  [the longest x1 1.25 us: local(): pl.pallas_call(table_kernel, out_shape=(shape_of(SB_DEV + CAP, 4, SITE_BL...]
    all_to_all x2, starting transfers between devices: 15.8 us -> 17.4 us  [exchange(): return lax.all_to_all(values, AXES, split_axis=0, concat_axis=0, tiled=True)]
    all_to_all x2, waiting for transfers between devices: 12.8 us -> 11.2 us  [exchange(): return lax.all_to_all(values, AXES, split_axis=0, concat_axis=0, tiled=True)]
    pallas_call x1, Pallas kernels: 4.63 us -> 3.43 us  [local(): pl.pallas_call(reduce_kernel, out_shape=(shape_of(SB_DEV, SITE_BLOCK), sh...]
    pallas_call x1, Pallas kernels: 3.79 us -> 2.6 us  [local(): pl.pallas_call(gather_kernel, out_shape=(shape_of(SLOTS, 4, SITE_BLOCK),...]
  transfers between devices with their start and end apart: 6 -> 6, of which waited for: 6 -> 4; matrix products, arithmetic and copies ran while one was open for 0% -> 0% of each run, Pallas kernels for 0% -> 2%
where the time goes in v3:
time: 85.6 us; the launch traced here: 85.2 us
  starting transfers between devices  24.8 us (29%)
  blocking collectives  23 us (27%)
  waiting for transfers between devices  17.3 us (20%)
  Pallas kernels  17.2 us (20%)
  local copies, waits for them, and re-layouts  2.19 us (3%)
    all_to_all x1, blocking collectives, exchange(): return lax.all_to_all(values, AXES, split_axis=0, concat_axis=0, tiled=True)  23 us
    all_to_all x2, starting transfers between devices, exchange(): return lax.all_to_all(values, AXES, split_axis=0, concat_axis=0, tiled=True)  17.4 us
    all_to_all x2, waiting for transfers between devices, exchange(): return lax.all_to_all(values, AXES, split_axis=0, concat_axis=0, tiled=True)  11.2 us
    pallas_call x1, Pallas kernels, local(): pl.pallas_call(transport_kernel, out_shape=(shape_of(TILES, TILE), shape_...  7.41 us
    ppermute x2, starting transfers between devices, neighbours(): lax.ppermute(values, axis, [((i + 1) % count, i) for i in range(count)])  6.69 us
    ppermute x2, waiting for transfers between devices, neighbours(): lax.ppermute(values, axis, [(i, (i + 1) % count) for i in range(count)])  5.76 us
    pallas_call x1, Pallas kernels, local(): pl.pallas_call(reduce_kernel, out_shape=(shape_of(SB_DEV, SITE_BLOCK), sh...  3.43 us
    pallas_call x1, Pallas kernels, local(): pl.pallas_call(gather_kernel, out_shape=(shape_of(SLOTS, 4, SITE_BLOCK),...  2.6 us
  transfers between devices with their start and end apart: 6, of which 4 were waited for; matrix products, arithmetic and copies ran while one was open for 0% of the time, Pallas kernels for 2%

profile of v3, /device:TPU:1, one launch (start us, length us, event | category | flops | bytes accessed | tf_op | source)
XLA Modules:
  0.0 85.2 jit_solution(11759225987577983632)
XLA Ops:
  0.6 0.0 copy-start.3
  0.6 2.0 %request.1 = (s32[128,128]{1,0:T(8,128)}, s32[16,128]{1,0:T(8,128)}) custom-call(s32[16,16]{1,0:T(8,128)} %bitcast.22, s32[16,16]{1,0:T(8,128)} %bitcast.23, s32[2,1,8]{2,1,0:T(1,128)} %bitcast.24), custom_call_target="tpu_custom_call" | custom-call | tf_op jit(solution)/shard_map/request/pallas_call | solution.py:348
  2.7 11.5 %all-to-all-start = ((s32[128,1,128]{2,1,0:T(1,128)}), s32[128,1,128]{2,1,0:T(1,128)S(1)}, u32[]{:S(2)}, u32[]{:S(2)}) async-start(s32[128,1,128]{2,1,0:T(1,128)} %bitcast.21), calls=%async_computation | async-start | bytes 131072 | tf_op jit(solution)/shard_map/all_to_all | solution.py:333
  14.2 1.1 %collective-permute-start.1 = (f32[16,128]{1,0:T(8,128)}, f32[16,128]{1,0:T(8,128)S(1)}, u32[]{:S(2)}, u32[]{:S(2)}) collective-permute-start(f32[16,128]{1,0:T(8,128)} %bitcast.18), channel_id=1, source_target_pairs={{16,0},{32,16},{48,32},{64,48},{80,64},{96,80},{112,96},{0,112},{1... | collective-permute-start | bytes 24584 | tf_op jit(solution)/shard_map/ppermute | solution.py:339
  15.2 0.7 collective-permute-start
  15.9 1.2 %copy-done = f32[3,65536]{1,0:T(4,128)S(1)} copy-done((f32[3,65536]{1,0:T(4,128)S(1)}, f32[3,65536]{1,0:T(4,128)}, u32[]{:S(2)}) %copy-start) | copy-done | bytes 786456
  17.1 0.9 %copy-done.1 = f32[65536]{0:T(1024)S(1)} copy-done((f32[65536]{0:T(1024)S(1)}, f32[65536]{0:T(1024)}, u32[]{:S(2)}) %copy-start.1) | copy-done | bytes 262168
  18.1 1.3 %table.1 = (f32[516,4,128]{2,1,0:T(4,128)S(1)}, f32[2064,128]{1,0:T(8,128)S(1)}) custom-call(f32[3,65536]{1,0:T(4,128)S(1)} %copy-done, f32[512,128]{1,0:T(8,128)S(1)} %bitcast.14), custom_call_target="tpu_custom_call" | custom-call | tf_op jit(solution)/shard_map/table/pallas_call | solution.py:367
  19.4 0.0 collective-permute-done.1.right_ref
  19.4 0.0 collective-permute-done.left_ref
  19.4 4.5 %all-to-all-done = s32[128,1,128]{2,1,0:T(1,128)S(1)} async-done(((s32[128,1,128]{2,1,0:T(1,128)}), s32[128,1,128]{2,1,0:T(1,128)S(1)}, u32[]{:S(2)}, u32[]{:S(2)}) %all-to-all-start) | async-done | bytes 65568 | tf_op jit(solution)/shard_map/all_to_all | solution.py:333
  23.9 2.6 %gather.1 = (f32[512,4,128]{2,1,0:T(4,128)}, s32[8,128]{1,0:T(8,128)S(1)}, f32[16,128]{1,0:T(8,128)S(1)}) custom-call(s32[128,128]{1,0:T(8,128)S(1)} %bitcast.15, f32[516,4,128]{2,1,0:T(4,128)S(1)} %get-tuple-element.16.table_ref, f32[16,128]{1,0:T(8,128)S(1)} %collective-permute-done.left_ref, f32[16,128]{1,0:T(8,128)S(1)} %bitcast.20, ...), custom_call_target="tpu_custom_call" | custom-call | tf_op jit(solution)/shard_map/gather/pallas_call | solution.py:380
  26.5 0.0 copy-start.2
  26.5 0.0 copy-start.4
  26.5 5.9 %all-to-all-start.1 = ((f32[512,4,128]{2,1,0:T(4,128)}), f32[512,4,128]{2,1,0:T(4,128)S(1)}, u32[]{:S(2)}, u32[]{:S(2)}) async-start(f32[512,4,128]{2,1,0:T(4,128)} %get-tuple-element.17), calls=%async_computation.1 | async-start | bytes 2097152 | tf_op jit(solution)/shard_map/all_to_all | solution.py:333
  32.5 5.6 %collective-permute-start.3 = (f32[16,128]{1,0:T(8,128)S(1)}, f32[16,128]{1,0:T(8,128)S(1)}, u32[]{:S(2)}, u32[]{:S(2)}) collective-permute-start(f32[16,128]{1,0:T(8,128)S(1)} %get-tuple-element.18.mid_ref), channel_id=1, source_target_pairs={{1,0},{2,1},{3,2},{4,3},{5,4},{6,5},{7,6},{8,7},{9,8},{10,9},{11,1... | collective-permute-start | bytes 24584 | tf_op jit(solution)/shard_map/ppermute | solution.py:339
  38.1 0.0 collective-permute-start.2
  38.1 0.4 prepare.1.lhs_ref
  38.5 0.3 collective-permute-done.3.below_ref
  38.9 5.8 %collective-permute-done.2.above_ref = f32[16,128]{1,0:T(8,128)S(1)} collective-permute-done((f32[16,128]{1,0:T(8,128)S(1)}, f32[16,128]{1,0:T(8,128)S(1)}, u32[]{:S(2)}, u32[]{:S(2)}) %collective-permute-start.2) | collective-permute-done | bytes 8224 | tf_op jit(solution)/shard_map/ppermute | solution.py:338
  44.6 6.7 %all-to-all-done.1.arrived_ref = f32[512,4,128]{2,1,0:T(4,128)S(1)} async-done(((f32[512,4,128]{2,1,0:T(4,128)}), f32[512,4,128]{2,1,0:T(4,128)S(1)}, u32[]{:S(2)}, u32[]{:S(2)}) %all-to-all-start.1) | async-done | bytes 1048608 | tf_op jit(solution)/shard_map/all_to_all | solution.py:333
  51.4 7.4 %transport.1 = (f32[16,128]{1,0:T(8,128)}, f32[512,4,128]{2,1,0:T(4,128)S(1)}) custom-call(s32[16,128]{1,0:T(8,128)S(1)} %copy-done.4, f32[512,4,128]{2,1,0:T(4,128)S(1)} %all-to-all-done.1.arrived_ref, bf16[16,128,48]{2,1,0:T(8,128)(2,1)S(1)} %prepare.1.lhs_ref, f32[3,16,128]{2,1,0:T(8,128)S(1)} %bitcast.17, ...), custom_call_target="tpu_custom_call" | custom-call | tf_op jit(solution)/shard_map/transport/pallas_call | solution.py:404
  58.8 23.0 %all_to_all.21.back_ref = f32[512,4,128]{2,1,0:T(4,128)S(1)} all-to-all(f32[512,4,128]{2,1,0:T(4,128)S(1)} %get-tuple-element.21), channel_id=1, replica_groups=mesh['gx'=8,'gy'=16] {'gx','gy'}, dimensions={0} | all-to-all | bytes 2097152 | tf_op jit(solution)/shard_map/all_to_all | solution.py:333
  81.8 3.4 %reduce.1 = (f32[512,128]{1,0:T(8,128)}, f32[3,65536]{1,0:T(4,128)}, f32[2064,128]{1,0:T(8,128)S(1)}) custom-call(s32[8,128]{1,0:T(8,128)S(1)} %get-tuple-element.20.ids_ref, f32[512,4,128]{2,1,0:T(4,128)S(1)} %all_to_all.21.back_ref, f32[2064,128]{1,0:T(8,128)S(1)} %get-tuple-element.22.start_ref), custom_call_target="tpu_custom_call", output_to_operand_aliasing={{2}: (2, {})} | custom-call | tf_op jit(solution)/shard_map/reduce/pallas_call | solution.py:423
  (5 shorter events, 0.0 us)
Async XLA Ops:
  0.6 23.3 %copy-start.3 = (f32[2,8,128]{2,1,0:T(8,128)S(1)}, f32[2,8,128]{2,1,0:T(8,128)}, u32[]{:S(2)}) copy-start(f32[2,8,128]{2,1,0:T(8,128)} %param.7) | copy-start | bytes 24580
  2.7 21.2 %all-to-all-start = ((s32[128,1,128]{2,1,0:T(1,128)}), s32[128,1,128]{2,1,0:T(1,128)S(1)}, u32[]{:S(2)}, u32[]{:S(2)}) async-start(s32[128,1,128]{2,1,0:T(1,128)} %bitcast.21), calls=%async_computation | async-start | bytes 131072 | tf_op jit(solution)/shard_map/all_to_all | solution.py:333
  14.2 5.2 %collective-permute-start.1 = (f32[16,128]{1,0:T(8,128)}, f32[16,128]{1,0:T(8,128)S(1)}, u32[]{:S(2)}, u32[]{:S(2)}) collective-permute-start(f32[16,128]{1,0:T(8,128)} %bitcast.18), channel_id=1, source_target_pairs={{16,0},{32,16},{48,32},{64,48},{80,64},{96,80},{112,96},{0,112},{1... | collective-permute-start | bytes 24584 | tf_op jit(solution)/shard_map/ppermute | solution.py:339
  15.2 4.1 %collective-permute-start = (f32[16,128]{1,0:T(8,128)}, f32[16,128]{1,0:T(8,128)S(1)}, u32[]{:S(2)}, u32[]{:S(2)}) collective-permute-start(f32[16,128]{1,0:T(8,128)} %bitcast.19), channel_id=1, source_target_pairs={{0,16},{16,32},{32,48},{48,64},{64,80},{80,96},{96,112},{112,0},{1... | collective-permute-start | bytes 24584 | tf_op jit(solution)/shard_map/ppermute | solution.py:338
  15.9 1.2 %copy-start = (f32[3,65536]{1,0:T(4,128)S(1)}, f32[3,65536]{1,0:T(4,128)}, u32[]{:S(2)}) copy-start(f32[3,65536]{1,0:T(4,128)} %position_hbm.1) | copy-start | bytes 2359300
  17.1 0.9 %copy-start.1 = (f32[65536]{0:T(1024)S(1)}, f32[65536]{0:T(1024)}, u32[]{:S(2)}) copy-start(f32[65536]{0:T(1024)} %param.13) | copy-start | bytes 786436
  26.5 11.6 %copy-start.2 = (f32[3,2,8,128]{3,2,1,0:T(8,128)S(1)}, f32[3,2,8,128]{3,2,1,0:T(8,128)}, u32[]{:S(2)}) copy-start(f32[3,2,8,128]{3,2,1,0:T(8,128)} %param.8) | copy-start | bytes 73732
  26.5 24.8 %copy-start.4 = (s32[16,128]{1,0:T(8,128)S(1)}, s32[16,128]{1,0:T(8,128)}, u32[]{:S(2)}) copy-start(s32[16,128]{1,0:T(8,128)} %get-tuple-element.14.target_ref) | copy-start | bytes 24580
  26.5 24.8 %all-to-all-start.1 = ((f32[512,4,128]{2,1,0:T(4,128)}), f32[512,4,128]{2,1,0:T(4,128)S(1)}, u32[]{:S(2)}, u32[]{:S(2)}) async-start(f32[512,4,128]{2,1,0:T(4,128)} %get-tuple-element.17), calls=%async_computation.1 | async-start | bytes 2097152 | tf_op jit(solution)/shard_map/all_to_all | solution.py:333
  32.5 6.4 %collective-permute-start.3 = (f32[16,128]{1,0:T(8,128)S(1)}, f32[16,128]{1,0:T(8,128)S(1)}, u32[]{:S(2)}, u32[]{:S(2)}) collective-permute-start(f32[16,128]{1,0:T(8,128)S(1)} %get-tuple-element.18.mid_ref), channel_id=1, source_target_pairs={{1,0},{2,1},{3,2},{4,3},{5,4},{6,5},{7,6},{8,7},{9,8},{10,9},{11,1... | collective-permute-start | bytes 24584 | tf_op jit(solution)/shard_map/ppermute | solution.py:339
  38.1 6.6 %collective-permute-start.2 = (f32[16,128]{1,0:T(8,128)S(1)}, f32[16,128]{1,0:T(8,128)S(1)}, u32[]{:S(2)}, u32[]{:S(2)}) collective-permute-start(f32[16,128]{1,0:T(8,128)S(1)} %get-tuple-element.18.mid_ref), channel_id=1, source_target_pairs={{0,1},{1,2},{2,3},{3,4},{4,5},{5,6},{6,7},{7,8},{8,9},{9,10},{10,1... | collective-permute-start | bytes 24584 | tf_op jit(solution)/shard_map/ppermute | solution.py:338

commit v4 on v3

--- a/solution.py
+++ b/solution.py
@@ -27,6 +27,7 @@
 KAPPA = math.log2(math.e) / EPSILON
 ROOT = math.sqrt(KAPPA)
 DEAD = -1e30
+PIECES = 4
 F32 = jnp.float32
 BF16 = jnp.bfloat16
 I32 = jnp.int32
@@ -35,7 +36,6 @@
 SMEM = pl.BlockSpec(memory_space=pltpu.SMEM)
 AXES = ("gx", "gy")
 LIMIT = pltpu.CompilerParams(vmem_limit_bytes=16 << 20)
-WIDE = pltpu.CompilerParams(vmem_limit_bytes=60 * 1024 * 1024)
 
 
 def gauss_values():
@@ -57,12 +57,23 @@
 
 
 def request_kernel(
-    owner_hbm, slot_hbm, count_hbm, request_ref, target_ref, owner_ref, slot_ref, count_ref, sems
+    owner_hbm,
+    slot_hbm,
+    count_hbm,
+    cells_hbm,
+    request_ref,
+    target_ref,
+    owner_ref,
+    slot_ref,
+    count_ref,
+    cells_ref,
+    sems,
 ):
     copies = [
         pltpu.make_async_copy(owner_hbm, owner_ref, sems.at[0]),
         pltpu.make_async_copy(slot_hbm, slot_ref, sems.at[1]),
         pltpu.make_async_copy(count_hbm, count_ref, sems.at[2]),
+        pltpu.make_async_copy(cells_hbm, cells_ref, sems.at[3]),
     ]
     for copy in copies:
         copy.start()
@@ -99,7 +110,23 @@
         hot_low, spread.astype(BF16), (((0,), (0,)), ((), ())), preferred_element_type=F32
     )
     request = request + pltpu.roll(request, 128 - CAP, 1)
-    request_ref[...] = request.astype(I32) - 1
+    request_ref[pl.ds(0, OWNERS, stride=2), :] = request - 1.0
+    edge_shape = (TILE, 2 * TILE)
+    edge_lane = iota(edge_shape, 1)
+    column = jnp.where(edge_lane < TILE, 0, TILE - HALF) + edge_lane % HALF
+    pick = (iota(edge_shape, 0) == column).astype(F32)
+    edges = jnp.dot(
+        cells_ref[...], pick, preferred_element_type=F32, precision=lax.Precision.HIGHEST
+    )
+    edge_shape = (TILES, 2 * TILE)
+    own_row = (iota(edge_shape, 1) % TILE) // HALF == iota(edge_shape, 0)
+    edges = jnp.sum(jnp.where(own_row, edges, 0.0), axis=0, keepdims=True)
+    columns = lax.axis_size("gx")
+    after = lax.rem(lax.axis_index("gx") + 1, columns)
+    to_after = iota((OWNERS, 128), 0) // (OWNERS // columns) == after
+    request_ref[pl.ds(1, OWNERS, stride=2), :] = jnp.where(
+        to_after, edges[:, TILE:], edges[:, :TILE]
+    )
     target = jnp.where(lane == CAND, counts, 0)
     for k in range(CAND):
         place = owners[:, k : k + 1] * CAP + rank[k * TILES : (k + 1) * TILES]
@@ -107,72 +134,7 @@
     target_ref[...] = target
 
 
-def table_kernel(position_hbm, weight_hbm, table_ref, start_ref, position_ref, weight_ref, sems):
-    first = pltpu.make_async_copy(position_hbm, position_ref, sems.at[0])
-    second = pltpu.make_async_copy(weight_hbm, weight_ref, sems.at[1])
-    first.start()
-    second.start()
-    row = iota((4, 128), 0)
-    dead = jnp.where(row == 3, DEAD, 0.0)
-    for r in range(CAP):
-        table_ref[SB_DEV + r] = dead
-        start_ref[(SB_DEV + r) * 4 : (SB_DEV + r + 1) * 4, :] = jnp.zeros((4, 128), F32)
-    first.wait()
-    second.wait()
-
-    def block(b, carry):
-        start = pl.multiple_of(b * SITE_BLOCK, SITE_BLOCK)
-        place = position_ref[:, pl.ds(start, SITE_BLOCK)]
-        table_ref[b, 0:3, :] = (place - 0.5) * ROOT
-        table_ref[b, 3:4, :] = weight_ref[pl.ds(b, 1), :]
-        line = pl.multiple_of(b * 4, 4)
-        start_ref[pl.ds(line, 3), :] = PRIOR_MASS * place
-        start_ref[pl.ds(line + 3, 1), :] = jnp.zeros((1, 128), F32)
-        return carry
-
-    lax.fori_loop(0, SB_DEV, block, 0, unroll=8)
-
-
-def filter_columns(left_ref, mid_ref, right_ref, out_ref):
-    shape = (3 * TILE, TILE)
-    shift = iota(shape, 0) - iota(shape, 1) - TILE
-    taps = jnp.zeros(shape, F32)
-    for offset in range(HALF + 1):
-        taps = jnp.where(jnp.abs(shift) == offset, GAUSS[HALF + offset], taps)
-    cells = jnp.concatenate([left_ref[...], mid_ref[...], right_ref[...]], axis=1)
-    out_ref[...] = jnp.dot(
-        cells, taps, preferred_element_type=F32, precision=lax.Precision.HIGHEST
-    )
-
-
-def gather_kernel(
-    asked_ref,
-    table_ref,
-    left_ref,
-    mid_ref,
-    right_ref,
-    out_ref,
-    ids_ref,
-    first_ref,
-    ids_smem,
-    sem,
-):
-    asked = jnp.transpose(asked_ref[...].astype(F32))[0:8].astype(I32)
-    ids_ref[...] = jnp.where(asked < 0, SB_DEV + iota((8, 128), 0) % CAP, asked)
-    copy = pltpu.make_async_copy(ids_ref, ids_smem, sem)
-    copy.start()
-    filter_columns(left_ref, mid_ref, right_ref, first_ref)
-    copy.wait()
-
-    def peer(step, carry):
-        for r in range(CAP):
-            out_ref[step * CAP + r] = table_ref[ids_smem[r, step]]
-        return carry
-
-    lax.fori_loop(0, OWNERS, peer, 0, unroll=8)
-
-
-def prepare_kernel(point_ref, lhs_ref):
+def prepare(point_ref, lhs_ref):
     row = iota((8, 128), 0)
 
     def tile(t, carry):
@@ -191,18 +153,135 @@
     lax.fori_loop(0, TILES, tile, 0, unroll=4)
 
 
+def table_kernel(
+    position_hbm,
+    weight_hbm,
+    point_hbm,
+    table_ref,
+    start_ref,
+    lhs_ref,
+    position_ref,
+    weight_ref,
+    point_ref,
+    sems,
+):
+    points = pltpu.make_async_copy(point_hbm, point_ref, sems.at[PIECES + 1])
+    points.start()
+    copies = [pltpu.make_async_copy(weight_hbm, weight_ref, sems.at[PIECES])]
+    width = SB_DEV * SITE_BLOCK // PIECES
+    for piece in range(PIECES):
+        part = pl.ds(piece * width, width)
+        copies.append(
+            pltpu.make_async_copy(
+                position_hbm.at[:, part], position_ref.at[:, part], sems.at[piece]
+            )
+        )
+    for copy in copies:
+        copy.start()
+    row = iota((4, 128), 0)
+    dead = jnp.where(row == 3, DEAD, 0.0)
+    for r in range(CAP):
+        table_ref[SB_DEV + r] = dead
+        start_ref[(SB_DEV + r) * 4 : (SB_DEV + r + 1) * 4, :] = jnp.zeros((4, 128), F32)
+
+    def block(b, carry):
+        start = pl.multiple_of(b * SITE_BLOCK, SITE_BLOCK)
+        place = position_ref[:, pl.ds(start, SITE_BLOCK)]
+        table_ref[b, 0:3, :] = (place - 0.5) * ROOT
+        table_ref[b, 3:4, :] = weight_ref[pl.ds(b, 1), :]
+        line = pl.multiple_of(b * 4, 4)
+        start_ref[pl.ds(line, 3), :] = PRIOR_MASS * place
+        start_ref[pl.ds(line + 3, 1), :] = jnp.zeros((1, 128), F32)
+        return carry
+
+    points.wait()
+    prepare(point_ref, lhs_ref)
+    copies[0].wait()
+    blocks = SB_DEV // PIECES
+    for piece in range(PIECES):
+        copies[piece + 1].wait()
+        lax.fori_loop(piece * blocks, (piece + 1) * blocks, block, 0, unroll=8)
+
+
+def smooth(halo_ref, tiles, rows_ref, load_ref):
+    count_x, count_y = lax.axis_size("gx"), lax.axis_size("gy")
+    here_x, here_y = lax.axis_index("gx"), lax.axis_index("gy")
+    shape = (3 * TILE, TILE)
+    row = iota(shape, 0)
+    source = jnp.where(
+        row < TILE, row, row % HALF + jnp.where(row < 2 * TILE, -HALF, TILE)
+    )
+    shift = (source - iota(shape, 1)).astype(F32)
+    taps = jnp.where(
+        jnp.abs(shift) <= HALF,
+        GAUSS_PEAK * jnp.exp(shift * shift * (-0.5 / (SIGMA_CELLS * SIGMA_CELLS))),
+        0.0,
+    )
+    shape = (TILES, TILE)
+    own_row = iota(shape, 1) // HALF == iota(shape, 0)
+    rows = []
+    for step, tile in zip((count_y - 1, 0, 1), tiles):
+        parts = [tile]
+        for side in (count_x - 1, 1):
+            peer = lax.rem(here_x + side, count_x) * count_y + lax.rem(here_y + step, count_y)
+            halo = halo_ref[pl.ds(2 * peer + 1, 1), :]
+            parts.append(jnp.where(own_row, halo, 0.0))
+        rows.append(jnp.concatenate(parts, axis=1))
+    first = jnp.dot(
+        jnp.concatenate(rows, axis=0),
+        taps,
+        preferred_element_type=F32,
+        precision=lax.Precision.HIGHEST,
+    )
+    planes = []
+    for z in range(PZ):
+        for part in range(3):
+            at = part * TILES + z * CY
+            rows_ref[z, part * CY : (part + 1) * CY, :] = first[at : at + CY]
+        total = GAUSS[0] * rows_ref[z, 0:CY, :]
+        for j in range(1, 2 * HALF + 1):
+            total = total + GAUSS[j] * rows_ref[z, j : j + CY, :]
+        planes.append(total)
+    load_ref[0:CY, :] = GAUSS[HALF] * planes[0] + GAUSS[HALF + 1] * planes[1]
+    load_ref[CY : 2 * CY, :] = GAUSS[HALF - 1] * planes[0] + GAUSS[HALF] * planes[1]
+
+
+def gather_kernel(
+    asked_ref,
+    table_ref,
+    above_ref,
+    mid_ref,
+    below_ref,
+    out_ref,
+    ids_ref,
+    load_ref,
+    rows_ref,
+    ids_smem,
+    sem,
+):
+    asked = jnp.transpose(asked_ref[pl.ds(0, OWNERS, stride=2), :])[0:8].astype(I32)
+    ids_ref[...] = jnp.where(asked < 0, SB_DEV + iota((8, 128), 0) % CAP, asked)
+    copy = pltpu.make_async_copy(ids_ref, ids_smem, sem)
+    copy.start()
+    smooth(asked_ref, (above_ref[...], mid_ref[...], below_ref[...]), rows_ref, load_ref)
+    copy.wait()
+
+    def peer(step, carry):
+        for r in range(CAP):
+            out_ref[step * CAP + r] = table_ref[ids_smem[r, step]]
+        return carry
+
+    lax.fori_loop(0, OWNERS, peer, 0, unroll=8)
+
+
 def transport_kernel(
     target_ref,
     arrived_ref,
     lhs_ref,
     point_ref,
-    above_ref,
-    mid_ref,
-    below_ref,
+    load_ref,
     potential_ref,
     out_ref,
-    rows_ref,
-    load_ref,
     top_ref,
     sum_ref,
     even_ref,
@@ -210,18 +289,6 @@
     even_load_ref,
     odd_load_ref,
 ):
-    planes = []
-    for z in range(PZ):
-        rows_ref[z, 0:CY, :] = above_ref[z * CY : (z + 1) * CY, :]
-        rows_ref[z, CY : 2 * CY, :] = mid_ref[z * CY : (z + 1) * CY, :]
-        rows_ref[z, 2 * CY : 3 * CY, :] = below_ref[z * CY : (z + 1) * CY, :]
-        total = GAUSS[0] * rows_ref[z, 0:CY, :]
-        for j in range(1, 2 * HALF + 1):
-            total = total + GAUSS[j] * rows_ref[z, j : j + CY, :]
-        planes.append(total)
-    load_ref[0:CY, :] = GAUSS[HALF] * planes[0] + GAUSS[HALF + 1] * planes[1]
-    load_ref[CY : 2 * CY, :] = GAUSS[HALF - 1] * planes[0] + GAUSS[HALF] * planes[1]
-
     row = iota((8, 128), 0)
     fixed = (row < 4) | (row == 7)
     factor = jnp.where(row == 7, KAPPA, 1.0)
@@ -329,6 +396,10 @@
     return jax.ShapeDtypeStruct(dims, dtype)
 
 
+def in_hbm(values):
+    return pltpu.with_memory_space_constraint(values, pltpu.HBM)
+
+
 def exchange(values):
     return lax.all_to_all(values, AXES, split_axis=0, concat_axis=0, tiled=True)
 
@@ -344,40 +415,55 @@
     density, point_position, block_owner, block_slot, block_count, site_position, site_weight
 ):
     cells = density.reshape(TILES, TILE)
-    left, right = neighbours(cells, "gx")
+    points = point_position.reshape(3, TILES, TILE)
+    above, below = neighbours(cells, "gy")
     request, target = pl.pallas_call(
         request_kernel,
-        out_shape=(shape_of(OWNERS, 128, dtype=I32), shape_of(TILES, 128, dtype=I32)),
-        in_specs=[HBM] * 3,
+        out_shape=(
+            shape_of(2 * OWNERS, 128),
+            shape_of(TILES, 128, dtype=I32),
+        ),
+        in_specs=[HBM] * 4,
         out_specs=(VMEM, VMEM),
         scratch_shapes=[
             pltpu.VMEM((TILES, CAND), I32),
             pltpu.VMEM((TILES, CAND), I32),
             pltpu.VMEM((PZ, 1, CY), I32),
-            pltpu.SemaphoreType.DMA((3,)),
+            pltpu.VMEM((TILES, TILE), F32),
+            pltpu.SemaphoreType.DMA((4,)),
         ],
-        compiler_params=WIDE,
+        compiler_params=LIMIT,
         name="request",
     )(
-        block_owner.reshape(TILES, CAND),
-        block_slot.reshape(TILES, CAND),
-        jnp.transpose(block_count, (0, 2, 1)),
+        in_hbm(block_owner.reshape(TILES, CAND)),
+        in_hbm(block_slot.reshape(TILES, CAND)),
+        in_hbm(jnp.transpose(block_count, (0, 2, 1))),
+        in_hbm(cells),
     )
     asked = exchange(request)
-    table, start = pl.pallas_call(
+    table, start, lhs = pl.pallas_call(
         table_kernel,
-        out_shape=(shape_of(SB_DEV + CAP, 4, SITE_BLOCK), shape_of((SB_DEV + CAP) * 4, SITE_BLOCK)),
-        in_specs=[HBM] * 2,
-        out_specs=(VMEM, VMEM),
+        out_shape=(
+            shape_of(SB_DEV + CAP, 4, SITE_BLOCK),
+            shape_of((SB_DEV + CAP) * 4, SITE_BLOCK),
+            shape_of(TILES, TILE, 48, dtype=BF16),
+        ),
+        in_specs=[HBM] * 3,
+        out_specs=(VMEM,) * 3,
         scratch_shapes=[
             pltpu.VMEM((3, SB_DEV * SITE_BLOCK), F32),
             pltpu.VMEM((SB_DEV, SITE_BLOCK), F32),
-            pltpu.SemaphoreType.DMA((2,)),
+            pltpu.VMEM((3, TILES, TILE), F32),
+            pltpu.SemaphoreType.DMA((PIECES + 2,)),
         ],
         compiler_params=LIMIT,
         name="table",
-    )(site_position, site_weight.reshape(SB_DEV, SITE_BLOCK))
-    blocks, ids, first_pass = pl.pallas_call(
+    )(
+        in_hbm(site_position),
+        in_hbm(site_weight.reshape(SB_DEV, SITE_BLOCK)),
+        in_hbm(points),
+    )
+    blocks, ids, load = pl.pallas_call(
         gather_kernel,
         out_shape=(
             shape_of(SLOTS, 4, SITE_BLOCK),
@@ -387,28 +473,20 @@
         in_specs=[VMEM] * 5,
         out_specs=(VMEM, VMEM, VMEM),
         compiler_params=LIMIT,
-        scratch_shapes=[pltpu.SMEM((8, 128), I32), pltpu.SemaphoreType.DMA],
+        scratch_shapes=[
+            pltpu.VMEM((PZ, 3 * CY, 128), F32),
+            pltpu.SMEM((8, 128), I32),
+            pltpu.SemaphoreType.DMA,
+        ],
         name="gather",
-    )(asked, table, left, cells, right)
+    )(asked, table, above, cells, below)
     arrived = exchange(blocks)
-    points = point_position.reshape(3, TILES, TILE)
-    lhs = pl.pallas_call(
-        prepare_kernel,
-        out_shape=shape_of(TILES, TILE, 48, dtype=BF16),
-        in_specs=[VMEM],
-        out_specs=VMEM,
-        compiler_params=LIMIT,
-        name="prepare",
-    )(points)
-    above, below = neighbours(first_pass, "gy")
     potential, moments = pl.pallas_call(
         transport_kernel,
         out_shape=(shape_of(TILES, TILE), shape_of(SLOTS, 4, SITE_BLOCK)),
-        in_specs=[SMEM] + [VMEM] * 6,
+        in_specs=[SMEM] + [VMEM] * 4,
         out_specs=(VMEM, VMEM),
         scratch_shapes=[
-            pltpu.VMEM((PZ, 3 * CY, 128), F32),
-            pltpu.VMEM((TILES, 128), F32),
             pltpu.VMEM((TILES, 128), F32),
             pltpu.VMEM((TILES, 128), F32),
             pltpu.VMEM((CAND // 2, 256, 256), BF16),
@@ -418,7 +496,7 @@
         ],
         compiler_params=LIMIT,
         name="transport",
-    )(target, arrived, lhs, points, above, first_pass, below)
+    )(target, arrived, lhs, points, load)
     returned = exchange(moments)
     site_mass, barycentre, _ = pl.pallas_call(
         reduce_kernel,

time: 85.6 us -> 86.1 us (level)
  blocking collectives: 23 us -> 47.4 us
  waiting for transfers between devices: 17.3 us -> 3.63 us
  starting transfers between devices: 24.8 us -> 17.1 us
  local copies, waits for them, and re-layouts: 2.19 us -> 0.01 us
    all_to_all x1 -> x2, blocking collectives: 23 us -> 47.4 us  [exchange(): return lax.all_to_all(values, AXES, split_axis=0, concat_axis=0, tiled=True)]
    all_to_all x2 -> x1, waiting for transfers between devices: 11.2 us -> 0.01 us  [exchange(): return lax.all_to_all(values, AXES, split_axis=0, concat_axis=0, tiled=True)]
    all_to_all x2 -> x1, starting transfers between devices: 17.4 us -> 11.5 us  [exchange(): return lax.all_to_all(values, AXES, split_axis=0, concat_axis=0, tiled=True)]
    unnamed x10 -> x4, local copies, waits for them, and re-layouts: 2.19 us -> 0.01 us
    ppermute x2 -> x1, waiting for transfers between devices: 5.76 us -> 3.62 us  [neighbours(): lax.ppermute(values, axis, [(i, (i + 1) % count) for i in range(count)])]
    pallas_call x1, Pallas kernels: 1.25 us -> 2.39 us  [local(): pl.pallas_call(table_kernel, out_shape=(shape_of(SB_DEV + CAP, 4, SITE_BL...]
    ppermute x2 -> x1, starting transfers between devices: 6.69 us -> 5.61 us  [neighbours(): lax.ppermute(values, axis, [((i + 1) % count, i) for i in range(count)])]
    pallas_call x1, Pallas kernels: 2.6 us -> 1.7 us  [local(): pl.pallas_call(gather_kernel, out_shape=(shape_of(SLOTS, 4, SITE_BLOCK),...]
  transfers between devices with their start and end apart: 6 -> 3, of which waited for: 4 -> 1; matrix products, arithmetic and copies ran while one was open for 0% -> 0% of each run, Pallas kernels for 2% -> 3%
where the time goes in v4:
time: 86.1 us; the launch traced here: 85.8 us
  blocking collectives  47.4 us (55%)
  starting transfers between devices  17.1 us (20%)
  Pallas kernels  17 us (20%)
  waiting for transfers between devices  3.63 us (4%)
    all_to_all x2, blocking collectives, exchange(): return lax.all_to_all(values, AXES, split_axis=0, concat_axis=0, tiled=True)  47.4 us
    all_to_all x1, starting transfers between devices, exchange(): return lax.all_to_all(values, AXES, split_axis=0, concat_axis=0, tiled=True)  11.5 us
    pallas_call x1, Pallas kernels, local(): pl.pallas_call(transport_kernel, out_shape=(shape_of(TILES, TILE), shape_...  7.43 us
    ppermute x1, starting transfers between devices, neighbours(): lax.ppermute(values, axis, [((i + 1) % count, i) for i in range(count)])  5.61 us
    ppermute x1, waiting for transfers between devices, neighbours(): lax.ppermute(values, axis, [(i, (i + 1) % count) for i in range(count)])  3.62 us
    pallas_call x1, Pallas kernels, local(): pl.pallas_call(reduce_kernel, out_shape=(shape_of(SB_DEV, SITE_BLOCK), sh...  3.43 us
    pallas_call x1, Pallas kernels, local(): pl.pallas_call(table_kernel, out_shape=(shape_of(SB_DEV + CAP, 4, SITE_BL...  2.39 us
    pallas_call x1, Pallas kernels, local(): pl.pallas_call(request_kernel, out_shape=(shape_of(2 * OWNERS, 128), shap...  2.06 us
  transfers between devices with their start and end apart: 3, of which 1 were waited for; matrix products, arithmetic and copies ran while one was open for 0% of the time, Pallas kernels for 3%

profile of v4, /device:TPU:1, one launch (start us, length us, event | category | flops | bytes accessed | tf_op | source)
XLA Modules:
  0.0 85.8 jit_solution(3526135514891302957)
XLA Ops:
  0.6 0.0 copy-start.1
  0.6 2.1 %request.1 = (f32[256,128]{1,0:T(8,128)}, s32[16,128]{1,0:T(8,128)S(1)}) custom-call(s32[16,16]{1,0:T(8,128)} %bitcast.20, s32[16,16]{1,0:T(8,128)} %bitcast.21, s32[2,1,8]{2,1,0:T(1,128)} %bitcast.22, f32[16,128]{1,0:T(8,128)} %bitcast.15), custom_call_target="tpu_custom_call" | custom-call | tf_op jit(solution)/shard_map/request/pallas_call | solution.py:420
  2.7 11.5 %all-to-all-start = ((f32[128,2,128]{2,1,0:T(2,128)}), f32[128,2,128]{2,1,0:T(2,128)S(1)}, u32[]{:S(2)}, u32[]{:S(2)}) async-start(f32[128,2,128]{2,1,0:T(2,128)} %bitcast.5), calls=%async_computation | async-start | bytes 262144 | tf_op jit(solution)/shard_map/all_to_all | solution.py:404
  14.2 5.6 %collective-permute-start.1 = (f32[16,128]{1,0:T(8,128)}, f32[16,128]{1,0:T(8,128)S(1)}, u32[]{:S(2)}, u32[]{:S(2)}) collective-permute-start(f32[16,128]{1,0:T(8,128)} %bitcast.16), channel_id=1, source_target_pairs={{1,0},{2,1},{3,2},{4,3},{5,4},{6,5},{7,6},{8,7},{9,8},{10,9},{11,1... | collective-permute-start | bytes 24584 | tf_op jit(solution)/shard_map/ppermute | solution.py:410
  19.8 0.0 collective-permute-start
  19.8 2.4 %table.1 = (f32[516,4,128]{2,1,0:T(4,128)S(1)}, f32[2064,128]{1,0:T(8,128)S(1)}, bf16[16,128,48]{2,1,0:T(8,128)(2,1)S(1)}) custom-call(f32[3,65536]{1,0:T(4,128)} %position_hbm.1, f32[512,128]{1,0:T(8,128)} %bitcast.19, f32[3,16,128]{2,1,0:T(8,128)} %bitcast.13), custom_call_target="tpu_custom_call" | custom-call | tf_op jit(solution)/shard_map/table/pallas_call | solution.py:444
  22.2 0.0 collective-permute-done.1.below_ref
  22.2 3.6 %collective-permute-done.above_ref = f32[16,128]{1,0:T(8,128)S(1)} collective-permute-done((f32[16,128]{1,0:T(8,128)}, f32[16,128]{1,0:T(8,128)S(1)}, u32[]{:S(2)}, u32[]{:S(2)}) %collective-permute-start) | collective-permute-done | bytes 8224 | tf_op jit(solution)/shard_map/ppermute | solution.py:409
  25.9 0.0 all-to-all-done
  25.9 0.0 copy-done.1
  25.9 1.7 %gather.1 = (f32[512,4,128]{2,1,0:T(4,128)S(1)}, s32[8,128]{1,0:T(8,128)S(1)}, f32[16,128]{1,0:T(8,128)S(1)}) custom-call(f32[256,128]{1,0:T(8,128)S(1)} %bitcast.12, f32[516,4,128]{2,1,0:T(4,128)S(1)} %get-tuple-element.17.table_ref, f32[16,128]{1,0:T(8,128)S(1)} %collective-permute-done.above_ref, f32[16,128]{1,0:T(8,128)S(1)} %bitcast.18, ...), custom_call_target="tpu_custom_call" | custom-call | tf_op jit(solution)/shard_map/gather/pallas_call | solution.py:466
  27.6 0.0 copy-start
  27.6 24.4 %all_to_all.21.arrived_ref = f32[512,4,128]{2,1,0:T(4,128)S(1)} all-to-all(f32[512,4,128]{2,1,0:T(4,128)S(1)} %get-tuple-element.18), channel_id=1, replica_groups=mesh['gx'=8,'gy'=16] {'gx','gy'}, dimensions={0} | all-to-all | bytes 2097152 | tf_op jit(solution)/shard_map/all_to_all | solution.py:404
  52.0 0.0 copy-done
  52.0 7.4 %transport.1 = (f32[16,128]{1,0:T(8,128)}, f32[512,4,128]{2,1,0:T(4,128)S(1)}) custom-call(s32[16,128]{1,0:T(8,128)S(1)} %get-tuple-element.15.target_ref, f32[512,4,128]{2,1,0:T(4,128)S(1)} %all_to_all.21.arrived_ref, bf16[16,128,48]{2,1,0:T(8,128)(2,1)S(1)} %get-tuple-element.19.lhs_ref, f32[3,16,128]{2,1,0:T(8,128)S(1)} %bitcast.14, ...), custom_call_target="tpu_custom_call" | custom-call | tf_op jit(solution)/shard_map/transport/pallas_call | solution.py:484
  59.4 23.0 %all_to_all.22.back_ref = f32[512,4,128]{2,1,0:T(4,128)S(1)} all-to-all(f32[512,4,128]{2,1,0:T(4,128)S(1)} %get-tuple-element.23), channel_id=1, replica_groups=mesh['gx'=8,'gy'=16] {'gx','gy'}, dimensions={0} | all-to-all | bytes 2097152 | tf_op jit(solution)/shard_map/all_to_all | solution.py:404
  82.4 3.4 %reduce.1 = (f32[512,128]{1,0:T(8,128)}, f32[3,65536]{1,0:T(4,128)}, f32[2064,128]{1,0:T(8,128)S(1)}) custom-call(s32[8,128]{1,0:T(8,128)S(1)} %get-tuple-element.22.ids_ref, f32[512,4,128]{2,1,0:T(4,128)S(1)} %all_to_all.22.back_ref, f32[2064,128]{1,0:T(8,128)S(1)} %get-tuple-element.24.start_ref), custom_call_target="tpu_custom_call", output_to_operand_aliasing={{2}: (2, {})} | custom-call | tf_op jit(solution)/shard_map/reduce/pallas_call | solution.py:501
Async XLA Ops:
  0.6 25.2 %copy-start.1 = (f32[2,8,128]{2,1,0:T(8,128)S(1)}, f32[2,8,128]{2,1,0:T(8,128)}, u32[]{:S(2)}) copy-start(f32[2,8,128]{2,1,0:T(8,128)} %param.7) | copy-start | bytes 24580
  2.7 23.1 %all-to-all-start = ((f32[128,2,128]{2,1,0:T(2,128)}), f32[128,2,128]{2,1,0:T(2,128)S(1)}, u32[]{:S(2)}, u32[]{:S(2)}) async-start(f32[128,2,128]{2,1,0:T(2,128)} %bitcast.5), calls=%async_computation | async-start | bytes 262144 | tf_op jit(solution)/shard_map/all_to_all | solution.py:404
  14.2 8.0 %collective-permute-start.1 = (f32[16,128]{1,0:T(8,128)}, f32[16,128]{1,0:T(8,128)S(1)}, u32[]{:S(2)}, u32[]{:S(2)}) collective-permute-start(f32[16,128]{1,0:T(8,128)} %bitcast.16), channel_id=1, source_target_pairs={{1,0},{2,1},{3,2},{4,3},{5,4},{6,5},{7,6},{8,7},{9,8},{10,9},{11,1... | collective-permute-start | bytes 24584 | tf_op jit(solution)/shard_map/ppermute | solution.py:410
  19.8 6.0 %collective-permute-start = (f32[16,128]{1,0:T(8,128)}, f32[16,128]{1,0:T(8,128)S(1)}, u32[]{:S(2)}, u32[]{:S(2)}) collective-permute-start(f32[16,128]{1,0:T(8,128)} %bitcast.17), channel_id=1, source_target_pairs={{0,1},{1,2},{2,3},{3,4},{4,5},{5,6},{6,7},{7,8},{8,9},{9,10},{10,1... | collective-permute-start | bytes 24584 | tf_op jit(solution)/shard_map/ppermute | solution.py:409
  27.6 24.4 %copy-start = (f32[3,2,8,128]{3,2,1,0:T(8,128)S(1)}, f32[3,2,8,128]{3,2,1,0:T(8,128)}, u32[]{:S(2)}) copy-start(f32[3,2,8,128]{3,2,1,0:T(8,128)} %param.8) | copy-start | bytes 73732

commit v5 on v4

--- a/solution.py
+++ b/solution.py
@@ -249,21 +249,31 @@
 def gather_kernel(
     asked_ref,
     table_ref,
-    above_ref,
-    mid_ref,
-    below_ref,
+    above_hbm,
+    mid_hbm,
+    below_hbm,
     out_ref,
     ids_ref,
     load_ref,
     rows_ref,
+    tiles_ref,
     ids_smem,
     sem,
+    tile_sems,
 ):
+    copies = [
+        pltpu.make_async_copy(tile, tiles_ref.at[part], tile_sems.at[part])
+        for part, tile in enumerate((above_hbm, mid_hbm, below_hbm))
+    ]
+    for tile_copy in copies:
+        tile_copy.start()
     asked = jnp.transpose(asked_ref[pl.ds(0, OWNERS, stride=2), :])[0:8].astype(I32)
     ids_ref[...] = jnp.where(asked < 0, SB_DEV + iota((8, 128), 0) % CAP, asked)
     copy = pltpu.make_async_copy(ids_ref, ids_smem, sem)
     copy.start()
-    smooth(asked_ref, (above_ref[...], mid_ref[...], below_ref[...]), rows_ref, load_ref)
+    for tile_copy in copies:
+        tile_copy.wait()
+    smooth(asked_ref, [tiles_ref[part] for part in range(3)], rows_ref, load_ref)
     copy.wait()
 
     def peer(step, carry):
@@ -411,12 +421,12 @@
     return before, after
 
 
-def local(
+def transport_step(
     density, point_position, block_owner, block_slot, block_count, site_position, site_weight
 ):
     cells = density.reshape(TILES, TILE)
     points = point_position.reshape(3, TILES, TILE)
-    above, below = neighbours(cells, "gy")
+    above, below = neighbours(in_hbm(cells), "gy")
     request, target = pl.pallas_call(
         request_kernel,
         out_shape=(
@@ -470,16 +480,18 @@
             shape_of(8, 128, dtype=I32),
             shape_of(TILES, TILE),
         ),
-        in_specs=[VMEM] * 5,
+        in_specs=[VMEM] * 2 + [HBM] * 3,
         out_specs=(VMEM, VMEM, VMEM),
         compiler_params=LIMIT,
         scratch_shapes=[
             pltpu.VMEM((PZ, 3 * CY, 128), F32),
+            pltpu.VMEM((3, TILES, TILE), F32),
             pltpu.SMEM((8, 128), I32),
             pltpu.SemaphoreType.DMA,
+            pltpu.SemaphoreType.DMA((3,)),
         ],
         name="gather",
-    )(asked, table, above, cells, below)
+    )(asked, table, in_hbm(above), in_hbm(cells), in_hbm(below))
     arrived = exchange(blocks)
     potential, moments = pl.pallas_call(
         transport_kernel,
@@ -530,4 +542,4 @@
         P(("gx", "gy")),
     )
     out_specs = (P(None, "gy", "gx"), P(("gx", "gy")), P(None, ("gx", "gy")))
-    return jax.shard_map(local, mesh=mesh, in_specs=in_specs, out_specs=out_specs, check_vma=False)
+    return jax.shard_map(transport_step, mesh=mesh, in_specs=in_specs, out_specs=out_specs, check_vma=False)

time: 86.1 us -> 87 us (1.010)
  no operation moved by 1% of the time
where the time goes in v5:
time: 87 us; the launch traced here: 86.6 us
  blocking collectives  47.4 us (54%)
  Pallas kernels  17.2 us (20%)
  starting transfers between devices  17.1 us (20%)
  waiting for transfers between devices  3.62 us (4%)
    all_to_all x2, blocking collectives, exchange(): return lax.all_to_all(values, AXES, split_axis=0, concat_axis=0, tiled=True)  47.4 us
    all_to_all x1, starting transfers between devices, exchange(): return lax.all_to_all(values, AXES, split_axis=0, concat_axis=0, tiled=True)  11.5 us
    pallas_call x1, Pallas kernels, transport_step(): pl.pallas_call(transport_kernel, out_shape=(shape_of(TILES, TILE), shape_...  7.43 us
    ppermute x1, starting transfers between devices, neighbours(): lax.ppermute(values, axis, [((i + 1) % count, i) for i in range(count)])  5.61 us
    ppermute x1, waiting for transfers between devices, neighbours(): lax.ppermute(values, axis, [(i, (i + 1) % count) for i in range(count)])  3.61 us
    pallas_call x1, Pallas kernels, transport_step(): pl.pallas_call(reduce_kernel, out_shape=(shape_of(SB_DEV, SITE_BLOCK), sh...  3.43 us
    pallas_call x1, Pallas kernels, transport_step(): pl.pallas_call(table_kernel, out_shape=(shape_of(SB_DEV + CAP, 4, SITE_BL...  2.39 us
    pallas_call x1, Pallas kernels, transport_step(): pl.pallas_call(request_kernel, out_shape=(shape_of(2 * OWNERS, 128), shap...  2.04 us
  transfers between devices with their start and end apart: 3, of which 1 were waited for; matrix products, arithmetic and copies ran while one was open for 0% of the time, Pallas kernels for 3%

profile of v5, /device:TPU:1, one launch (start us, length us, event | category | flops | bytes accessed | tf_op | source)
XLA Modules:
  0.0 86.6 jit_solution(18374345936542722472)
XLA Ops:
  0.6 2.0 %request.1 = (f32[256,128]{1,0:T(8,128)}, s32[16,128]{1,0:T(8,128)S(1)}) custom-call(s32[16,16]{1,0:T(8,128)} %bitcast.20, s32[16,16]{1,0:T(8,128)} %bitcast.21, s32[2,1,8]{2,1,0:T(1,128)} %bitcast.22, f32[16,128]{1,0:T(8,128)} %bitcast.16), custom_call_target="tpu_custom_call" | custom-call | tf_op jit(solution)/shard_map/request/pallas_call | solution.py:430
  2.7 11.5 %all-to-all-start = ((f32[128,2,128]{2,1,0:T(2,128)}), f32[128,2,128]{2,1,0:T(2,128)S(1)}, u32[]{:S(2)}, u32[]{:S(2)}) async-start(f32[128,2,128]{2,1,0:T(2,128)} %bitcast.5), calls=%async_computation | async-start | bytes 262144 | tf_op jit(solution)/shard_map/all_to_all | solution.py:414
  14.2 5.6 %collective-permute-start.1 = (f32[16,128]{1,0:T(8,128)}, f32[16,128]{1,0:T(8,128)S(1)}, u32[]{:S(2)}, u32[]{:S(2)}) collective-permute-start(f32[16,128]{1,0:T(8,128)} %bitcast.17), channel_id=1, source_target_pairs={{1,0},{2,1},{3,2},{4,3},{5,4},{6,5},{7,6},{8,7},{9,8},{10,9},{11,1... | collective-permute-start | bytes 24584 | tf_op jit(solution)/shard_map/ppermute | solution.py:420
  19.8 0.0 collective-permute-start
  19.8 2.4 %table.1 = (f32[516,4,128]{2,1,0:T(4,128)S(1)}, f32[2064,128]{1,0:T(8,128)S(1)}, bf16[16,128,48]{2,1,0:T(8,128)(2,1)S(1)}) custom-call(f32[3,65536]{1,0:T(4,128)} %position_hbm.1, f32[512,128]{1,0:T(8,128)} %bitcast.15, f32[3,16,128]{2,1,0:T(8,128)} %bitcast.13), custom_call_target="tpu_custom_call" | custom-call | tf_op jit(solution)/shard_map/table/pallas_call | solution.py:454
  22.2 0.0 collective-permute-done.1.below_hbm
  22.2 0.0 copy-start.1
  22.2 3.6 %collective-permute-done.above_hbm = f32[16,128]{1,0:T(8,128)S(1)} collective-permute-done((f32[16,128]{1,0:T(8,128)}, f32[16,128]{1,0:T(8,128)S(1)}, u32[]{:S(2)}, u32[]{:S(2)}) %collective-permute-start) | collective-permute-done | bytes 8224 | tf_op jit(solution)/shard_map/ppermute | solution.py:419
  25.8 0.0 copy-start.2
  25.8 0.0 all-to-all-done
  25.8 0.0 copy-done.1
  25.8 0.6 copy-done.2
  26.4 1.9 %gather.1 = (f32[512,4,128]{2,1,0:T(4,128)S(1)}, s32[8,128]{1,0:T(8,128)S(1)}, f32[16,128]{1,0:T(8,128)S(1)}) custom-call(f32[256,128]{1,0:T(8,128)S(1)} %bitcast.12, f32[516,4,128]{2,1,0:T(4,128)S(1)} %get-tuple-element.17.table_ref, f32[16,128]{1,0:T(8,128)} %copy-done.2, f32[16,128]{1,0:T(8,128)} %bitcast.19, f32[16,128]{1,0:T(8,128)} %copy-done.1), custom_call_target="tpu_custom_call" | custom-call | tf_op jit(solution)/shard_map/gather/pallas_call | solution.py:476
  28.4 0.0 copy-start
  28.4 24.4 %all_to_all.21.arrived_ref = f32[512,4,128]{2,1,0:T(4,128)S(1)} all-to-all(f32[512,4,128]{2,1,0:T(4,128)S(1)} %get-tuple-element.18), channel_id=1, replica_groups=mesh['gx'=8,'gy'=16] {'gx','gy'}, dimensions={0} | all-to-all | bytes 2097152 | tf_op jit(solution)/shard_map/all_to_all | solution.py:414
  52.8 0.0 copy-done
  52.8 7.4 %transport.1 = (f32[16,128]{1,0:T(8,128)}, f32[512,4,128]{2,1,0:T(4,128)S(1)}) custom-call(s32[16,128]{1,0:T(8,128)S(1)} %get-tuple-element.15.target_ref, f32[512,4,128]{2,1,0:T(4,128)S(1)} %all_to_all.21.arrived_ref, bf16[16,128,48]{2,1,0:T(8,128)(2,1)S(1)} %get-tuple-element.19.lhs_ref, f32[3,16,128]{2,1,0:T(8,128)S(1)} %bitcast.14, ...), custom_call_target="tpu_custom_call" | custom-call | tf_op jit(solution)/shard_map/transport/pallas_call | solution.py:496
  60.2 23.0 %all_to_all.22.back_ref = f32[512,4,128]{2,1,0:T(4,128)S(1)} all-to-all(f32[512,4,128]{2,1,0:T(4,128)S(1)} %get-tuple-element.23), channel_id=1, replica_groups=mesh['gx'=8,'gy'=16] {'gx','gy'}, dimensions={0} | all-to-all | bytes 2097152 | tf_op jit(solution)/shard_map/all_to_all | solution.py:414
  83.2 3.4 %reduce.1 = (f32[512,128]{1,0:T(8,128)}, f32[3,65536]{1,0:T(4,128)}, f32[2064,128]{1,0:T(8,128)S(1)}) custom-call(s32[8,128]{1,0:T(8,128)S(1)} %get-tuple-element.22.ids_ref, f32[512,4,128]{2,1,0:T(4,128)S(1)} %all_to_all.22.back_ref, f32[2064,128]{1,0:T(8,128)S(1)} %get-tuple-element.24.start_ref), custom_call_target="tpu_custom_call", output_to_operand_aliasing={{2}: (2, {})} | custom-call | tf_op jit(solution)/shard_map/reduce/pallas_call | solution.py:513
Async XLA Ops:
  2.7 23.1 %all-to-all-start = ((f32[128,2,128]{2,1,0:T(2,128)}), f32[128,2,128]{2,1,0:T(2,128)S(1)}, u32[]{:S(2)}, u32[]{:S(2)}) async-start(f32[128,2,128]{2,1,0:T(2,128)} %bitcast.5), calls=%async_computation | async-start | bytes 262144 | tf_op jit(solution)/shard_map/all_to_all | solution.py:414
  14.2 8.0 %collective-permute-start.1 = (f32[16,128]{1,0:T(8,128)}, f32[16,128]{1,0:T(8,128)S(1)}, u32[]{:S(2)}, u32[]{:S(2)}) collective-permute-start(f32[16,128]{1,0:T(8,128)} %bitcast.17), channel_id=1, source_target_pairs={{1,0},{2,1},{3,2},{4,3},{5,4},{6,5},{7,6},{8,7},{9,8},{10,9},{11,1... | collective-permute-start | bytes 24584 | tf_op jit(solution)/shard_map/ppermute | solution.py:420
  19.8 6.0 %collective-permute-start = (f32[16,128]{1,0:T(8,128)}, f32[16,128]{1,0:T(8,128)S(1)}, u32[]{:S(2)}, u32[]{:S(2)}) collective-permute-start(f32[16,128]{1,0:T(8,128)} %bitcast.18), channel_id=1, source_target_pairs={{0,1},{1,2},{2,3},{3,4},{4,5},{5,6},{6,7},{7,8},{8,9},{9,10},{10,1... | collective-permute-start | bytes 24584 | tf_op jit(solution)/shard_map/ppermute | solution.py:419
  22.2 3.6 %copy-start.1 = (f32[16,128]{1,0:T(8,128)}, f32[16,128]{1,0:T(8,128)S(1)}, u32[]{:S(2)}) copy-start(f32[16,128]{1,0:T(8,128)S(1)} %collective-permute-done.1.below_hbm) | copy-start | bytes 24580
  25.8 0.6 copy-start.2
  28.4 24.4 %copy-start = (f32[3,2,8,128]{3,2,1,0:T(8,128)S(1)}, f32[3,2,8,128]{3,2,1,0:T(8,128)}, u32[]{:S(2)}) copy-start(f32[3,2,8,128]{3,2,1,0:T(8,128)} %param.8) | copy-start | bytes 73732

commit v6 on v4

--- a/solution.py
+++ b/solution.py
@@ -203,7 +203,8 @@
         lax.fori_loop(piece * blocks, (piece + 1) * blocks, block, 0, unroll=8)
 
 
-def smooth(halo_ref, tiles, rows_ref, load_ref):
+def smooth_kernel(halo_ref, above_ref, mid_ref, below_ref, load_ref, rows_ref):
+    tiles = (above_ref[...], mid_ref[...], below_ref[...])
     count_x, count_y = lax.axis_size("gx"), lax.axis_size("gy")
     here_x, here_y = lax.axis_index("gx"), lax.axis_index("gy")
     shape = (3 * TILE, TILE)
@@ -249,13 +250,8 @@
 def gather_kernel(
     asked_ref,
     table_ref,
-    above_ref,
-    mid_ref,
-    below_ref,
     out_ref,
     ids_ref,
-    load_ref,
-    rows_ref,
     ids_smem,
     sem,
 ):
@@ -263,7 +259,6 @@
     ids_ref[...] = jnp.where(asked < 0, SB_DEV + iota((8, 128), 0) % CAP, asked)
     copy = pltpu.make_async_copy(ids_ref, ids_smem, sem)
     copy.start()
-    smooth(asked_ref, (above_ref[...], mid_ref[...], below_ref[...]), rows_ref, load_ref)
     copy.wait()
 
     def peer(step, carry):
@@ -416,7 +411,6 @@
 ):
     cells = density.reshape(TILES, TILE)
     points = point_position.reshape(3, TILES, TILE)
-    above, below = neighbours(cells, "gy")
     request, target = pl.pallas_call(
         request_kernel,
         out_shape=(
@@ -463,24 +457,30 @@
         in_hbm(site_weight.reshape(SB_DEV, SITE_BLOCK)),
         in_hbm(points),
     )
-    blocks, ids, load = pl.pallas_call(
+    blocks, ids = pl.pallas_call(
         gather_kernel,
         out_shape=(
             shape_of(SLOTS, 4, SITE_BLOCK),
             shape_of(8, 128, dtype=I32),
-            shape_of(TILES, TILE),
         ),
-        in_specs=[VMEM] * 5,
-        out_specs=(VMEM, VMEM, VMEM),
+        in_specs=[VMEM] * 2,
+        out_specs=(VMEM, VMEM),
         compiler_params=LIMIT,
-        scratch_shapes=[
-            pltpu.VMEM((PZ, 3 * CY, 128), F32),
-            pltpu.SMEM((8, 128), I32),
-            pltpu.SemaphoreType.DMA,
-        ],
+        scratch_shapes=[pltpu.SMEM((8, 128), I32), pltpu.SemaphoreType.DMA],
         name="gather",
-    )(asked, table, above, cells, below)
+    )(asked, table)
+    cells, blocks = lax.optimization_barrier((cells, blocks))
     arrived = exchange(blocks)
+    above, below = neighbours(cells, "gy")
+    load = pl.pallas_call(
+        smooth_kernel,
+        out_shape=shape_of(TILES, TILE),
+        in_specs=[VMEM] * 4,
+        out_specs=VMEM,
+        scratch_shapes=[pltpu.VMEM((PZ, 3 * CY, 128), F32)],
+        compiler_params=LIMIT,
+        name="smooth",
+    )(asked, above, cells, below)
     potential, moments = pl.pallas_call(
         transport_kernel,
         out_shape=(shape_of(TILES, TILE), shape_of(SLOTS, 4, SITE_BLOCK)),

time: 86.1 us -> 84.1 us (0.977)
  blocking collectives: 47.4 us -> 23 us
  waiting for transfers between devices: 3.63 us -> 19.9 us
  starting transfers between devices: 17.1 us -> 21.3 us
  local copies, waits for them, and re-layouts: 0.01 us -> 1.76 us
    all_to_all x2 -> x1, blocking collectives: 47.4 us -> 23 us  [exchange(): return lax.all_to_all(values, AXES, split_axis=0, concat_axis=0, tiled=True)]
    all_to_all x1 -> x2, waiting for transfers between devices: 0.01 us -> 13.4 us  [exchange(): return lax.all_to_all(values, AXES, split_axis=0, concat_axis=0, tiled=True)]
    all_to_all x1 -> x2, starting transfers between devices: 11.5 us -> 15.5 us  [exchange(): return lax.all_to_all(values, AXES, split_axis=0, concat_axis=0, tiled=True)]
    ppermute x1, waiting for transfers between devices: 3.62 us -> 5.75 us  [neighbours(): lax.ppermute(values, axis, [(i, (i + 1) % count) for i in range(count)])]
    unnamed x4 -> x10, local copies, waits for them, and re-layouts: 0.01 us -> 1.76 us
  transfers between devices with their start and end apart: 3 -> 4, of which waited for: 1 -> 4; matrix products, arithmetic and copies ran while one was open for 0% -> 0% of each run, Pallas kernels for 3% -> 3%
where the time goes in v6:
time: 84.1 us; the launch traced here: 83.7 us
  blocking collectives  23 us (27%)
  starting transfers between devices  21.3 us (25%)
  waiting for transfers between devices  19.9 us (24%)
  Pallas kernels  17.1 us (20%)
  local copies, waits for them, and re-layouts  1.76 us (2%)
    all_to_all x1, blocking collectives, exchange(): return lax.all_to_all(values, AXES, split_axis=0, concat_axis=0, tiled=True)  23 us
    all_to_all x2, starting transfers between devices, exchange(): return lax.all_to_all(values, AXES, split_axis=0, concat_axis=0, tiled=True)  15.5 us
    all_to_all x2, waiting for transfers between devices, exchange(): return lax.all_to_all(values, AXES, split_axis=0, concat_axis=0, tiled=True)  13.4 us
    pallas_call x1, Pallas kernels, local(): pl.pallas_call(transport_kernel, out_shape=(shape_of(TILES, TILE), shape_...  7.41 us
    ppermute x1, waiting for transfers between devices, neighbours(): lax.ppermute(values, axis, [(i, (i + 1) % count) for i in range(count)])  5.75 us
    ppermute x1, starting transfers between devices, neighbours(): lax.ppermute(values, axis, [((i + 1) % count, i) for i in range(count)])  5.75 us
    pallas_call x1, Pallas kernels, local(): pl.pallas_call(reduce_kernel, out_shape=(shape_of(SB_DEV, SITE_BLOCK), sh...  3.43 us
    pallas_call x1, Pallas kernels, local(): pl.pallas_call(table_kernel, out_shape=(shape_of(SB_DEV + CAP, 4, SITE_BL...  2.39 us
  transfers between devices with their start and end apart: 4, of which 4 were waited for; matrix products, arithmetic and copies ran while one was open for 0% of the time, Pallas kernels for 3%

profile of v6, /device:TPU:1, one launch (start us, length us, event | category | flops | bytes accessed | tf_op | source)
XLA Modules:
  0.0 83.7 jit_solution(5814987437035946440)
XLA Ops:
  0.6 2.0 %request.1 = (f32[256,128]{1,0:T(8,128)}, s32[16,128]{1,0:T(8,128)S(1)}) custom-call(s32[16,16]{1,0:T(8,128)} %bitcast.21, s32[16,16]{1,0:T(8,128)} %bitcast.22, s32[2,1,8]{2,1,0:T(1,128)} %bitcast.23, f32[16,128]{1,0:T(8,128)} %bitcast.16), custom_call_target="tpu_custom_call" | custom-call | tf_op jit(solution)/shard_map/request/pallas_call | solution.py:414
  2.7 11.5 %all-to-all-start = ((f32[128,2,128]{2,1,0:T(2,128)}), f32[128,2,128]{2,1,0:T(2,128)S(1)}, u32[]{:S(2)}, u32[]{:S(2)}) async-start(f32[128,2,128]{2,1,0:T(2,128)} %bitcast.5), calls=%async_computation | async-start | bytes 262144 | tf_op jit(solution)/shard_map/all_to_all | solution.py:399
  14.2 2.4 %table.1 = (f32[516,4,128]{2,1,0:T(4,128)S(1)}, f32[2064,128]{1,0:T(8,128)S(1)}, bf16[16,128,48]{2,1,0:T(8,128)(2,1)S(1)}) custom-call(f32[3,65536]{1,0:T(4,128)} %position_hbm.1, f32[512,128]{1,0:T(8,128)} %bitcast.20, f32[3,16,128]{2,1,0:T(8,128)} %bitcast.14), custom_call_target="tpu_custom_call" | custom-call | tf_op jit(solution)/shard_map/table/pallas_call | solution.py:438
  16.6 0.0 copy-start.1
  16.6 0.8 copy-done.1
  17.4 7.0 %all-to-all-done = f32[128,2,128]{2,1,0:T(2,128)S(1)} async-done(((f32[128,2,128]{2,1,0:T(2,128)}), f32[128,2,128]{2,1,0:T(2,128)S(1)}, u32[]{:S(2)}, u32[]{:S(2)}) %all-to-all-start) | async-done | bytes 131104 | tf_op jit(solution)/shard_map/all_to_all | solution.py:399
  24.4 1.5 %gather.1 = (f32[512,4,128]{2,1,0:T(4,128)S(1)}, s32[8,128]{1,0:T(8,128)S(1)}) custom-call(f32[256,128]{1,0:T(8,128)S(1)} %bitcast.12, f32[516,4,128]{2,1,0:T(4,128)S(1)} %get-tuple-element.18.table_ref), custom_call_target="tpu_custom_call" | custom-call | tf_op jit(solution)/shard_map/gather/pallas_call | solution.py:460
  25.9 0.0 copy-start
  25.9 1.0 %copy-done = f32[512,4,128]{2,1,0:T(4,128)} copy-done((f32[512,4,128]{2,1,0:T(4,128)}, f32[512,4,128]{2,1,0:T(4,128)S(1)}, u32[]{:S(2)}) %copy-start) | copy-done | bytes 1048600
  26.8 0.0 copy-start.4
  26.8 0.0 copy-start.2
  26.9 4.0 %all-to-all-start.1 = ((f32[512,4,128]{2,1,0:T(4,128)}), f32[512,4,128]{2,1,0:T(4,128)S(1)}, u32[]{:S(2)}, u32[]{:S(2)}) async-start(f32[512,4,128]{2,1,0:T(4,128)} %copy-done), calls=%async_computation.1 | async-start | bytes 2097152 | tf_op jit(solution)/shard_map/all_to_all | solution.py:399
  30.9 0.0 copy-done.4
  30.9 5.8 %collective-permute-start.1 = (f32[16,128]{1,0:T(8,128)S(1)}, f32[16,128]{1,0:T(8,128)S(1)}, u32[]{:S(2)}, u32[]{:S(2)}) collective-permute-start(f32[16,128]{1,0:T(8,128)S(1)} %bitcast.17), channel_id=1, source_target_pairs={{1,0},{2,1},{3,2},{4,3},{5,4},{6,5},{7,6},{8,7},{9,8},{10,9},{11,1... | collective-permute-start | bytes 24584 | tf_op jit(solution)/shard_map/ppermute | solution.py:405
  36.6 0.0 collective-permute-start
  36.6 0.8 collective-permute-done.1.below_ref
  37.4 5.8 %collective-permute-done.above_ref = f32[16,128]{1,0:T(8,128)S(1)} collective-permute-done((f32[16,128]{1,0:T(8,128)S(1)}, f32[16,128]{1,0:T(8,128)S(1)}, u32[]{:S(2)}, u32[]{:S(2)}) %collective-permute-start) | collective-permute-done | bytes 8224 | tf_op jit(solution)/shard_map/ppermute | solution.py:404
  43.2 0.4 smooth.1.load_ref
  43.5 6.4 %all-to-all-done.1.arrived_ref = f32[512,4,128]{2,1,0:T(4,128)S(1)} async-done(((f32[512,4,128]{2,1,0:T(4,128)}), f32[512,4,128]{2,1,0:T(4,128)S(1)}, u32[]{:S(2)}, u32[]{:S(2)}) %all-to-all-start.1) | async-done | bytes 1048608 | tf_op jit(solution)/shard_map/all_to_all | solution.py:399
  49.9 0.0 copy-done.2
  49.9 0.0 copy-done.3
  49.9 7.4 %transport.1 = (f32[16,128]{1,0:T(8,128)}, f32[512,4,128]{2,1,0:T(4,128)S(1)}) custom-call(s32[16,128]{1,0:T(8,128)S(1)} %get-tuple-element.16.target_ref, f32[512,4,128]{2,1,0:T(4,128)S(1)} %all-to-all-done.1.arrived_ref, bf16[16,128,48]{2,1,0:T(8,128)(2,1)S(1)} %copy-done.2, f32[3,16,128]{2,1,0:T(8,128)S(1)} %bitcast.15, f32[16,128]{1,0:T(8,128)S(1)} %smooth.1.load_ref), custom_call_target="tpu_custom_call" | custom-call | tf_op jit(solution)/shard_map/transport/pallas_call | solution.py:484
  57.3 23.0 %all_to_all.21.back_ref = f32[512,4,128]{2,1,0:T(4,128)S(1)} all-to-all(f32[512,4,128]{2,1,0:T(4,128)S(1)} %get-tuple-element.25), channel_id=1, replica_groups=mesh['gx'=8,'gy'=16] {'gx','gy'}, dimensions={0} | all-to-all | bytes 2097152 | tf_op jit(solution)/shard_map/all_to_all | solution.py:399
  80.3 3.4 %reduce.1 = (f32[512,128]{1,0:T(8,128)}, f32[3,65536]{1,0:T(4,128)}, f32[2064,128]{1,0:T(8,128)S(1)}) custom-call(s32[8,128]{1,0:T(8,128)S(1)} %get-tuple-element.24.ids_ref, f32[512,4,128]{2,1,0:T(4,128)S(1)} %all_to_all.21.back_ref, f32[2064,128]{1,0:T(8,128)S(1)} %get-tuple-element.26.start_ref), custom_call_target="tpu_custom_call", output_to_operand_aliasing={{2}: (2, {})} | custom-call | tf_op jit(solution)/shard_map/reduce/pallas_call | solution.py:501
  (1 shorter events, 0.0 us)
Async XLA Ops:
  2.7 21.7 %all-to-all-start = ((f32[128,2,128]{2,1,0:T(2,128)}), f32[128,2,128]{2,1,0:T(2,128)S(1)}, u32[]{:S(2)}, u32[]{:S(2)}) async-start(f32[128,2,128]{2,1,0:T(2,128)} %bitcast.5), calls=%async_computation | async-start | bytes 262144 | tf_op jit(solution)/shard_map/all_to_all | solution.py:399
  16.6 0.8 copy-start.1
  25.9 1.0 %copy-start = (f32[512,4,128]{2,1,0:T(4,128)}, f32[512,4,128]{2,1,0:T(4,128)S(1)}, u32[]{:S(2)}) copy-start(f32[512,4,128]{2,1,0:T(4,128)S(1)} %get-tuple-element.20) | copy-start | bytes 3145732
  26.8 4.0 %copy-start.4 = (f32[2,8,128]{2,1,0:T(8,128)S(1)}, f32[2,8,128]{2,1,0:T(8,128)}, u32[]{:S(2)}) copy-start(f32[2,8,128]{2,1,0:T(8,128)} %param.7) | copy-start | bytes 24580
  26.8 23.1 %copy-start.2 = (bf16[16,128,48]{2,1,0:T(8,128)(2,1)S(1)}, bf16[16,128,48]{2,1,0:T(8,128)(2,1)}, u32[]{:S(2)}) copy-start(bf16[16,128,48]{2,1,0:T(8,128)(2,1)} %copy-done.1) | copy-start | bytes 589828
  26.8 23.1 %copy-start.3 = (f32[3,2,8,128]{3,2,1,0:T(8,128)S(1)}, f32[3,2,8,128]{3,2,1,0:T(8,128)}, u32[]{:S(2)}) copy-start(f32[3,2,8,128]{3,2,1,0:T(8,128)} %param.8) | copy-start | bytes 73732
  26.9 23.0 %all-to-all-start.1 = ((f32[512,4,128]{2,1,0:T(4,128)}), f32[512,4,128]{2,1,0:T(4,128)S(1)}, u32[]{:S(2)}, u32[]{:S(2)}) async-start(f32[512,4,128]{2,1,0:T(4,128)} %copy-done), calls=%async_computation.1 | async-start | bytes 2097152 | tf_op jit(solution)/shard_map/all_to_all | solution.py:399
  30.9 6.5 %collective-permute-start.1 = (f32[16,128]{1,0:T(8,128)S(1)}, f32[16,128]{1,0:T(8,128)S(1)}, u32[]{:S(2)}, u32[]{:S(2)}) collective-permute-start(f32[16,128]{1,0:T(8,128)S(1)} %bitcast.17), channel_id=1, source_target_pairs={{1,0},{2,1},{3,2},{4,3},{5,4},{6,5},{7,6},{8,7},{9,8},{10,9},{11,1... | collective-permute-start | bytes 24584 | tf_op jit(solution)/shard_map/ppermute | solution.py:405
  36.6 6.5 %collective-permute-start = (f32[16,128]{1,0:T(8,128)S(1)}, f32[16,128]{1,0:T(8,128)S(1)}, u32[]{:S(2)}, u32[]{:S(2)}) collective-permute-start(f32[16,128]{1,0:T(8,128)S(1)} %bitcast.18), channel_id=1, source_target_pairs={{0,1},{1,2},{2,3},{3,4},{4,5},{5,6},{6,7},{7,8},{8,9},{9,10},{10,1... | collective-permute-start | bytes 24584 | tf_op jit(solution)/shard_map/ppermute | solution.py:404

commit v7 on v6

--- a/solution.py
+++ b/solution.py
@@ -28,6 +28,7 @@
 ROOT = math.sqrt(KAPPA)
 DEAD = -1e30
 PIECES = 4
+BLOCKS = SB_DEV // PIECES
 F32 = jnp.float32
 BF16 = jnp.bfloat16
 I32 = jnp.int32
@@ -35,7 +36,7 @@
 HBM = pl.BlockSpec(memory_space=pltpu.HBM)
 SMEM = pl.BlockSpec(memory_space=pltpu.SMEM)
 AXES = ("gx", "gy")
-LIMIT = pltpu.CompilerParams(vmem_limit_bytes=16 << 20)
+LIMIT = pltpu.CompilerParams(vmem_limit_bytes=8 << 20)
 
 
 def gauss_values():
@@ -102,15 +103,16 @@
     hot_low = hot.astype(BF16)
     before = jnp.dot(lower, hot_low, preferred_element_type=F32)
     rank = jnp.sum(before * hot, axis=1, keepdims=True).astype(I32)
-    wide = iota((ENTRIES, 128), 1)
+    own_rank = iota((ENTRIES, 128), 1) % CAP == rank
     high_part = (value & -32).astype(F32)
     low_part = (value & 31).astype(F32)
-    spread = jnp.where(wide == rank, high_part, 0.0) + jnp.where(wide == rank + CAP, low_part, 0.0)
+    spread = jnp.concatenate(
+        [jnp.where(own_rank, high_part, 0.0), jnp.where(own_rank, low_part, 0.0)], axis=1
+    )
     request = lax.dot_general(
         hot_low, spread.astype(BF16), (((0,), (0,)), ((), ())), preferred_element_type=F32
     )
-    request = request + pltpu.roll(request, 128 - CAP, 1)
-    request_ref[pl.ds(0, OWNERS, stride=2), :] = request - 1.0
+    request_ref[pl.ds(0, OWNERS, stride=2), :] = request[:, :128] + request[:, 128:] - 1.0
     edge_shape = (TILE, 2 * TILE)
     edge_lane = iota(edge_shape, 1)
     column = jnp.where(edge_lane < TILE, 0, TILE - HALF) + edge_lane % HALF
@@ -153,54 +155,53 @@
     lax.fori_loop(0, TILES, tile, 0, unroll=4)
 
 
-def table_kernel(
-    position_hbm,
-    weight_hbm,
-    point_hbm,
-    table_ref,
-    start_ref,
-    lhs_ref,
-    position_ref,
-    weight_ref,
-    point_ref,
-    sems,
-):
-    points = pltpu.make_async_copy(point_hbm, point_ref, sems.at[PIECES + 1])
-    points.start()
-    copies = [pltpu.make_async_copy(weight_hbm, weight_ref, sems.at[PIECES])]
+def piece_copies(source, target, sems):
     width = SB_DEV * SITE_BLOCK // PIECES
+    copies = []
     for piece in range(PIECES):
         part = pl.ds(piece * width, width)
         copies.append(
-            pltpu.make_async_copy(
-                position_hbm.at[:, part], position_ref.at[:, part], sems.at[piece]
-            )
+            pltpu.make_async_copy(source.at[:, part], target.at[:, part], sems.at[piece])
         )
+    return copies
+
+
+def table_kernel(position_hbm, weight_hbm, table_ref, position_ref, weight_ref, sems):
+    weights = pltpu.make_async_copy(weight_hbm, weight_ref, sems.at[PIECES])
+    copies = piece_copies(position_hbm, position_ref, sems)
+    weights.start()
     for copy in copies:
         copy.start()
-    row = iota((4, 128), 0)
-    dead = jnp.where(row == 3, DEAD, 0.0)
+    dead = jnp.where(iota((4, 128), 0) == 3, DEAD, 0.0)
     for r in range(CAP):
-        table_ref[SB_DEV + r] = dead
+        table_ref[(SB_DEV + r) * 4 : (SB_DEV + r + 1) * 4, :] = dead
+    weights.wait()
+    for piece in range(PIECES):
+        copies[piece].wait()
+        for b in range(piece * BLOCKS, (piece + 1) * BLOCKS):
+            place = position_ref[:, b * SITE_BLOCK : (b + 1) * SITE_BLOCK]
+            table_ref[4 * b : 4 * b + 3, :] = (place - 0.5) * ROOT
+            table_ref[4 * b + 3 : 4 * b + 4, :] = weight_ref[b : b + 1, :]
+
+
+def setup_kernel(position_hbm, point_ref, start_ref, lhs_ref, position_ref, sems):
+    copies = piece_copies(position_hbm, position_ref, sems)
+    for copy in copies:
+        copy.start()
+    prepare(point_ref, lhs_ref)
+    for r in range(CAP):
         start_ref[(SB_DEV + r) * 4 : (SB_DEV + r + 1) * 4, :] = jnp.zeros((4, 128), F32)
 
     def block(b, carry):
         start = pl.multiple_of(b * SITE_BLOCK, SITE_BLOCK)
-        place = position_ref[:, pl.ds(start, SITE_BLOCK)]
-        table_ref[b, 0:3, :] = (place - 0.5) * ROOT
-        table_ref[b, 3:4, :] = weight_ref[pl.ds(b, 1), :]
         line = pl.multiple_of(b * 4, 4)
-        start_ref[pl.ds(line, 3), :] = PRIOR_MASS * place
+        start_ref[pl.ds(line, 3), :] = PRIOR_MASS * position_ref[:, pl.ds(start, SITE_BLOCK)]
         start_ref[pl.ds(line + 3, 1), :] = jnp.zeros((1, 128), F32)
         return carry
 
-    points.wait()
-    prepare(point_ref, lhs_ref)
-    copies[0].wait()
-    blocks = SB_DEV // PIECES
     for piece in range(PIECES):
-        copies[piece + 1].wait()
-        lax.fori_loop(piece * blocks, (piece + 1) * blocks, block, 0, unroll=8)
+        copies[piece].wait()
+        lax.fori_loop(piece * BLOCKS, (piece + 1) * BLOCKS, block, 0, unroll=8)
 
 
 def smooth_kernel(halo_ref, above_ref, mid_ref, below_ref, load_ref, rows_ref):
@@ -247,26 +248,32 @@
     load_ref[CY : 2 * CY, :] = GAUSS[HALF - 1] * planes[0] + GAUSS[HALF] * planes[1]
 
 
-def gather_kernel(
-    asked_ref,
-    table_ref,
-    out_ref,
-    ids_ref,
-    ids_smem,
-    sem,
-):
-    asked = jnp.transpose(asked_ref[pl.ds(0, OWNERS, stride=2), :])[0:8].astype(I32)
-    ids_ref[...] = jnp.where(asked < 0, SB_DEV + iota((8, 128), 0) % CAP, asked)
+def gather_kernel(asked_ref, table_ref, out_hbm, ids_ref, out_ref, ids_smem, sem, out_sems):
+    shape = (OWNERS, 128)
+    asked = asked_ref[pl.ds(0, OWNERS, stride=2), :]
+    lane = iota(shape, 1)
+    place = jnp.where(asked < 0.0, (SB_DEV + lane % CAP).astype(F32), asked) * 4.0
+    own = iota(shape, 0) % (128 // CAP) == lane // CAP
+    place = jnp.where(own, place, 0.0)
+    rows = [
+        jnp.sum(place[g * 32 : (g + 1) * 32], axis=0, keepdims=True) for g in range(PIECES)
+    ]
+    ids_ref[...] = jnp.concatenate(rows + rows, axis=0).astype(I32)
     copy = pltpu.make_async_copy(ids_ref, ids_smem, sem)
     copy.start()
     copy.wait()
-
-    def peer(step, carry):
-        for r in range(CAP):
-            out_ref[step * CAP + r] = table_ref[ids_smem[r, step]]
-        return carry
-
-    lax.fori_loop(0, OWNERS, peer, 0, unroll=8)
+    copies = []
+    for piece in range(PIECES):
+        for c in range(BLOCKS):
+            line = pl.multiple_of(ids_smem[piece, c], 4)
+            out_ref[piece * BLOCKS + c] = table_ref[pl.ds(line, 4), :]
+        part = pl.ds(piece * BLOCKS, BLOCKS)
+        copies.append(
+            pltpu.make_async_copy(out_ref.at[part], out_hbm.at[part], out_sems.at[piece])
+        )
+        copies[piece].start()
+    for copy in copies:
+        copy.wait()
 
 
 def transport_kernel(
@@ -359,32 +366,46 @@
     potential_ref[...] = jnp.log(sum_ref[...]) + (top_ref[...] - square) / EPSILON
 
 
-def reduce_kernel(ids_ref, back_ref, start_ref, mass_ref, centre_ref, acc_ref, scale_ref):
-    def peer(step, carry):
-        places = []
-        sums = []
-        for r in range(CAP):
-            place = pl.ds(pl.multiple_of(ids_ref[r, step] * 4, 4), 4)
-            places.append(place)
-            sums.append(acc_ref[place, :] + back_ref[step * CAP + r])
-        for place, total in zip(places, sums):
-            acc_ref[place, :] = total
-        return carry
-
-    lax.fori_loop(0, OWNERS, peer, 0, unroll=4)
-    mass = acc_ref[pl.ds(3, SB_DEV, stride=4), :]
-    mass_ref[...] = mass
-    scale_ref[...] = 1.0 / (mass + PRIOR_MASS)
-
-    def finish(b, carry):
-        start = pl.multiple_of(b * SITE_BLOCK, SITE_BLOCK)
-        line = pl.multiple_of(b * 4, 4)
-        centre_ref[:, pl.ds(start, SITE_BLOCK)] = (
-            acc_ref[pl.ds(line, 3), :] * scale_ref[pl.ds(b, 1), :]
+def reduce_kernel(
+    ids_ref, back_ref, start_ref, mass_hbm, centre_hbm, acc_ref, mass_ref, scale_ref, centre_ref, sems
+):
+    for piece in range(PIECES):
+        for peer in range(BLOCKS // CAP):
+            places = []
+            sums = []
+            for r in range(CAP):
+                c = peer * CAP + r
+                place = pl.ds(pl.multiple_of(ids_ref[piece, c], 4), 4)
+                places.append(place)
+                sums.append(acc_ref[place, :] + back_ref[piece * BLOCKS + c])
+            for place, total in zip(places, sums):
+                acc_ref[place, :] = total
+    copies = []
+    width = BLOCKS * SITE_BLOCK
+    for piece in range(PIECES):
+        part = pl.ds(piece * BLOCKS, BLOCKS)
+        mass = acc_ref[pl.ds(piece * BLOCKS * 4 + 3, BLOCKS, stride=4), :]
+        mass_ref[part, :] = mass
+        copies.append(
+            pltpu.make_async_copy(
+                mass_ref.at[part], mass_hbm.at[part], sems.at[PIECES + piece]
+            )
         )
-        return carry
-
-    lax.fori_loop(0, SB_DEV, finish, 0, unroll=16)
+        copies[-1].start()
+        scale_ref[part, :] = 1.0 / (mass + PRIOR_MASS)
+        for b in range(piece * BLOCKS, (piece + 1) * BLOCKS):
+            centre_ref[:, b * SITE_BLOCK : (b + 1) * SITE_BLOCK] = (
+                acc_ref[4 * b : 4 * b + 3, :] * scale_ref[b : b + 1, :]
+            )
+        part = pl.ds(piece * width, width)
+        copies.append(
+            pltpu.make_async_copy(
+                centre_ref.at[:, part], centre_hbm.at[:, part], sems.at[piece]
+            )
+        )
+        copies[-1].start()
+    for copy in copies:
+        copy.wait()
 
 
 def shape_of(*dims, dtype=F32):
@@ -435,43 +456,53 @@
         in_hbm(cells),
     )
     asked = exchange(request)
-    table, start, lhs = pl.pallas_call(
+    table = pl.pallas_call(
         table_kernel,
+        out_shape=shape_of((SB_DEV + CAP) * 4, SITE_BLOCK),
+        in_specs=[HBM] * 2,
+        out_specs=VMEM,
+        scratch_shapes=[
+            pltpu.VMEM((3, SB_DEV * SITE_BLOCK), F32),
+            pltpu.VMEM((SB_DEV, SITE_BLOCK), F32),
+            pltpu.SemaphoreType.DMA((PIECES + 1,)),
+        ],
+        compiler_params=LIMIT,
+        name="table",
+    )(in_hbm(site_position), in_hbm(site_weight.reshape(SB_DEV, SITE_BLOCK)))
+    blocks, ids = pl.pallas_call(
+        gather_kernel,
+        out_shape=(shape_of(SLOTS, 4, SITE_BLOCK), shape_of(8, 128, dtype=I32)),
+        in_specs=[VMEM] * 2,
+        out_specs=(HBM, VMEM),
+        compiler_params=LIMIT,
+        scratch_shapes=[
+            pltpu.VMEM((SLOTS, 4, SITE_BLOCK), F32),
+            pltpu.SMEM((8, 128), I32),
+            pltpu.SemaphoreType.DMA,
+            pltpu.SemaphoreType.DMA((PIECES,)),
+        ],
+        name="gather",
+    )(asked, table)
+    cells, points, site_position, blocks = lax.optimization_barrier(
+        (cells, points, site_position, blocks)
+    )
+    arrived = exchange(blocks)
+    above, below = neighbours(cells, "gy")
+    start, lhs = pl.pallas_call(
+        setup_kernel,
         out_shape=(
-            shape_of(SB_DEV + CAP, 4, SITE_BLOCK),
             shape_of((SB_DEV + CAP) * 4, SITE_BLOCK),
             shape_of(TILES, TILE, 48, dtype=BF16),
         ),
-        in_specs=[HBM] * 3,
-        out_specs=(VMEM,) * 3,
+        in_specs=[HBM, VMEM],
+        out_specs=(VMEM, VMEM),
         scratch_shapes=[
             pltpu.VMEM((3, SB_DEV * SITE_BLOCK), F32),
-            pltpu.VMEM((SB_DEV, SITE_BLOCK), F32),
-            pltpu.VMEM((3, TILES, TILE), F32),
-            pltpu.SemaphoreType.DMA((PIECES + 2,)),
-        ],
-        compiler_params=LIMIT,
-        name="table",
-    )(
-        in_hbm(site_position),
-        in_hbm(site_weight.reshape(SB_DEV, SITE_BLOCK)),
-        in_hbm(points),
-    )
-    blocks, ids = pl.pallas_call(
-        gather_kernel,
-        out_shape=(
-            shape_of(SLOTS, 4, SITE_BLOCK),
-            shape_of(8, 128, dtype=I32),
-        ),
-        in_specs=[VMEM] * 2,
-        out_specs=(VMEM, VMEM),
-        compiler_params=LIMIT,
-        scratch_shapes=[pltpu.SMEM((8, 128), I32), pltpu.SemaphoreType.DMA],
-        name="gather",
-    )(asked, table)
-    cells, blocks = lax.optimization_barrier((cells, blocks))
-    arrived = exchange(blocks)
-    above, below = neighbours(cells, "gy")
+            pltpu.SemaphoreType.DMA((PIECES,)),
+        ],
+        compiler_params=LIMIT,
+        name="setup",
+    )(in_hbm(site_position), points)
     load = pl.pallas_call(
         smooth_kernel,
         out_shape=shape_of(TILES, TILE),
@@ -506,8 +537,13 @@
             shape_of((SB_DEV + CAP) * 4, SITE_BLOCK),
         ),
         in_specs=[SMEM] + [VMEM] * 2,
-        out_specs=(VMEM, VMEM, VMEM),
-        scratch_shapes=[pltpu.VMEM((SB_DEV, SITE_BLOCK), F32)],
+        out_specs=(HBM, HBM, VMEM),
+        scratch_shapes=[
+            pltpu.VMEM((SB_DEV, SITE_BLOCK), F32),
+            pltpu.VMEM((SB_DEV, SITE_BLOCK), F32),
+            pltpu.VMEM((3, SB_DEV * SITE_BLOCK), F32),
+            pltpu.SemaphoreType.DMA((2 * PIECES,)),
+        ],
         input_output_aliases={2: 2},
         compiler_params=LIMIT,
         name="reduce",

time: 84.1 us -> 82.5 us (0.981)
  local copies, waits for them, and re-layouts: 1.76 us -> 0.01 us
    unnamed x10 -> x4, local copies, waits for them, and re-layouts: 1.76 us -> 0.01 us
    all_to_all x2, waiting for transfers between devices: 13.4 us -> 15 us  [exchange(): return lax.all_to_all(values, AXES, split_axis=0, concat_axis=0, tiled=True)]
    ppermute x1, waiting for transfers between devices: 5.75 us -> 4.63 us  [neighbours(): lax.ppermute(values, axis, [(i, (i + 1) % count) for i in range(count)])]
    pallas_call x1 -> x2, Pallas kernels: 2.39 us -> 3.48 us  [the longest x1 1.89 us: local(): pl.pallas_call(setup_kernel, out_shape=(shape_of((SB_DEV + CAP) * 4, SITE...]
  transfers between devices with their start and end apart: 4 -> 4, of which waited for: 4 -> 3; matrix products, arithmetic and copies ran while one was open for 0% -> 0% of each run, Pallas kernels for 3% -> 5%
where the time goes in v7:
time: 82.5 us; the launch traced here: 82.1 us
  blocking collectives  23 us (28%)
  starting transfers between devices  21.1 us (26%)
  waiting for transfers between devices  19.6 us (24%)
  Pallas kernels  17.6 us (21%)
    all_to_all x1, blocking collectives, exchange(): return lax.all_to_all(values, AXES, split_axis=0, concat_axis=0, tiled=True)  23 us
    all_to_all x2, starting transfers between devices, exchange(): return lax.all_to_all(values, AXES, split_axis=0, concat_axis=0, tiled=True)  15.5 us
    all_to_all x2, waiting for transfers between devices, exchange(): return lax.all_to_all(values, AXES, split_axis=0, concat_axis=0, tiled=True)  15 us
    pallas_call x1, Pallas kernels, local(): pl.pallas_call(transport_kernel, out_shape=(shape_of(TILES, TILE), shape_...  7.42 us
    ppermute x1, starting transfers between devices, neighbours(): lax.ppermute(values, axis, [((i + 1) % count, i) for i in range(count)])  5.65 us
    ppermute x1, waiting for transfers between devices, neighbours(): lax.ppermute(values, axis, [(i, (i + 1) % count) for i in range(count)])  4.63 us
    pallas_call x1, Pallas kernels, local(): pl.pallas_call(reduce_kernel, out_shape=(shape_of(SB_DEV, SITE_BLOCK), sh...  2.72 us
    pallas_call x1, Pallas kernels, local(): pl.pallas_call(request_kernel, out_shape=(shape_of(2 * OWNERS, 128), shap...  1.97 us
  transfers between devices with their start and end apart: 4, of which 3 were waited for; matrix products, arithmetic and copies ran while one was open for 0% of the time, Pallas kernels for 5%

profile of v7, /device:TPU:1, one launch (start us, length us, event | category | flops | bytes accessed | tf_op | source)
XLA Modules:
  0.0 82.1 jit_solution(11902588402160979648)
XLA Ops:
  0.6 2.0 %request.1 = (f32[256,128]{1,0:T(8,128)}, s32[16,128]{1,0:T(8,128)S(1)}) custom-call(s32[16,16]{1,0:T(8,128)} %bitcast.21, s32[16,16]{1,0:T(8,128)} %bitcast.22, s32[2,1,8]{2,1,0:T(1,128)} %bitcast.23, f32[16,128]{1,0:T(8,128)} %bitcast.16), custom_call_target="tpu_custom_call" | custom-call | tf_op jit(solution)/shard_map/request/pallas_call | solution.py:435
  2.6 11.5 %all-to-all-start = ((f32[128,2,128]{2,1,0:T(2,128)}), f32[128,2,128]{2,1,0:T(2,128)S(1)}, u32[]{:S(2)}, u32[]{:S(2)}) async-start(f32[128,2,128]{2,1,0:T(2,128)} %bitcast.6), calls=%async_computation | async-start | bytes 262144 | tf_op jit(solution)/shard_map/all_to_all | solution.py:420
  14.1 1.6 %table.1.table_ref = f32[2064,128]{1,0:T(8,128)S(1)} custom-call(f32[3,65536]{1,0:T(4,128)} %position_hbm.2, f32[512,128]{1,0:T(8,128)} %bitcast.20), custom_call_target="tpu_custom_call" | custom-call | tf_op jit(solution)/shard_map/table/pallas_call | solution.py:459
  15.7 8.6 %all-to-all-done = f32[128,2,128]{2,1,0:T(2,128)S(1)} async-done(((f32[128,2,128]{2,1,0:T(2,128)}), f32[128,2,128]{2,1,0:T(2,128)S(1)}, u32[]{:S(2)}, u32[]{:S(2)}) %all-to-all-start) | async-done | bytes 131104 | tf_op jit(solution)/shard_map/all_to_all | solution.py:420
  24.3 1.7 %gather.1 = (f32[512,4,128]{2,1,0:T(4,128)}, s32[8,128]{1,0:T(8,128)S(1)}) custom-call(f32[256,128]{1,0:T(8,128)S(1)} %bitcast.12, f32[2064,128]{1,0:T(8,128)S(1)} %table.1.table_ref), custom_call_target="tpu_custom_call" | custom-call | tf_op jit(solution)/shard_map/gather/pallas_call | solution.py:472
  26.0 0.0 copy-start.1
  26.0 0.0 copy-start
  26.0 4.0 %all-to-all-start.1 = ((f32[512,4,128]{2,1,0:T(4,128)}), f32[512,4,128]{2,1,0:T(4,128)S(1)}, u32[]{:S(2)}, u32[]{:S(2)}) async-start(f32[512,4,128]{2,1,0:T(4,128)} %get-tuple-element.20), calls=%async_computation.1 | async-start | bytes 2097152 | tf_op jit(solution)/shard_map/all_to_all | solution.py:420
  30.0 0.0 copy-done.1
  30.1 5.7 %collective-permute-start.1 = (f32[16,128]{1,0:T(8,128)S(1)}, f32[16,128]{1,0:T(8,128)S(1)}, u32[]{:S(2)}, u32[]{:S(2)}) collective-permute-start(f32[16,128]{1,0:T(8,128)S(1)} %bitcast.17), channel_id=1, source_target_pairs={{1,0},{2,1},{3,2},{4,3},{5,4},{6,5},{7,6},{8,7},{9,8},{10,9},{11,1... | collective-permute-start | bytes 24584 | tf_op jit(solution)/shard_map/ppermute | solution.py:426
  35.7 0.0 collective-permute-start
  35.7 0.0 copy-done
  35.7 1.9 %setup.1 = (f32[2064,128]{1,0:T(8,128)S(1)}, bf16[16,128,48]{2,1,0:T(8,128)(2,1)S(1)}) custom-call(f32[3,65536]{1,0:T(4,128)} %position_hbm.2, f32[3,16,128]{2,1,0:T(8,128)S(1)} %bitcast.14), custom_call_target="tpu_custom_call" | custom-call | tf_op jit(solution)/shard_map/setup/pallas_call | solution.py:491
  37.6 0.0 collective-permute-done.1.below_ref
  37.6 4.6 %collective-permute-done.above_ref = f32[16,128]{1,0:T(8,128)S(1)} collective-permute-done((f32[16,128]{1,0:T(8,128)S(1)}, f32[16,128]{1,0:T(8,128)S(1)}, u32[]{:S(2)}, u32[]{:S(2)}) %collective-permute-start) | collective-permute-done | bytes 8224 | tf_op jit(solution)/shard_map/ppermute | solution.py:425
  42.2 0.4 smooth.1.load_ref
  42.6 6.4 %all-to-all-done.1.arrived_ref = f32[512,4,128]{2,1,0:T(4,128)S(1)} async-done(((f32[512,4,128]{2,1,0:T(4,128)}), f32[512,4,128]{2,1,0:T(4,128)S(1)}, u32[]{:S(2)}, u32[]{:S(2)}) %all-to-all-start.1) | async-done | bytes 1048608 | tf_op jit(solution)/shard_map/all_to_all | solution.py:420
  49.0 7.4 %transport.1 = (f32[16,128]{1,0:T(8,128)}, f32[512,4,128]{2,1,0:T(4,128)S(1)}) custom-call(s32[16,128]{1,0:T(8,128)S(1)} %get-tuple-element.17.target_ref, f32[512,4,128]{2,1,0:T(4,128)S(1)} %all-to-all-done.1.arrived_ref, bf16[16,128,48]{2,1,0:T(8,128)(2,1)S(1)} %get-tuple-element.23.lhs_ref, f32[3,16,128]{2,1,0:T(8,128)S(1)} %bitcast.15, ...), custom_call_target="tpu_custom_call" | custom-call | tf_op jit(solution)/shard_map/transport/pallas_call | solution.py:515
  56.4 23.0 %all_to_all.21.back_ref = f32[512,4,128]{2,1,0:T(4,128)S(1)} all-to-all(f32[512,4,128]{2,1,0:T(4,128)S(1)} %get-tuple-element.27), channel_id=1, replica_groups=mesh['gx'=8,'gy'=16] {'gx','gy'}, dimensions={0} | all-to-all | bytes 2097152 | tf_op jit(solution)/shard_map/all_to_all | solution.py:420
  79.4 2.7 %reduce.1 = (f32[512,128]{1,0:T(8,128)}, f32[3,65536]{1,0:T(4,128)}, f32[2064,128]{1,0:T(8,128)S(1)}) custom-call(s32[8,128]{1,0:T(8,128)S(1)} %get-tuple-element.26.ids_ref, f32[512,4,128]{2,1,0:T(4,128)S(1)} %all_to_all.21.back_ref, f32[2064,128]{1,0:T(8,128)S(1)} %get-tuple-element.28.start_ref), custom_call_target="tpu_custom_call", output_to_operand_aliasing={{2}: (2, {})} | custom-call | tf_op jit(solution)/shard_map/reduce/pallas_call | solution.py:532
Async XLA Ops:
  2.6 21.7 %all-to-all-start = ((f32[128,2,128]{2,1,0:T(2,128)}), f32[128,2,128]{2,1,0:T(2,128)S(1)}, u32[]{:S(2)}, u32[]{:S(2)}) async-start(f32[128,2,128]{2,1,0:T(2,128)} %bitcast.6), calls=%async_computation | async-start | bytes 262144 | tf_op jit(solution)/shard_map/all_to_all | solution.py:420
  26.0 4.0 %copy-start.1 = (f32[2,8,128]{2,1,0:T(8,128)S(1)}, f32[2,8,128]{2,1,0:T(8,128)}, u32[]{:S(2)}) copy-start(f32[2,8,128]{2,1,0:T(8,128)} %param.7) | copy-start | bytes 24580
  26.0 9.7 %copy-start = (f32[3,2,8,128]{3,2,1,0:T(8,128)S(1)}, f32[3,2,8,128]{3,2,1,0:T(8,128)}, u32[]{:S(2)}) copy-start(f32[3,2,8,128]{3,2,1,0:T(8,128)} %param.8) | copy-start | bytes 73732
  26.0 22.9 %all-to-all-start.1 = ((f32[512,4,128]{2,1,0:T(4,128)}), f32[512,4,128]{2,1,0:T(4,128)S(1)}, u32[]{:S(2)}, u32[]{:S(2)}) async-start(f32[512,4,128]{2,1,0:T(4,128)} %get-tuple-element.20), calls=%async_computation.1 | async-start | bytes 2097152 | tf_op jit(solution)/shard_map/all_to_all | solution.py:420
  30.1 7.6 %collective-permute-start.1 = (f32[16,128]{1,0:T(8,128)S(1)}, f32[16,128]{1,0:T(8,128)S(1)}, u32[]{:S(2)}, u32[]{:S(2)}) collective-permute-start(f32[16,128]{1,0:T(8,128)S(1)} %bitcast.17), channel_id=1, source_target_pairs={{1,0},{2,1},{3,2},{4,3},{5,4},{6,5},{7,6},{8,7},{9,8},{10,9},{11,1... | collective-permute-start | bytes 24584 | tf_op jit(solution)/shard_map/ppermute | solution.py:426
  35.7 6.5 %collective-permute-start = (f32[16,128]{1,0:T(8,128)S(1)}, f32[16,128]{1,0:T(8,128)S(1)}, u32[]{:S(2)}, u32[]{:S(2)}) collective-permute-start(f32[16,128]{1,0:T(8,128)S(1)} %bitcast.18), channel_id=1, source_target_pairs={{0,1},{1,2},{2,3},{3,4},{4,5},{5,6},{6,7},{7,8},{8,9},{9,10},{10,1... | collective-permute-start | bytes 24584 | tf_op jit(solution)/shard_map/ppermute | solution.py:425

commit v8 on v7

--- a/solution.py
+++ b/solution.py
@@ -78,14 +78,16 @@
     ]
     for copy in copies:
         copy.start()
-    lane = iota((TILES, 128), 1)
     corner = iota((CY, CY), 0) == iota((CY, CY), 1)
     square = (ENTRIES, ENTRIES)
-    lower = (iota(square, 1) < iota(square, 0)).astype(F32).astype(BF16)
+    upper = (iota(square, 0) < iota(square, 1)).astype(F32).astype(BF16)
+    pick = (iota((CAND, ENTRIES), 0) == iota((CAND, ENTRIES), 1) % CAND).astype(F32).astype(BF16)
+    own_tile = iota((TILES, ENTRIES), 0) == iota((TILES, ENTRIES), 1) // CAND
+    fold = (iota((ENTRIES, 128), 0) % CAND == iota((ENTRIES, 128), 1)).astype(F32)
+    fold = jnp.concatenate([fold * CAP, fold], axis=0).astype(BF16)
+    repeat = (iota((2 * CAP, 128), 0) % CAP == iota((2 * CAP, 128), 1) % CAP).astype(F32)
     for copy in copies:
         copy.wait()
-    owners = owner_ref[...]
-    slots = slot_ref[...]
     counts = jnp.concatenate(
         [
             jnp.sum(jnp.where(corner, count_ref[z], 0), axis=1, keepdims=True)
@@ -93,26 +95,32 @@
         ],
         axis=0,
     )
-    hots = []
-    values = []
-    for k in range(CAND):
-        hots.append((owners[:, k : k + 1] == lane).astype(F32))
-        values.append(jnp.where(k < counts, slots[:, k : k + 1] + 1, 0))
-    hot = jnp.concatenate(hots, axis=0)
-    value = jnp.concatenate(values, axis=0)
+    value = jnp.where(iota((TILES, CAND), 1) < counts, slot_ref[...] + 1, 0)
+    parts = jnp.concatenate([owner_ref[...], value & -32, value & 31], axis=0)
+    parts = jnp.dot(parts.astype(F32).astype(BF16), pick, preferred_element_type=F32)
+    owner, high_part, low_part = [
+        jnp.sum(
+            jnp.where(own_tile, parts[g * TILES : (g + 1) * TILES], 0.0), axis=0, keepdims=True
+        )
+        for g in range(3)
+    ]
+    hot = (iota((OWNERS, ENTRIES), 0).astype(F32) == owner).astype(F32)
     hot_low = hot.astype(BF16)
-    before = jnp.dot(lower, hot_low, preferred_element_type=F32)
-    rank = jnp.sum(before * hot, axis=1, keepdims=True).astype(I32)
-    own_rank = iota((ENTRIES, 128), 1) % CAP == rank
-    high_part = (value & -32).astype(F32)
-    low_part = (value & 31).astype(F32)
-    spread = jnp.concatenate(
-        [jnp.where(own_rank, high_part, 0.0), jnp.where(own_rank, low_part, 0.0)], axis=1
-    )
+    before = jnp.dot(hot_low, upper, preferred_element_type=F32)
+    rank = jnp.sum(before * hot, axis=0, keepdims=True)
+    shape = (2 * CAP, ENTRIES)
+    own_rank = (iota(shape, 0) % CAP).astype(F32) == rank
+    spread = jnp.where(own_rank, jnp.where(iota(shape, 0) < CAP, high_part, low_part), 0.0)
     request = lax.dot_general(
-        hot_low, spread.astype(BF16), (((0,), (0,)), ((), ())), preferred_element_type=F32
-    )
-    request_ref[pl.ds(0, OWNERS, stride=2), :] = request[:, :128] + request[:, 128:] - 1.0
+        hot_low, spread.astype(BF16), (((1,), (1,)), ((), ())), preferred_element_type=F32
+    )
+    request = jnp.dot(request.astype(BF16), repeat.astype(BF16), preferred_element_type=F32)
+    request_ref[pl.ds(0, OWNERS, stride=2), :] = request - 1.0
+    place = jnp.concatenate(
+        [jnp.where(own_tile, owner, 0.0), jnp.where(own_tile, rank, 0.0)], axis=1
+    )
+    place = jnp.dot(place.astype(BF16), fold, preferred_element_type=F32)
+    target_ref[...] = place.astype(I32)
     edge_shape = (TILE, 2 * TILE)
     edge_lane = iota(edge_shape, 1)
     column = jnp.where(edge_lane < TILE, 0, TILE - HALF) + edge_lane % HALF
@@ -129,11 +137,6 @@
     request_ref[pl.ds(1, OWNERS, stride=2), :] = jnp.where(
         to_after, edges[:, TILE:], edges[:, :TILE]
     )
-    target = jnp.where(lane == CAND, counts, 0)
-    for k in range(CAND):
-        place = owners[:, k : k + 1] * CAP + rank[k * TILES : (k + 1) * TILES]
-        target = jnp.where(lane == k, place, target)
-    target_ref[...] = target
 
 
 def prepare(point_ref, lhs_ref):
@@ -148,7 +151,7 @@
         a2 = rounded(rest)
         a3 = rest - a2
         lead = jnp.where(row == 7, 1.0, jnp.where(row >= 4, -1.0, a1))
-        lhs = jnp.concatenate([lead, lead, lead, a2, a2, a3], axis=0)
+        lhs = jnp.concatenate([lead, a2, lead, a2, lead, a3], axis=0)
         lhs_ref[t] = jnp.transpose(lhs).astype(BF16)
         return carry
 
@@ -310,11 +313,14 @@
             block = arrived_ref[target_ref[t, k]]
             both = jnp.concatenate([block, block], axis=0) - centre
             terms = both * jnp.where(fixed, factor, both)
-            t1 = rounded(terms)
-            rest = terms - t1
-            t2 = rounded(rest)
-            t3 = rest - t2
-            return jnp.concatenate([t1, t2, t3, t1, t2, t1], axis=0).astype(BF16)
+            t1 = jnp.concatenate([terms, terms], axis=0).astype(BF16)
+            first = t1.astype(F32)[:8]
+            rest = terms - first
+            t2 = jnp.concatenate([rest, rest], axis=0).astype(BF16)
+            t3 = rest - t2.astype(F32)[:8]
+            return jnp.concatenate(
+                [t1, t2, jnp.concatenate([t3, first], axis=0).astype(BF16)], axis=0
+            )
 
         total = None
         for q in range(CAND // 2):
@@ -367,24 +373,37 @@
 
 
 def reduce_kernel(
-    ids_ref, back_ref, start_ref, mass_hbm, centre_hbm, acc_ref, mass_ref, scale_ref, centre_ref, sems
+    ids_ref,
+    back_ref,
+    start_ref,
+    mass_hbm,
+    centre_hbm,
+    acc_ref,
+    other_ref,
+    mass_ref,
+    scale_ref,
+    centre_ref,
+    sems,
 ):
+    other_ref[...] = jnp.zeros_like(other_ref)
     for piece in range(PIECES):
         for peer in range(BLOCKS // CAP):
+            into = (acc_ref, other_ref)[peer % 2]
             places = []
             sums = []
             for r in range(CAP):
                 c = peer * CAP + r
                 place = pl.ds(pl.multiple_of(ids_ref[piece, c], 4), 4)
                 places.append(place)
-                sums.append(acc_ref[place, :] + back_ref[piece * BLOCKS + c])
+                sums.append(into[place, :] + back_ref[piece * BLOCKS + c])
             for place, total in zip(places, sums):
-                acc_ref[place, :] = total
+                into[place, :] = total
     copies = []
     width = BLOCKS * SITE_BLOCK
     for piece in range(PIECES):
         part = pl.ds(piece * BLOCKS, BLOCKS)
-        mass = acc_ref[pl.ds(piece * BLOCKS * 4 + 3, BLOCKS, stride=4), :]
+        lines = pl.ds(piece * BLOCKS * 4 + 3, BLOCKS, stride=4)
+        mass = acc_ref[lines, :] + other_ref[lines, :]
         mass_ref[part, :] = mass
         copies.append(
             pltpu.make_async_copy(
@@ -395,8 +414,8 @@
         scale_ref[part, :] = 1.0 / (mass + PRIOR_MASS)
         for b in range(piece * BLOCKS, (piece + 1) * BLOCKS):
             centre_ref[:, b * SITE_BLOCK : (b + 1) * SITE_BLOCK] = (
-                acc_ref[4 * b : 4 * b + 3, :] * scale_ref[b : b + 1, :]
-            )
+                acc_ref[4 * b : 4 * b + 3, :] + other_ref[4 * b : 4 * b + 3, :]
+            ) * scale_ref[b : b + 1, :]
         part = pl.ds(piece * width, width)
         copies.append(
             pltpu.make_async_copy(
@@ -539,6 +558,7 @@
         in_specs=[SMEM] + [VMEM] * 2,
         out_specs=(HBM, HBM, VMEM),
         scratch_shapes=[
+            pltpu.VMEM(((SB_DEV + CAP) * 4, SITE_BLOCK), F32),
             pltpu.VMEM((SB_DEV, SITE_BLOCK), F32),
             pltpu.VMEM((SB_DEV, SITE_BLOCK), F32),
             pltpu.VMEM((3, SB_DEV * SITE_BLOCK), F32),

time: 82.5 us -> 82.2 us (level)
  no operation moved by 1% of the time
where the time goes in v8:
time: 82.2 us; the launch traced here: 81.9 us
  blocking collectives  23 us (28%)
  starting transfers between devices  21.1 us (26%)
  waiting for transfers between devices  19.6 us (24%)
  Pallas kernels  17.4 us (21%)
    all_to_all x1, blocking collectives, exchange(): return lax.all_to_all(values, AXES, split_axis=0, concat_axis=0, tiled=True)  23 us
    all_to_all x2, starting transfers between devices, exchange(): return lax.all_to_all(values, AXES, split_axis=0, concat_axis=0, tiled=True)  15.5 us
    all_to_all x2, waiting for transfers between devices, exchange(): return lax.all_to_all(values, AXES, split_axis=0, concat_axis=0, tiled=True)  15 us
    pallas_call x1, Pallas kernels, local(): pl.pallas_call(transport_kernel, out_shape=(shape_of(TILES, TILE), shape_...  7.41 us
    ppermute x1, starting transfers between devices, neighbours(): lax.ppermute(values, axis, [((i + 1) % count, i) for i in range(count)])  5.65 us
    ppermute x1, waiting for transfers between devices, neighbours(): lax.ppermute(values, axis, [(i, (i + 1) % count) for i in range(count)])  4.63 us
    pallas_call x1, Pallas kernels, local(): pl.pallas_call(reduce_kernel, out_shape=(shape_of(SB_DEV, SITE_BLOCK), sh...  2.39 us
    pallas_call x1, Pallas kernels, local(): pl.pallas_call(request_kernel, out_shape=(shape_of(2 * OWNERS, 128), shap...  2.1 us
  transfers between devices with their start and end apart: 4, of which 3 were waited for; matrix products, arithmetic and copies ran while one was open for 0% of the time, Pallas kernels for 5%

profile of v8, /device:TPU:1, one launch (start us, length us, event | category | flops | bytes accessed | tf_op | source)
XLA Modules:
  0.0 81.9 jit_solution(2830232095793630478)
XLA Ops:
  0.6 2.1 %request.1 = (f32[256,128]{1,0:T(8,128)}, s32[16,128]{1,0:T(8,128)S(1)}) custom-call(s32[16,16]{1,0:T(8,128)} %bitcast.21, s32[16,16]{1,0:T(8,128)} %bitcast.22, s32[2,1,8]{2,1,0:T(1,128)} %bitcast.23, f32[16,128]{1,0:T(8,128)} %bitcast.16), custom_call_target="tpu_custom_call" | custom-call | tf_op jit(solution)/shard_map/request/pallas_call | solution.py:454
  2.7 11.5 %all-to-all-start = ((f32[128,2,128]{2,1,0:T(2,128)}), f32[128,2,128]{2,1,0:T(2,128)S(1)}, u32[]{:S(2)}, u32[]{:S(2)}) async-start(f32[128,2,128]{2,1,0:T(2,128)} %bitcast.6), calls=%async_computation | async-start | bytes 262144 | tf_op jit(solution)/shard_map/all_to_all | solution.py:439
  14.2 1.6 %table.1.table_ref = f32[2064,128]{1,0:T(8,128)S(1)} custom-call(f32[3,65536]{1,0:T(4,128)} %position_hbm.2, f32[512,128]{1,0:T(8,128)} %bitcast.20), custom_call_target="tpu_custom_call" | custom-call | tf_op jit(solution)/shard_map/table/pallas_call | solution.py:478
  15.8 8.6 %all-to-all-done = f32[128,2,128]{2,1,0:T(2,128)S(1)} async-done(((f32[128,2,128]{2,1,0:T(2,128)}), f32[128,2,128]{2,1,0:T(2,128)S(1)}, u32[]{:S(2)}, u32[]{:S(2)}) %all-to-all-start) | async-done | bytes 131104 | tf_op jit(solution)/shard_map/all_to_all | solution.py:439
  24.4 1.7 %gather.1 = (f32[512,4,128]{2,1,0:T(4,128)}, s32[8,128]{1,0:T(8,128)S(1)}) custom-call(f32[256,128]{1,0:T(8,128)S(1)} %bitcast.12, f32[2064,128]{1,0:T(8,128)S(1)} %table.1.table_ref), custom_call_target="tpu_custom_call" | custom-call | tf_op jit(solution)/shard_map/gather/pallas_call | solution.py:491
  26.1 0.0 copy-start.1
  26.2 0.0 copy-start
  26.2 4.0 %all-to-all-start.1 = ((f32[512,4,128]{2,1,0:T(4,128)}), f32[512,4,128]{2,1,0:T(4,128)S(1)}, u32[]{:S(2)}, u32[]{:S(2)}) async-start(f32[512,4,128]{2,1,0:T(4,128)} %get-tuple-element.20), calls=%async_computation.1 | async-start | bytes 2097152 | tf_op jit(solution)/shard_map/all_to_all | solution.py:439
  30.2 0.0 copy-done.1
  30.2 5.7 %collective-permute-start.1 = (f32[16,128]{1,0:T(8,128)S(1)}, f32[16,128]{1,0:T(8,128)S(1)}, u32[]{:S(2)}, u32[]{:S(2)}) collective-permute-start(f32[16,128]{1,0:T(8,128)S(1)} %bitcast.17), channel_id=1, source_target_pairs={{1,0},{2,1},{3,2},{4,3},{5,4},{6,5},{7,6},{8,7},{9,8},{10,9},{11,1... | collective-permute-start | bytes 24584 | tf_op jit(solution)/shard_map/ppermute | solution.py:445
  35.8 0.0 collective-permute-start
  35.8 0.0 copy-done
  35.8 1.9 %setup.1 = (f32[2064,128]{1,0:T(8,128)S(1)}, bf16[16,128,48]{2,1,0:T(8,128)(2,1)S(1)}) custom-call(f32[3,65536]{1,0:T(4,128)} %position_hbm.2, f32[3,16,128]{2,1,0:T(8,128)S(1)} %bitcast.14), custom_call_target="tpu_custom_call" | custom-call | tf_op jit(solution)/shard_map/setup/pallas_call | solution.py:510
  37.7 0.0 collective-permute-done.1.below_ref
  37.7 4.6 %collective-permute-done.above_ref = f32[16,128]{1,0:T(8,128)S(1)} collective-permute-done((f32[16,128]{1,0:T(8,128)S(1)}, f32[16,128]{1,0:T(8,128)S(1)}, u32[]{:S(2)}, u32[]{:S(2)}) %collective-permute-start) | collective-permute-done | bytes 8224 | tf_op jit(solution)/shard_map/ppermute | solution.py:444
  42.4 0.4 smooth.1.load_ref
  42.7 6.4 %all-to-all-done.1.arrived_ref = f32[512,4,128]{2,1,0:T(4,128)S(1)} async-done(((f32[512,4,128]{2,1,0:T(4,128)}), f32[512,4,128]{2,1,0:T(4,128)S(1)}, u32[]{:S(2)}, u32[]{:S(2)}) %all-to-all-start.1) | async-done | bytes 1048608 | tf_op jit(solution)/shard_map/all_to_all | solution.py:439
  49.1 7.4 %transport.1 = (f32[16,128]{1,0:T(8,128)}, f32[512,4,128]{2,1,0:T(4,128)S(1)}) custom-call(s32[16,128]{1,0:T(8,128)S(1)} %get-tuple-element.17.target_ref, f32[512,4,128]{2,1,0:T(4,128)S(1)} %all-to-all-done.1.arrived_ref, bf16[16,128,48]{2,1,0:T(8,128)(2,1)S(1)} %get-tuple-element.23.lhs_ref, f32[3,16,128]{2,1,0:T(8,128)S(1)} %bitcast.15, ...), custom_call_target="tpu_custom_call" | custom-call | tf_op jit(solution)/shard_map/transport/pallas_call | solution.py:534
  56.5 23.0 %all_to_all.21.back_ref = f32[512,4,128]{2,1,0:T(4,128)S(1)} all-to-all(f32[512,4,128]{2,1,0:T(4,128)S(1)} %get-tuple-element.27), channel_id=1, replica_groups=mesh['gx'=8,'gy'=16] {'gx','gy'}, dimensions={0} | all-to-all | bytes 2097152 | tf_op jit(solution)/shard_map/all_to_all | solution.py:439
  79.5 2.4 %reduce.1 = (f32[512,128]{1,0:T(8,128)}, f32[3,65536]{1,0:T(4,128)}, f32[2064,128]{1,0:T(8,128)S(1)}) custom-call(s32[8,128]{1,0:T(8,128)S(1)} %get-tuple-element.26.ids_ref, f32[512,4,128]{2,1,0:T(4,128)S(1)} %all_to_all.21.back_ref, f32[2064,128]{1,0:T(8,128)S(1)} %get-tuple-element.28.start_ref), custom_call_target="tpu_custom_call", output_to_operand_aliasing={{2}: (2, {})} | custom-call | tf_op jit(solution)/shard_map/reduce/pallas_call | solution.py:551
Async XLA Ops:
  2.7 21.7 %all-to-all-start = ((f32[128,2,128]{2,1,0:T(2,128)}), f32[128,2,128]{2,1,0:T(2,128)S(1)}, u32[]{:S(2)}, u32[]{:S(2)}) async-start(f32[128,2,128]{2,1,0:T(2,128)} %bitcast.6), calls=%async_computation | async-start | bytes 262144 | tf_op jit(solution)/shard_map/all_to_all | solution.py:439
  26.1 4.0 %copy-start.1 = (f32[2,8,128]{2,1,0:T(8,128)S(1)}, f32[2,8,128]{2,1,0:T(8,128)}, u32[]{:S(2)}) copy-start(f32[2,8,128]{2,1,0:T(8,128)} %param.7) | copy-start | bytes 24580
  26.2 9.7 %copy-start = (f32[3,2,8,128]{3,2,1,0:T(8,128)S(1)}, f32[3,2,8,128]{3,2,1,0:T(8,128)}, u32[]{:S(2)}) copy-start(f32[3,2,8,128]{3,2,1,0:T(8,128)} %param.8) | copy-start | bytes 73732
  26.2 22.9 %all-to-all-start.1 = ((f32[512,4,128]{2,1,0:T(4,128)}), f32[512,4,128]{2,1,0:T(4,128)S(1)}, u32[]{:S(2)}, u32[]{:S(2)}) async-start(f32[512,4,128]{2,1,0:T(4,128)} %get-tuple-element.20), calls=%async_computation.1 | async-start | bytes 2097152 | tf_op jit(solution)/shard_map/all_to_all | solution.py:439
  30.2 7.6 %collective-permute-start.1 = (f32[16,128]{1,0:T(8,128)S(1)}, f32[16,128]{1,0:T(8,128)S(1)}, u32[]{:S(2)}, u32[]{:S(2)}) collective-permute-start(f32[16,128]{1,0:T(8,128)S(1)} %bitcast.17), channel_id=1, source_target_pairs={{1,0},{2,1},{3,2},{4,3},{5,4},{6,5},{7,6},{8,7},{9,8},{10,9},{11,1... | collective-permute-start | bytes 24584 | tf_op jit(solution)/shard_map/ppermute | solution.py:445
  35.8 6.5 %collective-permute-start = (f32[16,128]{1,0:T(8,128)S(1)}, f32[16,128]{1,0:T(8,128)S(1)}, u32[]{:S(2)}, u32[]{:S(2)}) collective-permute-start(f32[16,128]{1,0:T(8,128)S(1)} %bitcast.18), channel_id=1, source_target_pairs={{0,1},{1,2},{2,3},{3,4},{4,5},{5,6},{6,7},{7,8},{8,9},{9,10},{10,1... | collective-permute-start | bytes 24584 | tf_op jit(solution)/shard_map/ppermute | solution.py:444

commit v9 on v8

--- a/solution.py
+++ b/solution.py
@@ -364,7 +364,7 @@
         moments(t, even_ref, even_load_ref)
         return carry
 
-    lax.fori_loop(0, TILES // 2, two_tiles, 0)
+    lax.fori_loop(0, TILES // 2, two_tiles, 0, unroll=8)
     moments(TILES - 1, odd_ref, odd_load_ref)
     square = (
         (point_ref[0] - 0.5) ** 2 + (point_ref[1] - 0.5) ** 2 + (point_ref[2] - 0.5) ** 2

time: 82.2 us -> 81.3 us (0.989)
  Pallas kernels: 17.4 us -> 16.5 us
    pallas_call x1, Pallas kernels: 7.41 us -> 6.49 us  [local(): pl.pallas_call(transport_kernel, out_shape=(shape_of(TILES, TILE), shape_...]
where the time goes in v9:
time: 81.3 us; the launch traced here: 81 us
  blocking collectives  23 us (28%)
  starting transfers between devices  21.1 us (26%)
  waiting for transfers between devices  19.6 us (24%)
  Pallas kernels  16.5 us (20%)
    all_to_all x1, blocking collectives, exchange(): return lax.all_to_all(values, AXES, split_axis=0, concat_axis=0, tiled=True)  23 us
    all_to_all x2, starting transfers between devices, exchange(): return lax.all_to_all(values, AXES, split_axis=0, concat_axis=0, tiled=True)  15.5 us
    all_to_all x2, waiting for transfers between devices, exchange(): return lax.all_to_all(values, AXES, split_axis=0, concat_axis=0, tiled=True)  15 us
    pallas_call x1, Pallas kernels, local(): pl.pallas_call(transport_kernel, out_shape=(shape_of(TILES, TILE), shape_...  6.49 us
    ppermute x1, starting transfers between devices, neighbours(): lax.ppermute(values, axis, [((i + 1) % count, i) for i in range(count)])  5.65 us
    ppermute x1, waiting for transfers between devices, neighbours(): lax.ppermute(values, axis, [(i, (i + 1) % count) for i in range(count)])  4.63 us
    pallas_call x1, Pallas kernels, local(): pl.pallas_call(reduce_kernel, out_shape=(shape_of(SB_DEV, SITE_BLOCK), sh...  2.39 us
    pallas_call x1, Pallas kernels, local(): pl.pallas_call(request_kernel, out_shape=(shape_of(2 * OWNERS, 128), shap...  2.1 us
  transfers between devices with their start and end apart: 4, of which 3 were waited for; matrix products, arithmetic and copies ran while one was open for 0% of the time, Pallas kernels for 5%

profile of v9, /device:TPU:1, one launch (start us, length us, event | category | flops | bytes accessed | tf_op | source)
XLA Modules:
  0.0 81.0 jit_solution(2711104912897020813)
XLA Ops:
  0.6 2.1 %request.1 = (f32[256,128]{1,0:T(8,128)}, s32[16,128]{1,0:T(8,128)S(1)}) custom-call(s32[16,16]{1,0:T(8,128)} %bitcast.21, s32[16,16]{1,0:T(8,128)} %bitcast.22, s32[2,1,8]{2,1,0:T(1,128)} %bitcast.23, f32[16,128]{1,0:T(8,128)} %bitcast.16), custom_call_target="tpu_custom_call" | custom-call | tf_op jit(solution)/shard_map/request/pallas_call | solution.py:454
  2.7 11.5 %all-to-all-start = ((f32[128,2,128]{2,1,0:T(2,128)}), f32[128,2,128]{2,1,0:T(2,128)S(1)}, u32[]{:S(2)}, u32[]{:S(2)}) async-start(f32[128,2,128]{2,1,0:T(2,128)} %bitcast.6), calls=%async_computation | async-start | bytes 262144 | tf_op jit(solution)/shard_map/all_to_all | solution.py:439
  14.2 1.6 %table.1.table_ref = f32[2064,128]{1,0:T(8,128)S(1)} custom-call(f32[3,65536]{1,0:T(4,128)} %position_hbm.2, f32[512,128]{1,0:T(8,128)} %bitcast.20), custom_call_target="tpu_custom_call" | custom-call | tf_op jit(solution)/shard_map/table/pallas_call | solution.py:478
  15.8 8.6 %all-to-all-done = f32[128,2,128]{2,1,0:T(2,128)S(1)} async-done(((f32[128,2,128]{2,1,0:T(2,128)}), f32[128,2,128]{2,1,0:T(2,128)S(1)}, u32[]{:S(2)}, u32[]{:S(2)}) %all-to-all-start) | async-done | bytes 131104 | tf_op jit(solution)/shard_map/all_to_all | solution.py:439
  24.4 1.7 %gather.1 = (f32[512,4,128]{2,1,0:T(4,128)}, s32[8,128]{1,0:T(8,128)S(1)}) custom-call(f32[256,128]{1,0:T(8,128)S(1)} %bitcast.12, f32[2064,128]{1,0:T(8,128)S(1)} %table.1.table_ref), custom_call_target="tpu_custom_call" | custom-call | tf_op jit(solution)/shard_map/gather/pallas_call | solution.py:491
  26.1 0.0 copy-start.1
  26.2 0.0 copy-start
  26.2 4.0 %all-to-all-start.1 = ((f32[512,4,128]{2,1,0:T(4,128)}), f32[512,4,128]{2,1,0:T(4,128)S(1)}, u32[]{:S(2)}, u32[]{:S(2)}) async-start(f32[512,4,128]{2,1,0:T(4,128)} %get-tuple-element.20), calls=%async_computation.1 | async-start | bytes 2097152 | tf_op jit(solution)/shard_map/all_to_all | solution.py:439
  30.2 0.0 copy-done.1
  30.2 5.7 %collective-permute-start.1 = (f32[16,128]{1,0:T(8,128)S(1)}, f32[16,128]{1,0:T(8,128)S(1)}, u32[]{:S(2)}, u32[]{:S(2)}) collective-permute-start(f32[16,128]{1,0:T(8,128)S(1)} %bitcast.17), channel_id=1, source_target_pairs={{1,0},{2,1},{3,2},{4,3},{5,4},{6,5},{7,6},{8,7},{9,8},{10,9},{11,1... | collective-permute-start | bytes 24584 | tf_op jit(solution)/shard_map/ppermute | solution.py:445
  35.8 0.0 collective-permute-start
  35.8 0.0 copy-done
  35.8 1.9 %setup.1 = (f32[2064,128]{1,0:T(8,128)S(1)}, bf16[16,128,48]{2,1,0:T(8,128)(2,1)S(1)}) custom-call(f32[3,65536]{1,0:T(4,128)} %position_hbm.2, f32[3,16,128]{2,1,0:T(8,128)S(1)} %bitcast.14), custom_call_target="tpu_custom_call" | custom-call | tf_op jit(solution)/shard_map/setup/pallas_call | solution.py:510
  37.7 0.0 collective-permute-done.1.below_ref
  37.7 4.6 %collective-permute-done.above_ref = f32[16,128]{1,0:T(8,128)S(1)} collective-permute-done((f32[16,128]{1,0:T(8,128)S(1)}, f32[16,128]{1,0:T(8,128)S(1)}, u32[]{:S(2)}, u32[]{:S(2)}) %collective-permute-start) | collective-permute-done | bytes 8224 | tf_op jit(solution)/shard_map/ppermute | solution.py:444
  42.4 0.4 smooth.1.load_ref
  42.7 6.4 %all-to-all-done.1.arrived_ref = f32[512,4,128]{2,1,0:T(4,128)S(1)} async-done(((f32[512,4,128]{2,1,0:T(4,128)}), f32[512,4,128]{2,1,0:T(4,128)S(1)}, u32[]{:S(2)}, u32[]{:S(2)}) %all-to-all-start.1) | async-done | bytes 1048608 | tf_op jit(solution)/shard_map/all_to_all | solution.py:439
  49.1 6.5 %transport.1 = (f32[16,128]{1,0:T(8,128)}, f32[512,4,128]{2,1,0:T(4,128)S(1)}) custom-call(s32[16,128]{1,0:T(8,128)S(1)} %get-tuple-element.17.target_ref, f32[512,4,128]{2,1,0:T(4,128)S(1)} %all-to-all-done.1.arrived_ref, bf16[16,128,48]{2,1,0:T(8,128)(2,1)S(1)} %get-tuple-element.23.lhs_ref, f32[3,16,128]{2,1,0:T(8,128)S(1)} %bitcast.15, ...), custom_call_target="tpu_custom_call" | custom-call | tf_op jit(solution)/shard_map/transport/pallas_call | solution.py:534
  55.6 23.0 %all_to_all.21.back_ref = f32[512,4,128]{2,1,0:T(4,128)S(1)} all-to-all(f32[512,4,128]{2,1,0:T(4,128)S(1)} %get-tuple-element.27), channel_id=1, replica_groups=mesh['gx'=8,'gy'=16] {'gx','gy'}, dimensions={0} | all-to-all | bytes 2097152 | tf_op jit(solution)/shard_map/all_to_all | solution.py:439
  78.6 2.4 %reduce.1 = (f32[512,128]{1,0:T(8,128)}, f32[3,65536]{1,0:T(4,128)}, f32[2064,128]{1,0:T(8,128)S(1)}) custom-call(s32[8,128]{1,0:T(8,128)S(1)} %get-tuple-element.26.ids_ref, f32[512,4,128]{2,1,0:T(4,128)S(1)} %all_to_all.21.back_ref, f32[2064,128]{1,0:T(8,128)S(1)} %get-tuple-element.28.start_ref), custom_call_target="tpu_custom_call", output_to_operand_aliasing={{2}: (2, {})} | custom-call | tf_op jit(solution)/shard_map/reduce/pallas_call | solution.py:551
Async XLA Ops:
  2.7 21.7 %all-to-all-start = ((f32[128,2,128]{2,1,0:T(2,128)}), f32[128,2,128]{2,1,0:T(2,128)S(1)}, u32[]{:S(2)}, u32[]{:S(2)}) async-start(f32[128,2,128]{2,1,0:T(2,128)} %bitcast.6), calls=%async_computation | async-start | bytes 262144 | tf_op jit(solution)/shard_map/all_to_all | solution.py:439
  26.1 4.0 %copy-start.1 = (f32[2,8,128]{2,1,0:T(8,128)S(1)}, f32[2,8,128]{2,1,0:T(8,128)}, u32[]{:S(2)}) copy-start(f32[2,8,128]{2,1,0:T(8,128)} %param.7) | copy-start | bytes 24580
  26.2 9.7 %copy-start = (f32[3,2,8,128]{3,2,1,0:T(8,128)S(1)}, f32[3,2,8,128]{3,2,1,0:T(8,128)}, u32[]{:S(2)}) copy-start(f32[3,2,8,128]{3,2,1,0:T(8,128)} %param.8) | copy-start | bytes 73732
  26.2 22.9 %all-to-all-start.1 = ((f32[512,4,128]{2,1,0:T(4,128)}), f32[512,4,128]{2,1,0:T(4,128)S(1)}, u32[]{:S(2)}, u32[]{:S(2)}) async-start(f32[512,4,128]{2,1,0:T(4,128)} %get-tuple-element.20), calls=%async_computation.1 | async-start | bytes 2097152 | tf_op jit(solution)/shard_map/all_to_all | solution.py:439
  30.2 7.6 %collective-permute-start.1 = (f32[16,128]{1,0:T(8,128)S(1)}, f32[16,128]{1,0:T(8,128)S(1)}, u32[]{:S(2)}, u32[]{:S(2)}) collective-permute-start(f32[16,128]{1,0:T(8,128)S(1)} %bitcast.17), channel_id=1, source_target_pairs={{1,0},{2,1},{3,2},{4,3},{5,4},{6,5},{7,6},{8,7},{9,8},{10,9},{11,1... | collective-permute-start | bytes 24584 | tf_op jit(solution)/shard_map/ppermute | solution.py:445
  35.8 6.5 %collective-permute-start = (f32[16,128]{1,0:T(8,128)S(1)}, f32[16,128]{1,0:T(8,128)S(1)}, u32[]{:S(2)}, u32[]{:S(2)}) collective-permute-start(f32[16,128]{1,0:T(8,128)S(1)} %bitcast.18), channel_id=1, source_target_pairs={{0,1},{1,2},{2,3},{3,4},{4,5},{5,6},{6,7},{7,8},{8,9},{9,10},{10,1... | collective-permute-start | bytes 24584 | tf_op jit(solution)/shard_map/ppermute | solution.py:444

commit v10 on v9

--- a/solution.py
+++ b/solution.py
@@ -29,6 +29,7 @@
 DEAD = -1e30
 PIECES = 4
 BLOCKS = SB_DEV // PIECES
+PART = BLOCKS // 2
 F32 = jnp.float32
 BF16 = jnp.bfloat16
 I32 = jnp.int32
@@ -187,11 +188,31 @@
             table_ref[4 * b + 3 : 4 * b + 4, :] = weight_ref[b : b + 1, :]
 
 
-def setup_kernel(position_hbm, point_ref, start_ref, lhs_ref, position_ref, sems):
+def filter_taps(taps_ref):
+    shape = (3 * TILE, TILE)
+    row = iota(shape, 0)
+    source = jnp.where(
+        row < TILE, row, row % HALF + jnp.where(row < 2 * TILE, -HALF, TILE)
+    )
+    shift = (source - iota(shape, 1)).astype(F32)
+    taps = jnp.where(
+        jnp.abs(shift) <= HALF,
+        GAUSS_PEAK * jnp.exp(shift * shift * (-0.5 / (SIGMA_CELLS * SIGMA_CELLS))),
+        0.0,
+    )
+    high = rounded(taps)
+    rest = taps - high
+    middle = rounded(rest)
+    for part, values in enumerate((high, middle, rest - middle)):
+        taps_ref[part] = values.astype(BF16)
+
+
+def setup_kernel(position_hbm, point_ref, start_ref, lhs_ref, taps_ref, position_ref, sems):
     copies = piece_copies(position_hbm, position_ref, sems)
     for copy in copies:
         copy.start()
     prepare(point_ref, lhs_ref)
+    filter_taps(taps_ref)
     for r in range(CAP):
         start_ref[(SB_DEV + r) * 4 : (SB_DEV + r + 1) * 4, :] = jnp.zeros((4, 128), F32)
 
@@ -207,21 +228,10 @@
         lax.fori_loop(piece * BLOCKS, (piece + 1) * BLOCKS, block, 0, unroll=8)
 
 
-def smooth_kernel(halo_ref, above_ref, mid_ref, below_ref, load_ref, rows_ref):
+def smooth_kernel(halo_ref, taps_ref, above_ref, mid_ref, below_ref, load_ref, rows_ref):
     tiles = (above_ref[...], mid_ref[...], below_ref[...])
     count_x, count_y = lax.axis_size("gx"), lax.axis_size("gy")
     here_x, here_y = lax.axis_index("gx"), lax.axis_index("gy")
-    shape = (3 * TILE, TILE)
-    row = iota(shape, 0)
-    source = jnp.where(
-        row < TILE, row, row % HALF + jnp.where(row < 2 * TILE, -HALF, TILE)
-    )
-    shift = (source - iota(shape, 1)).astype(F32)
-    taps = jnp.where(
-        jnp.abs(shift) <= HALF,
-        GAUSS_PEAK * jnp.exp(shift * shift * (-0.5 / (SIGMA_CELLS * SIGMA_CELLS))),
-        0.0,
-    )
     shape = (TILES, TILE)
     own_row = iota(shape, 1) // HALF == iota(shape, 0)
     rows = []
@@ -232,12 +242,17 @@
             halo = halo_ref[pl.ds(2 * peer + 1, 1), :]
             parts.append(jnp.where(own_row, halo, 0.0))
         rows.append(jnp.concatenate(parts, axis=1))
-    first = jnp.dot(
-        jnp.concatenate(rows, axis=0),
-        taps,
-        preferred_element_type=F32,
-        precision=lax.Precision.HIGHEST,
-    )
+    cells = jnp.concatenate(rows, axis=0)
+    high = rounded(cells)
+    rest = cells - high
+    middle = rounded(rest)
+    cells = jnp.concatenate([high, middle, rest - middle], axis=0).astype(BF16)
+    count = 3 * TILES
+    first = jnp.dot(cells[:count], taps_ref[2], preferred_element_type=F32)
+    second = jnp.dot(cells[: 2 * count], taps_ref[1], preferred_element_type=F32)
+    third = jnp.dot(cells, taps_ref[0], preferred_element_type=F32)
+    first = first + second[count:] + third[2 * count :]
+    first = first + second[:count] + third[count : 2 * count] + third[:count]
     planes = []
     for z in range(PZ):
         for part in range(3):
@@ -270,11 +285,14 @@
         for c in range(BLOCKS):
             line = pl.multiple_of(ids_smem[piece, c], 4)
             out_ref[piece * BLOCKS + c] = table_ref[pl.ds(line, 4), :]
-        part = pl.ds(piece * BLOCKS, BLOCKS)
-        copies.append(
-            pltpu.make_async_copy(out_ref.at[part], out_hbm.at[part], out_sems.at[piece])
-        )
-        copies[piece].start()
+            if (c + 1) % PART == 0:
+                part = pl.ds(piece * BLOCKS + c + 1 - PART, PART)
+                copies.append(
+                    pltpu.make_async_copy(
+                        out_ref.at[part], out_hbm.at[part], out_sems.at[len(copies)]
+                    )
+                )
+                copies[-1].start()
     for copy in copies:
         copy.wait()
 
@@ -399,20 +417,20 @@
             for place, total in zip(places, sums):
                 into[place, :] = total
     copies = []
-    width = BLOCKS * SITE_BLOCK
-    for piece in range(PIECES):
-        part = pl.ds(piece * BLOCKS, BLOCKS)
-        lines = pl.ds(piece * BLOCKS * 4 + 3, BLOCKS, stride=4)
+    width = PART * SITE_BLOCK
+    for piece in range(SB_DEV // PART):
+        part = pl.ds(piece * PART, PART)
+        lines = pl.ds(piece * PART * 4 + 3, PART, stride=4)
         mass = acc_ref[lines, :] + other_ref[lines, :]
         mass_ref[part, :] = mass
         copies.append(
             pltpu.make_async_copy(
-                mass_ref.at[part], mass_hbm.at[part], sems.at[PIECES + piece]
+                mass_ref.at[part], mass_hbm.at[part], sems.at[SB_DEV // PART + piece]
             )
         )
         copies[-1].start()
         scale_ref[part, :] = 1.0 / (mass + PRIOR_MASS)
-        for b in range(piece * BLOCKS, (piece + 1) * BLOCKS):
+        for b in range(piece * PART, (piece + 1) * PART):
             centre_ref[:, b * SITE_BLOCK : (b + 1) * SITE_BLOCK] = (
                 acc_ref[4 * b : 4 * b + 3, :] + other_ref[4 * b : 4 * b + 3, :]
             ) * scale_ref[b : b + 1, :]
@@ -498,7 +516,7 @@
             pltpu.VMEM((SLOTS, 4, SITE_BLOCK), F32),
             pltpu.SMEM((8, 128), I32),
             pltpu.SemaphoreType.DMA,
-            pltpu.SemaphoreType.DMA((PIECES,)),
+            pltpu.SemaphoreType.DMA((SB_DEV // PART,)),
         ],
         name="gather",
     )(asked, table)
@@ -507,14 +525,15 @@
     )
     arrived = exchange(blocks)
     above, below = neighbours(cells, "gy")
-    start, lhs = pl.pallas_call(
+    start, lhs, taps = pl.pallas_call(
         setup_kernel,
         out_shape=(
             shape_of((SB_DEV + CAP) * 4, SITE_BLOCK),
             shape_of(TILES, TILE, 48, dtype=BF16),
+            shape_of(3, 3 * TILE, TILE, dtype=BF16),
         ),
         in_specs=[HBM, VMEM],
-        out_specs=(VMEM, VMEM),
+        out_specs=(VMEM,) * 3,
         scratch_shapes=[
             pltpu.VMEM((3, SB_DEV * SITE_BLOCK), F32),
             pltpu.SemaphoreType.DMA((PIECES,)),
@@ -525,12 +544,12 @@
     load = pl.pallas_call(
         smooth_kernel,
         out_shape=shape_of(TILES, TILE),
-        in_specs=[VMEM] * 4,
+        in_specs=[VMEM] * 5,
         out_specs=VMEM,
         scratch_shapes=[pltpu.VMEM((PZ, 3 * CY, 128), F32)],
         compiler_params=LIMIT,
         name="smooth",
-    )(asked, above, cells, below)
+    )(asked, taps, above, cells, below)
     potential, moments = pl.pallas_call(
         transport_kernel,
         out_shape=(shape_of(TILES, TILE), shape_of(SLOTS, 4, SITE_BLOCK)),
@@ -562,7 +581,7 @@
             pltpu.VMEM((SB_DEV, SITE_BLOCK), F32),
             pltpu.VMEM((SB_DEV, SITE_BLOCK), F32),
             pltpu.VMEM((3, SB_DEV * SITE_BLOCK), F32),
-            pltpu.SemaphoreType.DMA((2 * PIECES,)),
+            pltpu.SemaphoreType.DMA((2 * SB_DEV // PART,)),
         ],
         input_output_aliases={2: 2},
         compiler_params=LIMIT,

time: 81.3 us -> 81.4 us (level)
  no operation moved by 1% of the time
where the time goes in v10:
time: 81.4 us; the launch traced here: 81 us
  blocking collectives  23 us (28%)
  starting transfers between devices  21.1 us (26%)
  waiting for transfers between devices  19.7 us (24%)
  Pallas kernels  16.4 us (20%)
    all_to_all x1, blocking collectives, exchange(): return lax.all_to_all(values, AXES, split_axis=0, concat_axis=0, tiled=True)  23 us
    all_to_all x2, starting transfers between devices, exchange(): return lax.all_to_all(values, AXES, split_axis=0, concat_axis=0, tiled=True)  15.5 us
    all_to_all x2, waiting for transfers between devices, exchange(): return lax.all_to_all(values, AXES, split_axis=0, concat_axis=0, tiled=True)  15.1 us
    pallas_call x1, Pallas kernels, local(): pl.pallas_call(transport_kernel, out_shape=(shape_of(TILES, TILE), shape_...  6.49 us
    ppermute x1, starting transfers between devices, neighbours(): lax.ppermute(values, axis, [((i + 1) % count, i) for i in range(count)])  5.65 us
    ppermute x1, waiting for transfers between devices, neighbours(): lax.ppermute(values, axis, [(i, (i + 1) % count) for i in range(count)])  4.63 us
    pallas_call x1, Pallas kernels, local(): pl.pallas_call(reduce_kernel, out_shape=(shape_of(SB_DEV, SITE_BLOCK), sh...  2.42 us
    pallas_call x1, Pallas kernels, local(): pl.pallas_call(request_kernel, out_shape=(shape_of(2 * OWNERS, 128), shap...  2.1 us
  transfers between devices with their start and end apart: 4, of which 3 were waited for; matrix products, arithmetic and copies ran while one was open for 0% of the time, Pallas kernels for 5%

profile of v10, /device:TPU:1, one launch (start us, length us, event | category | flops | bytes accessed | tf_op | source)
XLA Modules:
  0.0 81.0 jit_solution(811763938171255566)
XLA Ops:
  0.6 2.1 %request.1 = (f32[256,128]{1,0:T(8,128)}, s32[16,128]{1,0:T(8,128)S(1)}) custom-call(s32[16,16]{1,0:T(8,128)} %bitcast.21, s32[16,16]{1,0:T(8,128)} %bitcast.22, s32[2,1,8]{2,1,0:T(1,128)} %bitcast.23, f32[16,128]{1,0:T(8,128)} %bitcast.16), custom_call_target="tpu_custom_call" | custom-call | tf_op jit(solution)/shard_map/request/pallas_call | solution.py:472
  2.7 11.5 %all-to-all-start = ((f32[128,2,128]{2,1,0:T(2,128)}), f32[128,2,128]{2,1,0:T(2,128)S(1)}, u32[]{:S(2)}, u32[]{:S(2)}) async-start(f32[128,2,128]{2,1,0:T(2,128)} %bitcast.6), calls=%async_computation | async-start | bytes 262144 | tf_op jit(solution)/shard_map/all_to_all | solution.py:457
  14.2 1.6 %table.1.table_ref = f32[2064,128]{1,0:T(8,128)S(1)} custom-call(f32[3,65536]{1,0:T(4,128)} %position_hbm.2, f32[512,128]{1,0:T(8,128)} %bitcast.20), custom_call_target="tpu_custom_call" | custom-call | tf_op jit(solution)/shard_map/table/pallas_call | solution.py:496
  15.8 8.6 %all-to-all-done = f32[128,2,128]{2,1,0:T(2,128)S(1)} async-done(((f32[128,2,128]{2,1,0:T(2,128)}), f32[128,2,128]{2,1,0:T(2,128)S(1)}, u32[]{:S(2)}, u32[]{:S(2)}) %all-to-all-start) | async-done | bytes 131104 | tf_op jit(solution)/shard_map/all_to_all | solution.py:457
  24.4 1.7 %gather.1 = (f32[512,4,128]{2,1,0:T(4,128)}, s32[8,128]{1,0:T(8,128)S(1)}) custom-call(f32[256,128]{1,0:T(8,128)S(1)} %bitcast.12, f32[2064,128]{1,0:T(8,128)S(1)} %table.1.table_ref), custom_call_target="tpu_custom_call" | custom-call | tf_op jit(solution)/shard_map/gather/pallas_call | solution.py:509
  26.1 0.0 copy-start.1
  26.2 0.0 copy-start
  26.2 4.0 %all-to-all-start.1 = ((f32[512,4,128]{2,1,0:T(4,128)}), f32[512,4,128]{2,1,0:T(4,128)S(1)}, u32[]{:S(2)}, u32[]{:S(2)}) async-start(f32[512,4,128]{2,1,0:T(4,128)} %get-tuple-element.21), calls=%async_computation.1 | async-start | bytes 2097152 | tf_op jit(solution)/shard_map/all_to_all | solution.py:457
  30.2 0.0 copy-done.1
  30.2 5.7 %collective-permute-start.1 = (f32[16,128]{1,0:T(8,128)S(1)}, f32[16,128]{1,0:T(8,128)S(1)}, u32[]{:S(2)}, u32[]{:S(2)}) collective-permute-start(f32[16,128]{1,0:T(8,128)S(1)} %bitcast.17), channel_id=1, source_target_pairs={{1,0},{2,1},{3,2},{4,3},{5,4},{6,5},{7,6},{8,7},{9,8},{10,9},{11,1... | collective-permute-start | bytes 24584 | tf_op jit(solution)/shard_map/ppermute | solution.py:463
  35.8 0.0 collective-permute-start
  35.8 0.0 copy-done
  35.8 1.9 %setup.1 = (f32[2064,128]{1,0:T(8,128)S(1)}, bf16[16,128,48]{2,1,0:T(8,128)(2,1)S(1)}, bf16[3,384,128]{2,1,0:T(8,128)(2,1)S(1)}) custom-call(f32[3,65536]{1,0:T(4,128)} %position_hbm.2, f32[3,16,128]{2,1,0:T(8,128)S(1)} %bitcast.14), custom_call_target="tpu_custom_call" | custom-call | tf_op jit(solution)/shard_map/setup/pallas_call | solution.py:528
  37.7 0.0 collective-permute-done.1.below_ref
  37.7 4.6 %collective-permute-done.above_ref = f32[16,128]{1,0:T(8,128)S(1)} collective-permute-done((f32[16,128]{1,0:T(8,128)S(1)}, f32[16,128]{1,0:T(8,128)S(1)}, u32[]{:S(2)}, u32[]{:S(2)}) %collective-permute-start) | collective-permute-done | bytes 8224 | tf_op jit(solution)/shard_map/ppermute | solution.py:462
  42.4 0.3 smooth.1.load_ref
  42.6 6.5 %all-to-all-done.1.arrived_ref = f32[512,4,128]{2,1,0:T(4,128)S(1)} async-done(((f32[512,4,128]{2,1,0:T(4,128)}), f32[512,4,128]{2,1,0:T(4,128)S(1)}, u32[]{:S(2)}, u32[]{:S(2)}) %all-to-all-start.1) | async-done | bytes 1048608 | tf_op jit(solution)/shard_map/all_to_all | solution.py:457
  49.1 6.5 %transport.1 = (f32[16,128]{1,0:T(8,128)}, f32[512,4,128]{2,1,0:T(4,128)S(1)}) custom-call(s32[16,128]{1,0:T(8,128)S(1)} %get-tuple-element.18.target_ref, f32[512,4,128]{2,1,0:T(4,128)S(1)} %all-to-all-done.1.arrived_ref, bf16[16,128,48]{2,1,0:T(8,128)(2,1)S(1)} %get-tuple-element.24.lhs_ref, f32[3,16,128]{2,1,0:T(8,128)S(1)} %bitcast.15, ...), custom_call_target="tpu_custom_call" | custom-call | tf_op jit(solution)/shard_map/transport/pallas_call | solution.py:553
  55.6 23.0 %all_to_all.21.back_ref = f32[512,4,128]{2,1,0:T(4,128)S(1)} all-to-all(f32[512,4,128]{2,1,0:T(4,128)S(1)} %get-tuple-element.29), channel_id=1, replica_groups=mesh['gx'=8,'gy'=16] {'gx','gy'}, dimensions={0} | all-to-all | bytes 2097152 | tf_op jit(solution)/shard_map/all_to_all | solution.py:457
  78.6 2.4 %reduce.1 = (f32[512,128]{1,0:T(8,128)}, f32[3,65536]{1,0:T(4,128)}, f32[2064,128]{1,0:T(8,128)S(1)}) custom-call(s32[8,128]{1,0:T(8,128)S(1)} %get-tuple-element.28.ids_ref, f32[512,4,128]{2,1,0:T(4,128)S(1)} %all_to_all.21.back_ref, f32[2064,128]{1,0:T(8,128)S(1)} %get-tuple-element.30.start_ref), custom_call_target="tpu_custom_call", output_to_operand_aliasing={{2}: (2, {})} | custom-call | tf_op jit(solution)/shard_map/reduce/pallas_call | solution.py:570
Async XLA Ops:
  2.7 21.7 %all-to-all-start = ((f32[128,2,128]{2,1,0:T(2,128)}), f32[128,2,128]{2,1,0:T(2,128)S(1)}, u32[]{:S(2)}, u32[]{:S(2)}) async-start(f32[128,2,128]{2,1,0:T(2,128)} %bitcast.6), calls=%async_computation | async-start | bytes 262144 | tf_op jit(solution)/shard_map/all_to_all | solution.py:457
  26.1 4.0 %copy-start.1 = (f32[2,8,128]{2,1,0:T(8,128)S(1)}, f32[2,8,128]{2,1,0:T(8,128)}, u32[]{:S(2)}) copy-start(f32[2,8,128]{2,1,0:T(8,128)} %param.7) | copy-start | bytes 24580
  26.2 9.7 %copy-start = (f32[3,2,8,128]{3,2,1,0:T(8,128)S(1)}, f32[3,2,8,128]{3,2,1,0:T(8,128)}, u32[]{:S(2)}) copy-start(f32[3,2,8,128]{3,2,1,0:T(8,128)} %param.8) | copy-start | bytes 73732
  26.2 22.9 %all-to-all-start.1 = ((f32[512,4,128]{2,1,0:T(4,128)}), f32[512,4,128]{2,1,0:T(4,128)S(1)}, u32[]{:S(2)}, u32[]{:S(2)}) async-start(f32[512,4,128]{2,1,0:T(4,128)} %get-tuple-element.21), calls=%async_computation.1 | async-start | bytes 2097152 | tf_op jit(solution)/shard_map/all_to_all | solution.py:457
  30.2 7.6 %collective-permute-start.1 = (f32[16,128]{1,0:T(8,128)S(1)}, f32[16,128]{1,0:T(8,128)S(1)}, u32[]{:S(2)}, u32[]{:S(2)}) collective-permute-start(f32[16,128]{1,0:T(8,128)S(1)} %bitcast.17), channel_id=1, source_target_pairs={{1,0},{2,1},{3,2},{4,3},{5,4},{6,5},{7,6},{8,7},{9,8},{10,9},{11,1... | collective-permute-start | bytes 24584 | tf_op jit(solution)/shard_map/ppermute | solution.py:463
  35.8 6.5 %collective-permute-start = (f32[16,128]{1,0:T(8,128)S(1)}, f32[16,128]{1,0:T(8,128)S(1)}, u32[]{:S(2)}, u32[]{:S(2)}) collective-permute-start(f32[16,128]{1,0:T(8,128)S(1)} %bitcast.18), channel_id=1, source_target_pairs={{0,1},{1,2},{2,3},{3,4},{4,5},{5,6},{6,7},{7,8},{8,9},{9,10},{10,1... | collective-permute-start | bytes 24584 | tf_op jit(solution)/shard_map/ppermute | solution.py:462

commit v11 on v10

--- a/solution.py
+++ b/solution.py
@@ -391,7 +391,7 @@
 
 
 def reduce_kernel(
-    ids_ref,
+    ids_vmem,
     back_ref,
     start_ref,
     mass_hbm,
@@ -401,9 +401,14 @@
     mass_ref,
     scale_ref,
     centre_ref,
+    ids_ref,
+    ids_sem,
     sems,
 ):
+    ids_copy = pltpu.make_async_copy(ids_vmem, ids_ref, ids_sem)
+    ids_copy.start()
     other_ref[...] = jnp.zeros_like(other_ref)
+    ids_copy.wait()
     for piece in range(PIECES):
         for peer in range(BLOCKS // CAP):
             into = (acc_ref, other_ref)[peer % 2]
@@ -574,13 +579,15 @@
             shape_of(3, SB_DEV * SITE_BLOCK),
             shape_of((SB_DEV + CAP) * 4, SITE_BLOCK),
         ),
-        in_specs=[SMEM] + [VMEM] * 2,
+        in_specs=[VMEM] * 3,
         out_specs=(HBM, HBM, VMEM),
         scratch_shapes=[
             pltpu.VMEM(((SB_DEV + CAP) * 4, SITE_BLOCK), F32),
             pltpu.VMEM((SB_DEV, SITE_BLOCK), F32),
             pltpu.VMEM((SB_DEV, SITE_BLOCK), F32),
             pltpu.VMEM((3, SB_DEV * SITE_BLOCK), F32),
+            pltpu.SMEM((8, 128), I32),
+            pltpu.SemaphoreType.DMA,
             pltpu.SemaphoreType.DMA((2 * SB_DEV // PART,)),
         ],
         input_output_aliases={2: 2},

time: 81.4 us -> 81.3 us (level)
  no operation moved by 1% of the time
where the time goes in v11:
time: 81.3 us; the launch traced here: 80.9 us
  blocking collectives  23 us (28%)
  starting transfers between devices  21.1 us (26%)
  waiting for transfers between devices  19.7 us (24%)
  Pallas kernels  16.4 us (20%)
    all_to_all x1, blocking collectives, exchange(): return lax.all_to_all(values, AXES, split_axis=0, concat_axis=0, tiled=True)  23 us
    all_to_all x2, starting transfers between devices, exchange(): return lax.all_to_all(values, AXES, split_axis=0, concat_axis=0, tiled=True)  15.5 us
    all_to_all x2, waiting for transfers between devices, exchange(): return lax.all_to_all(values, AXES, split_axis=0, concat_axis=0, tiled=True)  15.1 us
    pallas_call x1, Pallas kernels, local(): pl.pallas_call(transport_kernel, out_shape=(shape_of(TILES, TILE), shape_...  6.51 us
    ppermute x1, starting transfers between devices, neighbours(): lax.ppermute(values, axis, [((i + 1) % count, i) for i in range(count)])  5.65 us
    ppermute x1, waiting for transfers between devices, neighbours(): lax.ppermute(values, axis, [(i, (i + 1) % count) for i in range(count)])  4.63 us
    pallas_call x1, Pallas kernels, local(): pl.pallas_call(reduce_kernel, out_shape=(shape_of(SB_DEV, SITE_BLOCK), sh...  2.34 us
    pallas_call x1, Pallas kernels, local(): pl.pallas_call(request_kernel, out_shape=(shape_of(2 * OWNERS, 128), shap...  2.1 us
  transfers between devices with their start and end apart: 4, of which 3 were waited for; matrix products, arithmetic and copies ran while one was open for 0% of the time, Pallas kernels for 5%

profile of v11, /device:TPU:1, one launch (start us, length us, event | category | flops | bytes accessed | tf_op | source)
XLA Modules:
  0.0 80.9 jit_solution(17879883345717885604)
XLA Ops:
  0.6 2.1 %request.1 = (f32[256,128]{1,0:T(8,128)}, s32[16,128]{1,0:T(8,128)S(1)}) custom-call(s32[16,16]{1,0:T(8,128)} %bitcast.21, s32[16,16]{1,0:T(8,128)} %bitcast.22, s32[2,1,8]{2,1,0:T(1,128)} %bitcast.23, f32[16,128]{1,0:T(8,128)} %bitcast.16), custom_call_target="tpu_custom_call" | custom-call | tf_op jit(solution)/shard_map/request/pallas_call | solution.py:477
  2.7 11.5 %all-to-all-start = ((f32[128,2,128]{2,1,0:T(2,128)}), f32[128,2,128]{2,1,0:T(2,128)S(1)}, u32[]{:S(2)}, u32[]{:S(2)}) async-start(f32[128,2,128]{2,1,0:T(2,128)} %bitcast.6), calls=%async_computation | async-start | bytes 262144 | tf_op jit(solution)/shard_map/all_to_all | solution.py:462
  14.2 1.6 %table.1.table_ref = f32[2064,128]{1,0:T(8,128)S(1)} custom-call(f32[3,65536]{1,0:T(4,128)} %position_hbm.2, f32[512,128]{1,0:T(8,128)} %bitcast.20), custom_call_target="tpu_custom_call" | custom-call | tf_op jit(solution)/shard_map/table/pallas_call | solution.py:501
  15.8 8.6 %all-to-all-done = f32[128,2,128]{2,1,0:T(2,128)S(1)} async-done(((f32[128,2,128]{2,1,0:T(2,128)}), f32[128,2,128]{2,1,0:T(2,128)S(1)}, u32[]{:S(2)}, u32[]{:S(2)}) %all-to-all-start) | async-done | bytes 131104 | tf_op jit(solution)/shard_map/all_to_all | solution.py:462
  24.4 1.7 %gather.1 = (f32[512,4,128]{2,1,0:T(4,128)}, s32[8,128]{1,0:T(8,128)S(1)}) custom-call(f32[256,128]{1,0:T(8,128)S(1)} %bitcast.12, f32[2064,128]{1,0:T(8,128)S(1)} %table.1.table_ref), custom_call_target="tpu_custom_call" | custom-call | tf_op jit(solution)/shard_map/gather/pallas_call | solution.py:514
  26.1 0.0 copy-start.1
  26.2 0.0 copy-start
  26.2 4.0 %all-to-all-start.1 = ((f32[512,4,128]{2,1,0:T(4,128)}), f32[512,4,128]{2,1,0:T(4,128)S(1)}, u32[]{:S(2)}, u32[]{:S(2)}) async-start(f32[512,4,128]{2,1,0:T(4,128)} %get-tuple-element.21), calls=%async_computation.1 | async-start | bytes 2097152 | tf_op jit(solution)/shard_map/all_to_all | solution.py:462
  30.2 0.0 copy-done.1
  30.2 5.7 %collective-permute-start.1 = (f32[16,128]{1,0:T(8,128)S(1)}, f32[16,128]{1,0:T(8,128)S(1)}, u32[]{:S(2)}, u32[]{:S(2)}) collective-permute-start(f32[16,128]{1,0:T(8,128)S(1)} %bitcast.17), channel_id=1, source_target_pairs={{1,0},{2,1},{3,2},{4,3},{5,4},{6,5},{7,6},{8,7},{9,8},{10,9},{11,1... | collective-permute-start | bytes 24584 | tf_op jit(solution)/shard_map/ppermute | solution.py:468
  35.8 0.0 collective-permute-start
  35.8 0.0 copy-done
  35.8 1.9 %setup.1 = (f32[2064,128]{1,0:T(8,128)S(1)}, bf16[16,128,48]{2,1,0:T(8,128)(2,1)S(1)}, bf16[3,384,128]{2,1,0:T(8,128)(2,1)S(1)}) custom-call(f32[3,65536]{1,0:T(4,128)} %position_hbm.2, f32[3,16,128]{2,1,0:T(8,128)S(1)} %bitcast.14), custom_call_target="tpu_custom_call" | custom-call | tf_op jit(solution)/shard_map/setup/pallas_call | solution.py:533
  37.7 0.0 collective-permute-done.1.below_ref
  37.7 4.6 %collective-permute-done.above_ref = f32[16,128]{1,0:T(8,128)S(1)} collective-permute-done((f32[16,128]{1,0:T(8,128)S(1)}, f32[16,128]{1,0:T(8,128)S(1)}, u32[]{:S(2)}, u32[]{:S(2)}) %collective-permute-start) | collective-permute-done | bytes 8224 | tf_op jit(solution)/shard_map/ppermute | solution.py:467
  42.4 0.3 smooth.1.load_ref
  42.6 6.5 %all-to-all-done.1.arrived_ref = f32[512,4,128]{2,1,0:T(4,128)S(1)} async-done(((f32[512,4,128]{2,1,0:T(4,128)}), f32[512,4,128]{2,1,0:T(4,128)S(1)}, u32[]{:S(2)}, u32[]{:S(2)}) %all-to-all-start.1) | async-done | bytes 1048608 | tf_op jit(solution)/shard_map/all_to_all | solution.py:462
  49.1 6.5 %transport.1 = (f32[16,128]{1,0:T(8,128)}, f32[512,4,128]{2,1,0:T(4,128)S(1)}) custom-call(s32[16,128]{1,0:T(8,128)S(1)} %get-tuple-element.18.target_ref, f32[512,4,128]{2,1,0:T(4,128)S(1)} %all-to-all-done.1.arrived_ref, bf16[16,128,48]{2,1,0:T(8,128)(2,1)S(1)} %get-tuple-element.24.lhs_ref, f32[3,16,128]{2,1,0:T(8,128)S(1)} %bitcast.15, ...), custom_call_target="tpu_custom_call" | custom-call | tf_op jit(solution)/shard_map/transport/pallas_call | solution.py:558
  55.6 23.0 %all_to_all.21.back_ref = f32[512,4,128]{2,1,0:T(4,128)S(1)} all-to-all(f32[512,4,128]{2,1,0:T(4,128)S(1)} %get-tuple-element.29), channel_id=1, replica_groups=mesh['gx'=8,'gy'=16] {'gx','gy'}, dimensions={0} | all-to-all | bytes 2097152 | tf_op jit(solution)/shard_map/all_to_all | solution.py:462
  78.6 2.3 %reduce.1 = (f32[512,128]{1,0:T(8,128)}, f32[3,65536]{1,0:T(4,128)}, f32[2064,128]{1,0:T(8,128)S(1)}) custom-call(s32[8,128]{1,0:T(8,128)S(1)} %get-tuple-element.28.ids_vmem, f32[512,4,128]{2,1,0:T(4,128)S(1)} %all_to_all.21.back_ref, f32[2064,128]{1,0:T(8,128)S(1)} %get-tuple-element.30.start_ref), custom_call_target="tpu_custom_call", output_to_operand_aliasing={{2}: (2, {})} | custom-call | tf_op jit(solution)/shard_map/reduce/pallas_call | solution.py:575
Async XLA Ops:
  2.7 21.7 %all-to-all-start = ((f32[128,2,128]{2,1,0:T(2,128)}), f32[128,2,128]{2,1,0:T(2,128)S(1)}, u32[]{:S(2)}, u32[]{:S(2)}) async-start(f32[128,2,128]{2,1,0:T(2,128)} %bitcast.6), calls=%async_computation | async-start | bytes 262144 | tf_op jit(solution)/shard_map/all_to_all | solution.py:462
  26.1 4.0 %copy-start.1 = (f32[2,8,128]{2,1,0:T(8,128)S(1)}, f32[2,8,128]{2,1,0:T(8,128)}, u32[]{:S(2)}) copy-start(f32[2,8,128]{2,1,0:T(8,128)} %param.7) | copy-start | bytes 24580
  26.2 9.7 %copy-start = (f32[3,2,8,128]{3,2,1,0:T(8,128)S(1)}, f32[3,2,8,128]{3,2,1,0:T(8,128)}, u32[]{:S(2)}) copy-start(f32[3,2,8,128]{3,2,1,0:T(8,128)} %param.8) | copy-start | bytes 73732
  26.2 22.9 %all-to-all-start.1 = ((f32[512,4,128]{2,1,0:T(4,128)}), f32[512,4,128]{2,1,0:T(4,128)S(1)}, u32[]{:S(2)}, u32[]{:S(2)}) async-start(f32[512,4,128]{2,1,0:T(4,128)} %get-tuple-element.21), calls=%async_computation.1 | async-start | bytes 2097152 | tf_op jit(solution)/shard_map/all_to_all | solution.py:462
  30.2 7.6 %collective-permute-start.1 = (f32[16,128]{1,0:T(8,128)S(1)}, f32[16,128]{1,0:T(8,128)S(1)}, u32[]{:S(2)}, u32[]{:S(2)}) collective-permute-start(f32[16,128]{1,0:T(8,128)S(1)} %bitcast.17), channel_id=1, source_target_pairs={{1,0},{2,1},{3,2},{4,3},{5,4},{6,5},{7,6},{8,7},{9,8},{10,9},{11,1... | collective-permute-start | bytes 24584 | tf_op jit(solution)/shard_map/ppermute | solution.py:468
  35.8 6.5 %collective-permute-start = (f32[16,128]{1,0:T(8,128)S(1)}, f32[16,128]{1,0:T(8,128)S(1)}, u32[]{:S(2)}, u32[]{:S(2)}) collective-permute-start(f32[16,128]{1,0:T(8,128)S(1)} %bitcast.18), channel_id=1, source_target_pairs={{0,1},{1,2},{2,3},{3,4},{4,5},{5,6},{6,7},{7,8},{8,9},{9,10},{10,1... | collective-permute-start | bytes 24584 | tf_op jit(solution)/shard_map/ppermute | solution.py:467
